TPU v7x, 512 devices: a whole 4x4x16 slice. The times are simulated.
512 devices in a mesh: seq: 32 (over y, x, core), head: 16 (over z).
Axes of the slice: x: 4, y: 4, z: 16, core: 2. Of those that a mesh axis runs over, the one named last changes fastest.
Arguments:
- queries: bfloat16 [4096, 2048], P('seq', 'head'), may hold values from -6 to 6
- keys: bfloat16 [4096, 2048], P('seq', 'head'), may hold values from -6 to 6
- values: bfloat16 [4096, 4096], P('seq', 'head'), may hold values from -6 to 6
- gate_code: int32 [4096, 32], P('seq', 'head'), may hold values from 1 to 1000
- beta_code: int32 [4096, 32], P('seq', 'head'), may hold values from 1 to 255
- out_grad: bfloat16 [4096, 2048], P('seq', 'head'), may hold values from -6 to 6
- w_out: bfloat16 [4096, 2048], P('head'), may hold values from -0.09375 to 0.09375
Outputs:
- attn_out: bfloat16 [4096, 4096], P('seq', 'head')
- q_grad: float32 [4096, 2048], P('seq', 'head')
- k_grad: float32 [4096, 2048], P('seq', 'head')
- v_grad: float32 [4096, 4096], P('seq', 'head')
- weight_grad: float32 [4096, 2048], P(('head', 'seq'))
All inputs are finite; a program needn't handle non-finite values.
Results may differ from a plain program's by a relative error of at most 0.0029.
Values may be sent and summed in bfloat16 or wider, within the bound.
No kernel may reach another device: no remote copies, remote signals or barrier semaphores. Data moves between devices by JAX's collectives and lax.ppermute only.
A program may use at most 64 MiB of HBM per device.

v0:
```python
import jax
import jax.numpy as jnp
from jax import lax
from jax.sharding import PartitionSpec as P

HEAD_DIM = 128
SPAN = 64


norm_eps = 1e-06
gate_step = 1e-06
beta_steps = 256.0
highest = lax.Precision.HIGHEST


def from_behind(value, axis, steps):
    count = lax.axis_size(axis)
    initial, last = (max(0, -steps), min(count, count - steps))
    return lax.ppermute(value, axis, [(source, source + steps) for source in range(initial, last)])


def normalize(block_rows):
    return block_rows * lax.rsqrt(
        jnp.sum(block_rows * block_rows, axis=-1, keepdims=True) + norm_eps
    )


def block_masks(block):
    row_ids = lax.broadcasted_iota(jnp.int32, (block, block), 0)
    col_ids = lax.broadcasted_iota(jnp.int32, (block, block), 1)
    return (row_ids > col_ids, row_ids >= col_ids)


def span_pass(query_blocks, key_blocks, value_blocks, decay_blocks, beta_blocks, state):
    strict, inclusive = block_masks(query_blocks.shape[1])

    def span_advance(state, pieces):
        query_block, key_block, value_block, decay_log, beta_block = pieces
        log_cum = jnp.cumsum(decay_log)
        decay_cum = jnp.exp(log_cum)
        ratio = jnp.exp(log_cum[:, None] - log_cum[None, :]) * beta_block[None, :]
        key_gram = jnp.dot(key_block, key_block.T, precision=highest)
        query_key = jnp.dot(query_block, key_block.T, precision=highest)
        lower_mix = jnp.where(strict, ratio * key_gram, 0.0)
        out_mix = jnp.where(inclusive, ratio * query_key, 0.0)
        right_side = value_block - decay_cum[:, None] * jnp.dot(key_block, state, precision=highest)
        new_values = lax.linalg.triangular_solve(
            lower_mix, right_side, left_side=True, lower=True, unit_diagonal=True
        )
        outputs = decay_cum[:, None] * jnp.dot(query_block, state, precision=highest) + jnp.dot(
            out_mix, new_values, precision=highest
        )
        weights = beta_block * jnp.exp(log_cum[-1] - log_cum)
        next_state = decay_cum[-1] * state + jnp.dot(
            key_block.T, weights[:, None] * new_values, precision=highest
        )
        return (next_state, outputs)

    final_state, outputs = lax.scan(
        span_advance, state, (query_blocks, key_blocks, value_blocks, decay_blocks, beta_blocks)
    )
    return (outputs, final_state)


def head_forward(query_head, key_head, value_pair, decay_pair, beta_pair, start_pair):
    length, width = query_head.shape
    blocks = length // SPAN
    query_blocks = (normalize(query_head) * width ** (-0.5)).reshape(blocks, SPAN, width)
    key_blocks = normalize(key_head).reshape(blocks, SPAN, width)

    def head_single(value_head, decay_head, beta_head, start_state):
        outputs, final_state = span_pass(
            query_blocks,
            key_blocks,
            value_head.reshape(blocks, SPAN, width),
            decay_head.reshape(blocks, SPAN),
            beta_head.reshape(blocks, SPAN),
            start_state,
        )
        return (outputs.reshape(length, width), final_state)

    return jax.vmap(head_single)(value_pair, decay_pair, beta_pair, start_pair)


def slab_effect(key_head, value_pair, decay_pair, beta_pair):
    length, width = key_head.shape
    blocks = length // SPAN
    key_blocks = normalize(key_head).reshape(blocks, SPAN, width)
    strict, inclusive = block_masks(SPAN)

    def slab_single(value_head, decay_head, beta_head):

        def single_advance(carried, pieces):
            state, transition = carried
            key_block, value_block, decay_log, beta_block = pieces
            log_cum = jnp.cumsum(decay_log)
            decay_cum = jnp.exp(log_cum)
            ratio = jnp.exp(log_cum[:, None] - log_cum[None, :]) * beta_block[None, :]
            key_gram = jnp.dot(key_block, key_block.T, precision=highest)
            lower_mix = jnp.where(strict, ratio * key_gram, 0.0)
            stacked = jnp.concatenate([value_block, decay_cum[:, None] * key_block], axis=1)
            solved = lax.linalg.triangular_solve(
                lower_mix, stacked, left_side=True, lower=True, unit_diagonal=True
            )
            new_values = solved[:, :width]
            mixed_keys = solved[:, width:]
            weights = beta_block * jnp.exp(log_cum[-1] - log_cum)
            weighted_keys = key_block * weights[:, None]
            next_state = decay_cum[-1] * state + jnp.dot(
                weighted_keys.T,
                new_values - jnp.dot(mixed_keys, state, precision=highest),
                precision=highest,
            )
            next_transition = decay_cum[-1] * transition - jnp.dot(
                weighted_keys.T,
                jnp.dot(mixed_keys, transition, precision=highest),
                precision=highest,
            )
            return ((next_state, next_transition), None)

        start_carry = (jnp.zeros((width, width), jnp.float32), jnp.eye(width, dtype=jnp.float32))
        (state, transition), unused = lax.scan(
            single_advance,
            start_carry,
            (
                key_blocks,
                value_head.reshape(blocks, SPAN, width),
                decay_head.reshape(blocks, SPAN),
                beta_head.reshape(blocks, SPAN),
            ),
        )
        return (transition, state)

    return jax.vmap(slab_single)(value_pair, decay_pair, beta_pair)


def start_adjoint(query_head, key_head, decay_pair, beta_pair, cot_pair):
    length, width = query_head.shape
    blocks = length // SPAN
    query_blocks = (normalize(query_head) * width ** (-0.5)).reshape(blocks, SPAN, width)
    key_blocks = normalize(key_head).reshape(blocks, SPAN, width)
    strict, inclusive = block_masks(SPAN)

    def start_single(decay_head, beta_head, cot_head):

        def retreat(grad_state, pieces):
            query_block, key_block, decay_log, beta_block, cot_block = pieces
            log_cum = jnp.cumsum(decay_log)
            decay_cum = jnp.exp(log_cum)
            ratio = jnp.exp(log_cum[:, None] - log_cum[None, :]) * beta_block[None, :]
            key_gram = jnp.dot(key_block, key_block.T, precision=highest)
            query_key = jnp.dot(query_block, key_block.T, precision=highest)
            lower_mix = jnp.where(strict, ratio * key_gram, 0.0)
            out_mix = jnp.where(inclusive, ratio * query_key, 0.0)
            mixed_keys = lax.linalg.triangular_solve(
                lower_mix,
                decay_cum[:, None] * key_block,
                left_side=True,
                lower=True,
                unit_diagonal=True,
            )
            weights = beta_block * jnp.exp(log_cum[-1] - log_cum)
            weighted_keys = key_block * weights[:, None]
            probe = decay_cum[:, None] * query_block - jnp.dot(
                out_mix, mixed_keys, precision=highest
            )
            through = decay_cum[-1] * grad_state - jnp.dot(
                mixed_keys.T,
                jnp.dot(weighted_keys, grad_state, precision=highest),
                precision=highest,
            )
            return (jnp.dot(probe.T, cot_block, precision=highest) + through, None)

        zeros_state = jnp.zeros((width, width), jnp.float32)
        result, unused = lax.scan(
            retreat,
            zeros_state,
            (
                query_blocks,
                key_blocks,
                decay_head.reshape(blocks, SPAN),
                beta_head.reshape(blocks, SPAN),
                cot_head.reshape(blocks, SPAN, width),
            ),
            reverse=True,
        )
        return result

    return jax.vmap(start_single)(decay_pair, beta_pair, cot_pair)


def matmul_states(left, right):
    return jnp.einsum("abij,abjk->abik", left, right, precision=highest)


def final_pass(
    query_head, key_head, value_pair, decay_pair, beta_pair, start_pair, cot_pair, end_pair
):

    def forward(query_in, key_in, value_in):
        return head_forward(query_in, key_in, value_in, decay_pair, beta_pair, start_pair)

    (core_out, final_unused), pullback = jax.vjp(forward, query_head, key_head, value_pair)
    return (core_out,) + pullback((cot_pair, end_pair))


def per_device(queries, keys, values, gate_code, beta_code, out_grad, w_out):
    length = queries.shape[0]
    width = HEAD_DIM
    key_count = queries.shape[1] // width
    group = values.shape[1] // queries.shape[1]
    query_heads = queries.astype(jnp.float32).reshape(length, key_count, width).transpose(1, 0, 2)
    key_heads = keys.astype(jnp.float32).reshape(length, key_count, width).transpose(1, 0, 2)
    value_heads = (
        values.astype(jnp.float32).reshape(length, key_count, group, width).transpose(1, 2, 0, 3)
    )
    decay_logs = (
        jnp.log1p(-gate_code.astype(jnp.float32) * gate_step)
        .reshape(length, key_count, group)
        .transpose(1, 2, 0)
    )
    betas = (
        (beta_code.astype(jnp.float32) / beta_steps)
        .reshape(length, key_count, group)
        .transpose(1, 2, 0)
    )
    transition, local_state = jax.vmap(slab_effect)(key_heads, value_heads, decay_logs, betas)
    full_grad = lax.all_gather(out_grad, "head", axis=1, tiled=True)
    out_cot = jnp.dot(full_grad, w_out.T, preferred_element_type=jnp.float32)
    cot_heads = out_cot.reshape(length, key_count, group, width).transpose(1, 2, 0, 3)
    empty_states = jnp.zeros_like(transition)
    carried = jax.vmap(start_adjoint)(query_heads, key_heads, decay_logs, betas, cot_heads)
    transposed = jnp.swapaxes(transition, -1, -2)
    slabs = lax.axis_size("seq")

    def forward_turn(turn, arrived):
        return from_behind(matmul_states(transition, arrived) + local_state, "seq", 1)

    start_state = lax.fori_loop(0, slabs - 1, forward_turn, empty_states)

    def backward_turn(turn, arrived):
        return from_behind(matmul_states(transposed, arrived) + carried, "seq", -1)

    end_grad = lax.fori_loop(0, slabs - 1, backward_turn, empty_states)
    core_out, query_grad, key_grad, value_grad = jax.vmap(final_pass)(
        query_heads, key_heads, value_heads, decay_logs, betas, start_state, cot_heads, end_grad
    )
    attn_out = (
        core_out.transpose(2, 0, 1, 3)
        .reshape(length, key_count * group * width)
        .astype(jnp.bfloat16)
    )
    q_grad = query_grad.transpose(1, 0, 2).reshape(length, key_count * width)
    k_grad = key_grad.transpose(1, 0, 2).reshape(length, key_count * width)
    v_grad = value_grad.transpose(2, 0, 1, 3).reshape(length, key_count * group * width)
    scaling = (length * lax.axis_size("seq")) ** (-0.5)
    weight_grad = (
        lax.psum_scatter(
            jnp.dot(attn_out.T, full_grad, preferred_element_type=jnp.float32),
            "seq",
            scatter_dimension=0,
            tiled=True,
        )
        * scaling
    )
    return (attn_out, q_grad, k_grad, v_grad, weight_grad)


def solution(mesh):
    in_specs = (
        P("seq", "head"),
        P("seq", "head"),
        P("seq", "head"),
        P("seq", "head"),
        P("seq", "head"),
        P("seq", "head"),
        P("head", None),
    )
    out_specs = (
        P("seq", "head"),
        P("seq", "head"),
        P("seq", "head"),
        P("seq", "head"),
        P(("head", "seq"), None),
    )
    return jax.shard_map(
        per_device, mesh=mesh, in_specs=in_specs, out_specs=out_specs, check_vma=False
    )
```

profile of v0, /device:TPU:7, one launch (start us, length us, event | category | flops | bytes accessed | tf_op | source)
XLA Modules:
  0.0 706.3 jit_solution(11094657248866685844)
XLA Ops:
  11.9 25.9 %while.114 = (s32[]{:T(128)}, f32[1,2,128,128]{3,2,1,0:T(8,128)S(1)}, f32[1,2,128,128]{3,2,1,0:T(8,128)S(1)}, f32[2,1,2,64]{3,2,1,0:T(2,128)S(1)}, f32[2,1,64,12...) while((s32[]{:T(128)}, ...), condition=%wide.region_3.4_spmd.clone, body=%wide.region_1.3_spmd.clone.sunk | while | flops 132489408 | bytes 2056892 | solution.py:122
  12.8 9.8 %custom-call.41 = f32[1,2,1,64,64]{3,4,2,1,0:T(8,128)S(1)} custom-call(f32[1,2,1,64,64]{4,3,2,1,0:T(8,128)S(1)} %select_add_fusion.2), custom_call_target="InvertDiagBlocksLowerTriangular" | custom-call | tf_op jit(solution)/shard_map/vmap(vmap())/while/body/eval_jaxpr/triangular_solve | solution.py:102
  25.8 9.8 %custom-call.41 = f32[1,2,1,64,64]{3,4,2,1,0:T(8,128)S(1)} custom-call(f32[1,2,1,64,64]{4,3,2,1,0:T(8,128)S(1)} %select_add_fusion.2), custom_call_target="InvertDiagBlocksLowerTriangular" | custom-call | tf_op jit(solution)/shard_map/vmap(vmap())/while/body/eval_jaxpr/triangular_solve | solution.py:102
  38.0 266.0 %while.110 = (s32[]{:T(128)}, f32[1,2,128,128]{3,2,1,0:T(8,128)S(1)}, f32[1,2,128,128]{3,2,1,0:T(8,128)S(1)}, f32[1,2,128,128]{3,2,1,0:T(8,128)S(1)}, s32[]{:T(128)}) while((s32[]{:T(128)}, f32[1,2,128,128]{3,2,1,0:T(8,128)S(1)}, f32[1,2,128,128]{3,2,1,0:T(8,128)S(1)}, f32[1,2,128,128]{3,2,1,0:T(8,128)S(1)}, s32[]{:T(128)}) %tuple.218), condition=%wide.region_5.6_spmd, body=%wide.region_4.5_spmd.sunk | while | flops 50364416 | bytes 1048677 | solution.py:239
  113.5 6.5 collective-permute-start
  165.6 6.5 collective-permute-start
  217.6 6.5 collective-permute-start
  269.6 6.5 collective-permute-start
  304.0 25.6 %while.113 = (s32[]{:T(128)}, f32[1,2,128,128]{3,2,1,0:T(8,128)S(1)}, bf16[2,1,2,64,128]{4,3,0,2,1:T(8,128)(2,1)S(1)}, f32[2,1,128,64]{2,3,1,0:T(8,128)S(1)}, f3...) while((s32[]{:T(128)}, ...), condition=%wide.region_9.11_spmd.clone.clone, body=%wide.region_7.10_spmd.clone.clone.sunk | while | flops 113562048 | bytes 2285849 | solution.py:59
  304.9 9.8 %custom-call.40 = f32[1,2,1,64,64]{3,4,2,1,0:T(8,128)S(1)} custom-call(f32[1,2,1,64,64]{4,3,2,1,0:T(8,128)S(1)} %add_bitcast_fusion.7), custom_call_target="InvertDiagBlocksLowerTriangular" | custom-call | tf_op jit(solution)/shard_map/vmap(jvp(vmap()))/while/body/eval_jaxpr/triangular_solve/custom-call.0 | solution.py:47
  317.8 9.8 %custom-call.40 = f32[1,2,1,64,64]{3,4,2,1,0:T(8,128)S(1)} custom-call(f32[1,2,1,64,64]{4,3,2,1,0:T(8,128)S(1)} %add_bitcast_fusion.7), custom_call_target="InvertDiagBlocksLowerTriangular" | custom-call | tf_op jit(solution)/shard_map/vmap(jvp(vmap()))/while/body/eval_jaxpr/triangular_solve/custom-call.0 | solution.py:47
  329.7 32.1 %all_gather.3 = bf16[128,2048]{1,0:T(8,128)(2,1)S(1)} all-gather(bf16[128,128]{1,0:T(8,128)(2,1)S(1)} %copy-done.3), channel_id=1, replica_groups=mesh['seq'=32,'head'=16] {'head'}, dimensions={1}, use_global_device_ids=true | all-gather | bytes 557056 | tf_op jit(solution)/shard_map/all_gather | solution.py:228
  364.3 25.8 %while.115 = (s32[]{:T(128)}, f32[1,2,128,128]{3,2,1,0:T(8,128)S(1)}, f32[2,1,2,64]{3,2,1,0:T(2,128)S(1)}, f32[2,1,64,128]{3,2,1,0:T(8,128)S(1)}, f32[2,1,2,64]{...) while((s32[]{:T(128)}, ...), condition=%wide.region_12.14_spmd.clone, body=%wide.region_10.13_spmd.clone.sunk | while | flops 113586368 | bytes 1705664 | solution.py:175
  365.2 9.8 %custom-call.42 = f32[1,2,1,64,64]{3,4,2,1,0:T(8,128)S(1)} custom-call(f32[1,2,1,64,64]{4,3,2,1,0:T(8,128)S(1)} %add_bitcast_fusion.8), custom_call_target="InvertDiagBlocksLowerTriangular" | custom-call | tf_op jit(solution)/shard_map/vmap(vmap())/while/body/eval_jaxpr/triangular_solve/custom-call.0 | solution.py:155
  378.1 9.8 %custom-call.42 = f32[1,2,1,64,64]{3,4,2,1,0:T(8,128)S(1)} custom-call(f32[1,2,1,64,64]{4,3,2,1,0:T(8,128)S(1)} %add_bitcast_fusion.8), custom_call_target="InvertDiagBlocksLowerTriangular" | custom-call | tf_op jit(solution)/shard_map/vmap(vmap())/while/body/eval_jaxpr/triangular_solve/custom-call.0 | solution.py:155
  390.2 276.0 %while.111 = (s32[]{:T(128)}, f32[1,2,128,128]{3,2,1,0:T(8,128)S(1)}, f32[1,2,128,128]{3,2,1,0:T(8,128)S(1)}, f32[1,2,128,128]{3,2,1,0:T(8,128)S(1)}, s32[]{:T(128)}) while((s32[]{:T(128)}, f32[1,2,128,128]{3,2,1,0:T(8,128)S(1)}, f32[1,2,128,128]{3,2,1,0:T(8,128)S(1)}, f32[1,2,128,128]{3,2,1,0:T(8,128)S(1)}, s32[]{:T(128)}) %tuple.227), condition=%wide.region_14.16_spmd, body=%wide.region_13.15_spmd.sunk | while | flops 50364416 | bytes 1048677 | solution.py:244
  393.8 12.0 %collective-permute-done.1 = f32[1,2,128,128]{3,2,1,0:T(8,128)S(1)} collective-permute-done((f32[1,2,128,128]{3,2,1,0:T(8,128)S(1)}, f32[1,2,128,128]{3,2,1,0:T(8,128)S(1)}, u32[]{:S(2)}, u32[]{:S(2)}) %collective-permute-start.1) | collective-permute-done | bytes 131104 | tf_op jit(solution)/shard_map/while/body/eval_jaxpr/ppermute | solution.py:19
  408.0 6.5 collective-permute-done.1
  416.7 6.5 collective-permute-done.1
  425.4 6.5 collective-permute-done.1
  434.1 6.5 collective-permute-done.1
  442.7 6.5 collective-permute-done.1
  451.4 6.5 collective-permute-done.1
  460.2 6.6 collective-permute-done.1
  469.0 6.5 collective-permute-done.1
  477.6 6.5 collective-permute-done.1
  486.3 6.5 collective-permute-done.1
  495.0 6.5 collective-permute-done.1
  503.7 6.5 collective-permute-done.1
  512.3 6.5 collective-permute-done.1
  521.0 6.5 collective-permute-done.1
  529.7 6.5 collective-permute-done.1
  538.3 6.5 collective-permute-done.1
  547.0 6.5 collective-permute-done.1
  555.7 6.5 collective-permute-done.1
  564.3 6.5 collective-permute-done.1
  573.0 6.5 collective-permute-done.1
  581.7 6.5 collective-permute-done.1
  590.4 6.5 collective-permute-done.1
  599.0 6.5 collective-permute-done.1
  607.7 6.5 collective-permute-done.1
  616.4 6.5 collective-permute-done.1
  625.0 6.5 collective-permute-done.1
  642.4 6.5 collective-permute-done.1
  651.1 6.5 collective-permute-done.1
  666.4 28.2 %while.112 = (s32[]{:T(128)}, f32[1,2,128,128]{2,3,1,0:T(8,128)S(1)}, f32[2,1,64,128]{3,2,1,0:T(8,128)S(1)}, f32[2,1,64,128]{3,2,1,0:T(8,128)S(1)}, f32[2,1,2,64...) while((s32[]{:T(128)}, ...), condition=%wide.region_18.20_spmd.clone, body=%wide.region_15.19_spmd.clone.sunk | while | flops 233140288 | bytes 3349265 | solution.py:59
  667.1 9.8 %custom-call.39 = f32[1,2,1,64,64]{3,4,2,1,0:T(8,128)S(1)} custom-call(f32[1,2,1,64,64]{4,3,2,1,0:T(8,128)S(1)} %add_bitcast_fusion.6), custom_call_target="InvertDiagBlocksLowerTriangular" | custom-call | tf_op jit(solution)/shard_map/vmap(transpose(jvp(vmap())))/while/body/eval_jaxpr/triangular_solve | solution.py:47
  681.2 9.8 %custom-call.39 = f32[1,2,1,64,64]{3,4,2,1,0:T(8,128)S(1)} custom-call(f32[1,2,1,64,64]{4,3,2,1,0:T(8,128)S(1)} %add_bitcast_fusion.6), custom_call_target="InvertDiagBlocksLowerTriangular" | custom-call | tf_op jit(solution)/shard_map/vmap(transpose(jvp(vmap())))/while/body/eval_jaxpr/triangular_solve | solution.py:47
  (379 shorter events, 359.8 us)
Async XLA Ops:
  7.2 690.8 %reduce-scatter.2.cloned.1.call-start = ((), (), s32[]{:S(2)}) async-start(), calls=%async_computation.1 | async-start | bytes 2162688 | tf_op jit(solution)/shard_map/reduce_scatter | solution.py:258
  44.2 8.4 %collective-permute-start = (f32[1,2,128,128]{3,2,1,0:T(8,128)S(1)}, f32[1,2,128,128]{3,2,1,0:T(8,128)S(1)}, u32[]{:S(2)}, u32[]{:S(2)}) collective-permute-start(f32[1,2,128,128]{3,2,1,0:T(8,128)S(1)} %fusion.351), channel_id=1, source_target_pairs={{0,16},{16,32},{32,48},{48,64},{64,80},{80,96},{96,112},{112,128},... | collective-permute-start | bytes 393224 | tf_op jit(solution)/shard_map/while/body/eval_jaxpr/ppermute | solution.py:19
  52.8 8.4 %collective-permute-start = (f32[1,2,128,128]{3,2,1,0:T(8,128)S(1)}, f32[1,2,128,128]{3,2,1,0:T(8,128)S(1)}, u32[]{:S(2)}, u32[]{:S(2)}) collective-permute-start(f32[1,2,128,128]{3,2,1,0:T(8,128)S(1)} %fusion.351), channel_id=1, source_target_pairs={{0,16},{16,32},{32,48},{48,64},{64,80},{80,96},{96,112},{112,128},... | collective-permute-start | bytes 393224 | tf_op jit(solution)/shard_map/while/body/eval_jaxpr/ppermute | solution.py:19
  61.5 8.4 %collective-permute-start = (f32[1,2,128,128]{3,2,1,0:T(8,128)S(1)}, f32[1,2,128,128]{3,2,1,0:T(8,128)S(1)}, u32[]{:S(2)}, u32[]{:S(2)}) collective-permute-start(f32[1,2,128,128]{3,2,1,0:T(8,128)S(1)} %fusion.351), channel_id=1, source_target_pairs={{0,16},{16,32},{32,48},{48,64},{64,80},{80,96},{96,112},{112,128},... | collective-permute-start | bytes 393224 | tf_op jit(solution)/shard_map/while/body/eval_jaxpr/ppermute | solution.py:19
  70.2 8.4 %collective-permute-start = (f32[1,2,128,128]{3,2,1,0:T(8,128)S(1)}, f32[1,2,128,128]{3,2,1,0:T(8,128)S(1)}, u32[]{:S(2)}, u32[]{:S(2)}) collective-permute-start(f32[1,2,128,128]{3,2,1,0:T(8,128)S(1)} %fusion.351), channel_id=1, source_target_pairs={{0,16},{16,32},{32,48},{48,64},{64,80},{80,96},{96,112},{112,128},... | collective-permute-start | bytes 393224 | tf_op jit(solution)/shard_map/while/body/eval_jaxpr/ppermute | solution.py:19
  78.9 8.4 %collective-permute-start = (f32[1,2,128,128]{3,2,1,0:T(8,128)S(1)}, f32[1,2,128,128]{3,2,1,0:T(8,128)S(1)}, u32[]{:S(2)}, u32[]{:S(2)}) collective-permute-start(f32[1,2,128,128]{3,2,1,0:T(8,128)S(1)} %fusion.351), channel_id=1, source_target_pairs={{0,16},{16,32},{32,48},{48,64},{64,80},{80,96},{96,112},{112,128},... | collective-permute-start | bytes 393224 | tf_op jit(solution)/shard_map/while/body/eval_jaxpr/ppermute | solution.py:19
  87.5 8.4 %collective-permute-start = (f32[1,2,128,128]{3,2,1,0:T(8,128)S(1)}, f32[1,2,128,128]{3,2,1,0:T(8,128)S(1)}, u32[]{:S(2)}, u32[]{:S(2)}) collective-permute-start(f32[1,2,128,128]{3,2,1,0:T(8,128)S(1)} %fusion.351), channel_id=1, source_target_pairs={{0,16},{16,32},{32,48},{48,64},{64,80},{80,96},{96,112},{112,128},... | collective-permute-start | bytes 393224 | tf_op jit(solution)/shard_map/while/body/eval_jaxpr/ppermute | solution.py:19
  96.2 8.4 %collective-permute-start = (f32[1,2,128,128]{3,2,1,0:T(8,128)S(1)}, f32[1,2,128,128]{3,2,1,0:T(8,128)S(1)}, u32[]{:S(2)}, u32[]{:S(2)}) collective-permute-start(f32[1,2,128,128]{3,2,1,0:T(8,128)S(1)} %fusion.351), channel_id=1, source_target_pairs={{0,16},{16,32},{32,48},{48,64},{64,80},{80,96},{96,112},{112,128},... | collective-permute-start | bytes 393224 | tf_op jit(solution)/shard_map/while/body/eval_jaxpr/ppermute | solution.py:19
  104.9 8.4 %collective-permute-start = (f32[1,2,128,128]{3,2,1,0:T(8,128)S(1)}, f32[1,2,128,128]{3,2,1,0:T(8,128)S(1)}, u32[]{:S(2)}, u32[]{:S(2)}) collective-permute-start(f32[1,2,128,128]{3,2,1,0:T(8,128)S(1)} %fusion.351), channel_id=1, source_target_pairs={{0,16},{16,32},{32,48},{48,64},{64,80},{80,96},{96,112},{112,128},... | collective-permute-start | bytes 393224 | tf_op jit(solution)/shard_map/while/body/eval_jaxpr/ppermute | solution.py:19
  113.5 8.4 %collective-permute-start = (f32[1,2,128,128]{3,2,1,0:T(8,128)S(1)}, f32[1,2,128,128]{3,2,1,0:T(8,128)S(1)}, u32[]{:S(2)}, u32[]{:S(2)}) collective-permute-start(f32[1,2,128,128]{3,2,1,0:T(8,128)S(1)} %fusion.351), channel_id=1, source_target_pairs={{0,16},{16,32},{32,48},{48,64},{64,80},{80,96},{96,112},{112,128},... | collective-permute-start | bytes 393224 | tf_op jit(solution)/shard_map/while/body/eval_jaxpr/ppermute | solution.py:19
  122.2 8.4 %collective-permute-start = (f32[1,2,128,128]{3,2,1,0:T(8,128)S(1)}, f32[1,2,128,128]{3,2,1,0:T(8,128)S(1)}, u32[]{:S(2)}, u32[]{:S(2)}) collective-permute-start(f32[1,2,128,128]{3,2,1,0:T(8,128)S(1)} %fusion.351), channel_id=1, source_target_pairs={{0,16},{16,32},{32,48},{48,64},{64,80},{80,96},{96,112},{112,128},... | collective-permute-start | bytes 393224 | tf_op jit(solution)/shard_map/while/body/eval_jaxpr/ppermute | solution.py:19
  130.9 8.4 %collective-permute-start = (f32[1,2,128,128]{3,2,1,0:T(8,128)S(1)}, f32[1,2,128,128]{3,2,1,0:T(8,128)S(1)}, u32[]{:S(2)}, u32[]{:S(2)}) collective-permute-start(f32[1,2,128,128]{3,2,1,0:T(8,128)S(1)} %fusion.351), channel_id=1, source_target_pairs={{0,16},{16,32},{32,48},{48,64},{64,80},{80,96},{96,112},{112,128},... | collective-permute-start | bytes 393224 | tf_op jit(solution)/shard_map/while/body/eval_jaxpr/ppermute | solution.py:19
  139.6 8.4 %collective-permute-start = (f32[1,2,128,128]{3,2,1,0:T(8,128)S(1)}, f32[1,2,128,128]{3,2,1,0:T(8,128)S(1)}, u32[]{:S(2)}, u32[]{:S(2)}) collective-permute-start(f32[1,2,128,128]{3,2,1,0:T(8,128)S(1)} %fusion.351), channel_id=1, source_target_pairs={{0,16},{16,32},{32,48},{48,64},{64,80},{80,96},{96,112},{112,128},... | collective-permute-start | bytes 393224 | tf_op jit(solution)/shard_map/while/body/eval_jaxpr/ppermute | solution.py:19
  148.2 8.4 %collective-permute-start = (f32[1,2,128,128]{3,2,1,0:T(8,128)S(1)}, f32[1,2,128,128]{3,2,1,0:T(8,128)S(1)}, u32[]{:S(2)}, u32[]{:S(2)}) collective-permute-start(f32[1,2,128,128]{3,2,1,0:T(8,128)S(1)} %fusion.351), channel_id=1, source_target_pairs={{0,16},{16,32},{32,48},{48,64},{64,80},{80,96},{96,112},{112,128},... | collective-permute-start | bytes 393224 | tf_op jit(solution)/shard_map/while/body/eval_jaxpr/ppermute | solution.py:19
  156.9 8.4 %collective-permute-start = (f32[1,2,128,128]{3,2,1,0:T(8,128)S(1)}, f32[1,2,128,128]{3,2,1,0:T(8,128)S(1)}, u32[]{:S(2)}, u32[]{:S(2)}) collective-permute-start(f32[1,2,128,128]{3,2,1,0:T(8,128)S(1)} %fusion.351), channel_id=1, source_target_pairs={{0,16},{16,32},{32,48},{48,64},{64,80},{80,96},{96,112},{112,128},... | collective-permute-start | bytes 393224 | tf_op jit(solution)/shard_map/while/body/eval_jaxpr/ppermute | solution.py:19
  165.6 8.4 %collective-permute-start = (f32[1,2,128,128]{3,2,1,0:T(8,128)S(1)}, f32[1,2,128,128]{3,2,1,0:T(8,128)S(1)}, u32[]{:S(2)}, u32[]{:S(2)}) collective-permute-start(f32[1,2,128,128]{3,2,1,0:T(8,128)S(1)} %fusion.351), channel_id=1, source_target_pairs={{0,16},{16,32},{32,48},{48,64},{64,80},{80,96},{96,112},{112,128},... | collective-permute-start | bytes 393224 | tf_op jit(solution)/shard_map/while/body/eval_jaxpr/ppermute | solution.py:19
  174.2 8.4 %collective-permute-start = (f32[1,2,128,128]{3,2,1,0:T(8,128)S(1)}, f32[1,2,128,128]{3,2,1,0:T(8,128)S(1)}, u32[]{:S(2)}, u32[]{:S(2)}) collective-permute-start(f32[1,2,128,128]{3,2,1,0:T(8,128)S(1)} %fusion.351), channel_id=1, source_target_pairs={{0,16},{16,32},{32,48},{48,64},{64,80},{80,96},{96,112},{112,128},... | collective-permute-start | bytes 393224 | tf_op jit(solution)/shard_map/while/body/eval_jaxpr/ppermute | solution.py:19
  182.9 8.4 %collective-permute-start = (f32[1,2,128,128]{3,2,1,0:T(8,128)S(1)}, f32[1,2,128,128]{3,2,1,0:T(8,128)S(1)}, u32[]{:S(2)}, u32[]{:S(2)}) collective-permute-start(f32[1,2,128,128]{3,2,1,0:T(8,128)S(1)} %fusion.351), channel_id=1, source_target_pairs={{0,16},{16,32},{32,48},{48,64},{64,80},{80,96},{96,112},{112,128},... | collective-permute-start | bytes 393224 | tf_op jit(solution)/shard_map/while/body/eval_jaxpr/ppermute | solution.py:19
  191.6 8.4 %collective-permute-start = (f32[1,2,128,128]{3,2,1,0:T(8,128)S(1)}, f32[1,2,128,128]{3,2,1,0:T(8,128)S(1)}, u32[]{:S(2)}, u32[]{:S(2)}) collective-permute-start(f32[1,2,128,128]{3,2,1,0:T(8,128)S(1)} %fusion.351), channel_id=1, source_target_pairs={{0,16},{16,32},{32,48},{48,64},{64,80},{80,96},{96,112},{112,128},... | collective-permute-start | bytes 393224 | tf_op jit(solution)/shard_map/while/body/eval_jaxpr/ppermute | solution.py:19
  200.3 8.4 %collective-permute-start = (f32[1,2,128,128]{3,2,1,0:T(8,128)S(1)}, f32[1,2,128,128]{3,2,1,0:T(8,128)S(1)}, u32[]{:S(2)}, u32[]{:S(2)}) collective-permute-start(f32[1,2,128,128]{3,2,1,0:T(8,128)S(1)} %fusion.351), channel_id=1, source_target_pairs={{0,16},{16,32},{32,48},{48,64},{64,80},{80,96},{96,112},{112,128},... | collective-permute-start | bytes 393224 | tf_op jit(solution)/shard_map/while/body/eval_jaxpr/ppermute | solution.py:19
  208.9 8.4 %collective-permute-start = (f32[1,2,128,128]{3,2,1,0:T(8,128)S(1)}, f32[1,2,128,128]{3,2,1,0:T(8,128)S(1)}, u32[]{:S(2)}, u32[]{:S(2)}) collective-permute-start(f32[1,2,128,128]{3,2,1,0:T(8,128)S(1)} %fusion.351), channel_id=1, source_target_pairs={{0,16},{16,32},{32,48},{48,64},{64,80},{80,96},{96,112},{112,128},... | collective-permute-start | bytes 393224 | tf_op jit(solution)/shard_map/while/body/eval_jaxpr/ppermute | solution.py:19
  217.6 8.4 %collective-permute-start = (f32[1,2,128,128]{3,2,1,0:T(8,128)S(1)}, f32[1,2,128,128]{3,2,1,0:T(8,128)S(1)}, u32[]{:S(2)}, u32[]{:S(2)}) collective-permute-start(f32[1,2,128,128]{3,2,1,0:T(8,128)S(1)} %fusion.351), channel_id=1, source_target_pairs={{0,16},{16,32},{32,48},{48,64},{64,80},{80,96},{96,112},{112,128},... | collective-permute-start | bytes 393224 | tf_op jit(solution)/shard_map/while/body/eval_jaxpr/ppermute | solution.py:19
  226.3 8.4 %collective-permute-start = (f32[1,2,128,128]{3,2,1,0:T(8,128)S(1)}, f32[1,2,128,128]{3,2,1,0:T(8,128)S(1)}, u32[]{:S(2)}, u32[]{:S(2)}) collective-permute-start(f32[1,2,128,128]{3,2,1,0:T(8,128)S(1)} %fusion.351), channel_id=1, source_target_pairs={{0,16},{16,32},{32,48},{48,64},{64,80},{80,96},{96,112},{112,128},... | collective-permute-start | bytes 393224 | tf_op jit(solution)/shard_map/while/body/eval_jaxpr/ppermute | solution.py:19
  234.9 8.4 %collective-permute-start = (f32[1,2,128,128]{3,2,1,0:T(8,128)S(1)}, f32[1,2,128,128]{3,2,1,0:T(8,128)S(1)}, u32[]{:S(2)}, u32[]{:S(2)}) collective-permute-start(f32[1,2,128,128]{3,2,1,0:T(8,128)S(1)} %fusion.351), channel_id=1, source_target_pairs={{0,16},{16,32},{32,48},{48,64},{64,80},{80,96},{96,112},{112,128},... | collective-permute-start | bytes 393224 | tf_op jit(solution)/shard_map/while/body/eval_jaxpr/ppermute | solution.py:19
  243.6 8.4 %collective-permute-start = (f32[1,2,128,128]{3,2,1,0:T(8,128)S(1)}, f32[1,2,128,128]{3,2,1,0:T(8,128)S(1)}, u32[]{:S(2)}, u32[]{:S(2)}) collective-permute-start(f32[1,2,128,128]{3,2,1,0:T(8,128)S(1)} %fusion.351), channel_id=1, source_target_pairs={{0,16},{16,32},{32,48},{48,64},{64,80},{80,96},{96,112},{112,128},... | collective-permute-start | bytes 393224 | tf_op jit(solution)/shard_map/while/body/eval_jaxpr/ppermute | solution.py:19
  252.3 8.4 %collective-permute-start = (f32[1,2,128,128]{3,2,1,0:T(8,128)S(1)}, f32[1,2,128,128]{3,2,1,0:T(8,128)S(1)}, u32[]{:S(2)}, u32[]{:S(2)}) collective-permute-start(f32[1,2,128,128]{3,2,1,0:T(8,128)S(1)} %fusion.351), channel_id=1, source_target_pairs={{0,16},{16,32},{32,48},{48,64},{64,80},{80,96},{96,112},{112,128},... | collective-permute-start | bytes 393224 | tf_op jit(solution)/shard_map/while/body/eval_jaxpr/ppermute | solution.py:19
  260.9 8.4 %collective-permute-start = (f32[1,2,128,128]{3,2,1,0:T(8,128)S(1)}, f32[1,2,128,128]{3,2,1,0:T(8,128)S(1)}, u32[]{:S(2)}, u32[]{:S(2)}) collective-permute-start(f32[1,2,128,128]{3,2,1,0:T(8,128)S(1)} %fusion.351), channel_id=1, source_target_pairs={{0,16},{16,32},{32,48},{48,64},{64,80},{80,96},{96,112},{112,128},... | collective-permute-start | bytes 393224 | tf_op jit(solution)/shard_map/while/body/eval_jaxpr/ppermute | solution.py:19
  269.6 8.4 %collective-permute-start = (f32[1,2,128,128]{3,2,1,0:T(8,128)S(1)}, f32[1,2,128,128]{3,2,1,0:T(8,128)S(1)}, u32[]{:S(2)}, u32[]{:S(2)}) collective-permute-start(f32[1,2,128,128]{3,2,1,0:T(8,128)S(1)} %fusion.351), channel_id=1, source_target_pairs={{0,16},{16,32},{32,48},{48,64},{64,80},{80,96},{96,112},{112,128},... | collective-permute-start | bytes 393224 | tf_op jit(solution)/shard_map/while/body/eval_jaxpr/ppermute | solution.py:19
  278.3 8.4 %collective-permute-start = (f32[1,2,128,128]{3,2,1,0:T(8,128)S(1)}, f32[1,2,128,128]{3,2,1,0:T(8,128)S(1)}, u32[]{:S(2)}, u32[]{:S(2)}) collective-permute-start(f32[1,2,128,128]{3,2,1,0:T(8,128)S(1)} %fusion.351), channel_id=1, source_target_pairs={{0,16},{16,32},{32,48},{48,64},{64,80},{80,96},{96,112},{112,128},... | collective-permute-start | bytes 393224 | tf_op jit(solution)/shard_map/while/body/eval_jaxpr/ppermute | solution.py:19
  287.0 8.4 %collective-permute-start = (f32[1,2,128,128]{3,2,1,0:T(8,128)S(1)}, f32[1,2,128,128]{3,2,1,0:T(8,128)S(1)}, u32[]{:S(2)}, u32[]{:S(2)}) collective-permute-start(f32[1,2,128,128]{3,2,1,0:T(8,128)S(1)} %fusion.351), channel_id=1, source_target_pairs={{0,16},{16,32},{32,48},{48,64},{64,80},{80,96},{96,112},{112,128},... | collective-permute-start | bytes 393224 | tf_op jit(solution)/shard_map/while/body/eval_jaxpr/ppermute | solution.py:19
  390.5 15.3 %collective-permute-start.1 = (f32[1,2,128,128]{3,2,1,0:T(8,128)S(1)}, f32[1,2,128,128]{3,2,1,0:T(8,128)S(1)}, u32[]{:S(2)}, u32[]{:S(2)}) collective-permute-start(f32[1,2,128,128]{3,2,1,0:T(8,128)S(1)} %fusion.354), channel_id=1, source_target_pairs={{16,0},{32,16},{48,32},{64,48},{80,64},{96,80},{112,96},{128,112},... | collective-permute-start | bytes 393224 | tf_op jit(solution)/shard_map/while/body/eval_jaxpr/ppermute | solution.py:19
  406.1 8.4 %collective-permute-start.1 = (f32[1,2,128,128]{3,2,1,0:T(8,128)S(1)}, f32[1,2,128,128]{3,2,1,0:T(8,128)S(1)}, u32[]{:S(2)}, u32[]{:S(2)}) collective-permute-start(f32[1,2,128,128]{3,2,1,0:T(8,128)S(1)} %fusion.354), channel_id=1, source_target_pairs={{16,0},{32,16},{48,32},{64,48},{80,64},{96,80},{112,96},{128,112},... | collective-permute-start | bytes 393224 | tf_op jit(solution)/shard_map/while/body/eval_jaxpr/ppermute | solution.py:19
  414.8 8.4 %collective-permute-start.1 = (f32[1,2,128,128]{3,2,1,0:T(8,128)S(1)}, f32[1,2,128,128]{3,2,1,0:T(8,128)S(1)}, u32[]{:S(2)}, u32[]{:S(2)}) collective-permute-start(f32[1,2,128,128]{3,2,1,0:T(8,128)S(1)} %fusion.354), channel_id=1, source_target_pairs={{16,0},{32,16},{48,32},{64,48},{80,64},{96,80},{112,96},{128,112},... | collective-permute-start | bytes 393224 | tf_op jit(solution)/shard_map/while/body/eval_jaxpr/ppermute | solution.py:19
  423.4 8.4 %collective-permute-start.1 = (f32[1,2,128,128]{3,2,1,0:T(8,128)S(1)}, f32[1,2,128,128]{3,2,1,0:T(8,128)S(1)}, u32[]{:S(2)}, u32[]{:S(2)}) collective-permute-start(f32[1,2,128,128]{3,2,1,0:T(8,128)S(1)} %fusion.354), channel_id=1, source_target_pairs={{16,0},{32,16},{48,32},{64,48},{80,64},{96,80},{112,96},{128,112},... | collective-permute-start | bytes 393224 | tf_op jit(solution)/shard_map/while/body/eval_jaxpr/ppermute | solution.py:19
  432.1 8.4 %collective-permute-start.1 = (f32[1,2,128,128]{3,2,1,0:T(8,128)S(1)}, f32[1,2,128,128]{3,2,1,0:T(8,128)S(1)}, u32[]{:S(2)}, u32[]{:S(2)}) collective-permute-start(f32[1,2,128,128]{3,2,1,0:T(8,128)S(1)} %fusion.354), channel_id=1, source_target_pairs={{16,0},{32,16},{48,32},{64,48},{80,64},{96,80},{112,96},{128,112},... | collective-permute-start | bytes 393224 | tf_op jit(solution)/shard_map/while/body/eval_jaxpr/ppermute | solution.py:19
  440.8 8.4 %collective-permute-start.1 = (f32[1,2,128,128]{3,2,1,0:T(8,128)S(1)}, f32[1,2,128,128]{3,2,1,0:T(8,128)S(1)}, u32[]{:S(2)}, u32[]{:S(2)}) collective-permute-start(f32[1,2,128,128]{3,2,1,0:T(8,128)S(1)} %fusion.354), channel_id=1, source_target_pairs={{16,0},{32,16},{48,32},{64,48},{80,64},{96,80},{112,96},{128,112},... | collective-permute-start | bytes 393224 | tf_op jit(solution)/shard_map/while/body/eval_jaxpr/ppermute | solution.py:19
  449.5 8.5 %collective-permute-start.1 = (f32[1,2,128,128]{3,2,1,0:T(8,128)S(1)}, f32[1,2,128,128]{3,2,1,0:T(8,128)S(1)}, u32[]{:S(2)}, u32[]{:S(2)}) collective-permute-start(f32[1,2,128,128]{3,2,1,0:T(8,128)S(1)} %fusion.354), channel_id=1, source_target_pairs={{16,0},{32,16},{48,32},{64,48},{80,64},{96,80},{112,96},{128,112},... | collective-permute-start | bytes 393224 | tf_op jit(solution)/shard_map/while/body/eval_jaxpr/ppermute | solution.py:19
  458.2 8.5 %collective-permute-start.1 = (f32[1,2,128,128]{3,2,1,0:T(8,128)S(1)}, f32[1,2,128,128]{3,2,1,0:T(8,128)S(1)}, u32[]{:S(2)}, u32[]{:S(2)}) collective-permute-start(f32[1,2,128,128]{3,2,1,0:T(8,128)S(1)} %fusion.354), channel_id=1, source_target_pairs={{16,0},{32,16},{48,32},{64,48},{80,64},{96,80},{112,96},{128,112},... | collective-permute-start | bytes 393224 | tf_op jit(solution)/shard_map/while/body/eval_jaxpr/ppermute | solution.py:19
  467.0 8.4 %collective-permute-start.1 = (f32[1,2,128,128]{3,2,1,0:T(8,128)S(1)}, f32[1,2,128,128]{3,2,1,0:T(8,128)S(1)}, u32[]{:S(2)}, u32[]{:S(2)}) collective-permute-start(f32[1,2,128,128]{3,2,1,0:T(8,128)S(1)} %fusion.354), channel_id=1, source_target_pairs={{16,0},{32,16},{48,32},{64,48},{80,64},{96,80},{112,96},{128,112},... | collective-permute-start | bytes 393224 | tf_op jit(solution)/shard_map/while/body/eval_jaxpr/ppermute | solution.py:19
  475.7 8.4 %collective-permute-start.1 = (f32[1,2,128,128]{3,2,1,0:T(8,128)S(1)}, f32[1,2,128,128]{3,2,1,0:T(8,128)S(1)}, u32[]{:S(2)}, u32[]{:S(2)}) collective-permute-start(f32[1,2,128,128]{3,2,1,0:T(8,128)S(1)} %fusion.354), channel_id=1, source_target_pairs={{16,0},{32,16},{48,32},{64,48},{80,64},{96,80},{112,96},{128,112},... | collective-permute-start | bytes 393224 | tf_op jit(solution)/shard_map/while/body/eval_jaxpr/ppermute | solution.py:19
  484.4 8.4 %collective-permute-start.1 = (f32[1,2,128,128]{3,2,1,0:T(8,128)S(1)}, f32[1,2,128,128]{3,2,1,0:T(8,128)S(1)}, u32[]{:S(2)}, u32[]{:S(2)}) collective-permute-start(f32[1,2,128,128]{3,2,1,0:T(8,128)S(1)} %fusion.354), channel_id=1, source_target_pairs={{16,0},{32,16},{48,32},{64,48},{80,64},{96,80},{112,96},{128,112},... | collective-permute-start | bytes 393224 | tf_op jit(solution)/shard_map/while/body/eval_jaxpr/ppermute | solution.py:19
  493.0 8.4 %collective-permute-start.1 = (f32[1,2,128,128]{3,2,1,0:T(8,128)S(1)}, f32[1,2,128,128]{3,2,1,0:T(8,128)S(1)}, u32[]{:S(2)}, u32[]{:S(2)}) collective-permute-start(f32[1,2,128,128]{3,2,1,0:T(8,128)S(1)} %fusion.354), channel_id=1, source_target_pairs={{16,0},{32,16},{48,32},{64,48},{80,64},{96,80},{112,96},{128,112},... | collective-permute-start | bytes 393224 | tf_op jit(solution)/shard_map/while/body/eval_jaxpr/ppermute | solution.py:19
  501.7 8.4 %collective-permute-start.1 = (f32[1,2,128,128]{3,2,1,0:T(8,128)S(1)}, f32[1,2,128,128]{3,2,1,0:T(8,128)S(1)}, u32[]{:S(2)}, u32[]{:S(2)}) collective-permute-start(f32[1,2,128,128]{3,2,1,0:T(8,128)S(1)} %fusion.354), channel_id=1, source_target_pairs={{16,0},{32,16},{48,32},{64,48},{80,64},{96,80},{112,96},{128,112},... | collective-permute-start | bytes 393224 | tf_op jit(solution)/shard_map/while/body/eval_jaxpr/ppermute | solution.py:19
  510.4 8.4 %collective-permute-start.1 = (f32[1,2,128,128]{3,2,1,0:T(8,128)S(1)}, f32[1,2,128,128]{3,2,1,0:T(8,128)S(1)}, u32[]{:S(2)}, u32[]{:S(2)}) collective-permute-start(f32[1,2,128,128]{3,2,1,0:T(8,128)S(1)} %fusion.354), channel_id=1, source_target_pairs={{16,0},{32,16},{48,32},{64,48},{80,64},{96,80},{112,96},{128,112},... | collective-permute-start | bytes 393224 | tf_op jit(solution)/shard_map/while/body/eval_jaxpr/ppermute | solution.py:19
  527.7 8.4 %collective-permute-start.1 = (f32[1,2,128,128]{3,2,1,0:T(8,128)S(1)}, f32[1,2,128,128]{3,2,1,0:T(8,128)S(1)}, u32[]{:S(2)}, u32[]{:S(2)}) collective-permute-start(f32[1,2,128,128]{3,2,1,0:T(8,128)S(1)} %fusion.354), channel_id=1, source_target_pairs={{16,0},{32,16},{48,32},{64,48},{80,64},{96,80},{112,96},{128,112},... | collective-permute-start | bytes 393224 | tf_op jit(solution)/shard_map/while/body/eval_jaxpr/ppermute | solution.py:19
  545.1 8.4 %collective-permute-start.1 = (f32[1,2,128,128]{3,2,1,0:T(8,128)S(1)}, f32[1,2,128,128]{3,2,1,0:T(8,128)S(1)}, u32[]{:S(2)}, u32[]{:S(2)}) collective-permute-start(f32[1,2,128,128]{3,2,1,0:T(8,128)S(1)} %fusion.354), channel_id=1, source_target_pairs={{16,0},{32,16},{48,32},{64,48},{80,64},{96,80},{112,96},{128,112},... | collective-permute-start | bytes 393224 | tf_op jit(solution)/shard_map/while/body/eval_jaxpr/ppermute | solution.py:19
  553.7 8.4 %collective-permute-start.1 = (f32[1,2,128,128]{3,2,1,0:T(8,128)S(1)}, f32[1,2,128,128]{3,2,1,0:T(8,128)S(1)}, u32[]{:S(2)}, u32[]{:S(2)}) collective-permute-start(f32[1,2,128,128]{3,2,1,0:T(8,128)S(1)} %fusion.354), channel_id=1, source_target_pairs={{16,0},{32,16},{48,32},{64,48},{80,64},{96,80},{112,96},{128,112},... | collective-permute-start | bytes 393224 | tf_op jit(solution)/shard_map/while/body/eval_jaxpr/ppermute | solution.py:19
  562.4 8.4 %collective-permute-start.1 = (f32[1,2,128,128]{3,2,1,0:T(8,128)S(1)}, f32[1,2,128,128]{3,2,1,0:T(8,128)S(1)}, u32[]{:S(2)}, u32[]{:S(2)}) collective-permute-start(f32[1,2,128,128]{3,2,1,0:T(8,128)S(1)} %fusion.354), channel_id=1, source_target_pairs={{16,0},{32,16},{48,32},{64,48},{80,64},{96,80},{112,96},{128,112},... | collective-permute-start | bytes 393224 | tf_op jit(solution)/shard_map/while/body/eval_jaxpr/ppermute | solution.py:19
  (19 other events, 561.0 us)
Sparse Core Ops, SparseCore 0:
  363.8 102.0 reduce-scatter.1
where the time goes:
time: 709 us; the launch traced here: 706 us
  waiting for transfers between devices  266 us (38%)
  starting transfers between devices  259 us (37%)
  other arithmetic  89.1 us (13%)
  matrix products  38.5 us (5%)
  blocking collectives  32.1 us (5%)
  between operations  14.4 us (2%)
    ppermute x62, waiting for transfers between devices, from_behind(): lax.ppermute(value, axis, [(source, source + steps) for source in range(i...  266 us
    ppermute x62, starting transfers between devices, from_behind(): lax.ppermute(value, axis, [(source, source + steps) for source in range(i...  258 us
    another operation x16, other arithmetic, span_advance(): lax.linalg.triangular_solve(lower_mix, right_side, left_side=True, lower=...  39.9 us
    all_gather x1, blocking collectives, per_device(): full_grad = lax.all_gather(out_grad, 'head', axis=1, tiled=True)  32.1 us
    another operation x10, other arithmetic, retreat(): lax.linalg.triangular_solve(lower_mix, decay_cum[:, None] * key_block, le...  20 us
    another operation x8, other arithmetic, single_advance(): lax.linalg.triangular_solve(lower_mix, stacked, left_side=True, lower=Tru...  19.9 us
    dot_general x62, matrix products, matmul_states(): return jnp.einsum('abij,abjk->abik', left, right, precision=highest)  16.5 us
  transfers between devices with their start and end apart: 63, of which 62 were waited for; matrix products, arithmetic and copies ran while one was open for 9% of the time, Pallas kernels for 0%

commit v1 on v0

v1 whole, which is shorter than its diff:
```python
import functools

import jax
import jax.numpy as jnp
from jax import lax
from jax.experimental import pallas as pl
from jax.experimental.pallas import tpu as pltpu
from jax.sharding import PartitionSpec as P

WIDTH = 128
norm_eps = 1e-06
gate_step = 1e-06
beta_steps = 256.0
F32 = jnp.float32
BF16 = jnp.bfloat16
HIGHEST = lax.Precision.HIGHEST


def mm(left, right, left_dim=1, right_dim=0):
    return lax.dot_general(
        left,
        right,
        (((left_dim,), (right_dim,)), ((), ())),
        precision=HIGHEST,
        preferred_element_type=F32,
    )


def mm_bf16(left, right, left_dim=1, right_dim=0):
    return lax.dot_general(
        left, right, (((left_dim,), (right_dim,)), ((), ())), preferred_element_type=F32
    )


def ids(length):
    rows = lax.broadcasted_iota(jnp.int32, (length, length), 0)
    cols = lax.broadcasted_iota(jnp.int32, (length, length), 1)
    return rows, cols


def unit_lower_inverse(lower, rows, cols):
    length = lower.shape[0]
    shift = 1
    pair = jnp.right_shift(rows, 1) == jnp.right_shift(cols, 1)
    inverse = jnp.where(rows == cols, 1.0, jnp.where(pair, -lower, 0.0))
    while (1 << shift) < length:
        wider = jnp.right_shift(rows, shift + 1) == jnp.right_shift(cols, shift + 1)
        inner = jnp.right_shift(rows, shift) == jnp.right_shift(cols, shift)
        off = jnp.where(wider & jnp.logical_not(inner), lower, 0.0)
        inverse = inverse - mm(inverse, mm(off, inverse))
        shift += 1
    return inverse


def inverse_norm(block):
    return lax.rsqrt(jnp.sum(block * block, axis=-1, keepdims=True) + norm_eps)


def prepare_kernel(
    q_ref, k_ref, v_ref, gate_ref, beta_ref,
    send_ref, tmat_ref, mix_ref, ratio_ref, uw_ref, probe_ref, local_ref, cols_ref,
):
    length = q_ref.shape[0]
    group = gate_ref.shape[1]
    dests = send_ref.shape[0]
    share = dests // group
    part = WIDTH // share
    q = q_ref[...].astype(F32)
    k = k_ref[...].astype(F32)
    qn = q * inverse_norm(q) * WIDTH ** (-0.5)
    kn = k * inverse_norm(k)
    rows, cols = ids(length)
    gram = mm(kn, kn, 1, 1)
    query_key = mm(qn, kn, 1, 1)
    tri = jnp.where(rows >= cols, 1.0, 0.0)
    logs = jnp.log1p(-(gate_ref[...].astype(F32) * gate_step))
    betas = beta_ref[...].astype(F32) / beta_steps
    for head in range(group):
        span = slice(head * WIDTH, (head + 1) * WIDTH)
        log_cum = mm(tri, jnp.broadcast_to(logs[:, head : head + 1], (length, length)))
        beta_col = jnp.broadcast_to(betas[:, head : head + 1], (length, length))
        ratio = jnp.exp(log_cum - log_cum.T) * beta_col.T
        ratio = jnp.where(rows >= cols, ratio, 0.0)
        lower = jnp.where(rows > cols, ratio * gram, 0.0)
        mix = ratio * query_key
        inverse = unit_lower_inverse(lower, rows, cols)
        decay = jnp.exp(log_cum)
        value = v_ref[:, span].astype(F32)
        uw = mm(inverse, jnp.concatenate([value, decay * kn], axis=1))
        mixed = mm(mix, uw)
        last = log_cum[length - 1 :, :]
        weight = beta_col * jnp.exp(last - log_cum)
        weighted = weight * kn
        uv, wk = uw[:, :WIDTH], uw[:, WIDTH:]
        transition = jnp.where(rows == cols, jnp.exp(last), 0.0) - mm(weighted, wk, 0, 0)
        state_t = mm(uv, weighted, 0, 0)
        for dest in range(share):
            send_ref[head * share + dest, :WIDTH, :] = transition
            send_ref[head * share + dest, WIDTH:, :] = state_t[dest * part : (dest + 1) * part, :]
        tmat_ref[head] = inverse
        mix_ref[head] = mix
        ratio_ref[head] = ratio
        uw_ref[head] = uw
        probe_ref[head] = decay * qn - mixed[:, WIDTH:]
        local_ref[:, span] = mixed[:, :WIDTH]
        cols_ref[head, 0] = decay
        cols_ref[head, 1] = weight


def cotangent_kernel(grad_ref, w_ref, probe_ref, cot_ref, send_ref):
    blocks = grad_ref.shape[0]
    group = probe_ref.shape[0]
    total = jnp.zeros(cot_ref.shape, F32)
    for block in range(0, blocks, 2):
        left = jnp.concatenate([grad_ref[block], grad_ref[block + 1]], axis=1)
        total += mm_bf16(left, w_ref[:, block * WIDTH : (block + 2) * WIDTH], 1, 1)
    cot_ref[...] = total
    dests, part, _ = send_ref.shape
    share = dests // group
    for head in range(group):
        carried_t = mm(total[:, head * WIDTH : (head + 1) * WIDTH], probe_ref[head], 0, 0)
        send_ref[head * share : (head + 1) * share] = carried_t.reshape(share, part, WIDTH)


def forward_scan_kernel(got_ref, send_ref):
    slabs, part = send_ref.shape[0], send_ref.shape[1]
    state = jnp.zeros((part, WIDTH), F32)
    for slab in range(slabs):
        send_ref[slab] = state
        if slab < slabs - 1:
            state = mm(state, got_ref[slab, :WIDTH, :], 1, 1) + got_ref[slab, WIDTH:, :]


def backward_scan_kernel(got_ref, cot_ref, send_ref):
    slabs, part = send_ref.shape[0], send_ref.shape[1]
    state = jnp.zeros((part, WIDTH), F32)
    for slab in reversed(range(slabs)):
        send_ref[slab] = state
        if slab > 0:
            state = mm(state, got_ref[slab, :WIDTH, :], 1, 0) + cot_ref[slab]


def output_kernel(state_ref, probe_ref, local_ref, grad_ref, attn_ref, send_ref):
    group = probe_ref.shape[0]
    dests, part, _ = send_ref.shape
    share = dests // group
    outs = []
    for head in range(group):
        state_t = state_ref[head * share : (head + 1) * share].reshape(WIDTH, WIDTH)
        outs.append(mm(probe_ref[head], state_t, 1, 1))
    attn = (jnp.concatenate(outs, axis=1) + local_ref[...]).astype(BF16)
    attn_ref[...] = attn
    for block in range(0, grad_ref.shape[0], 2):
        right = jnp.concatenate([grad_ref[block], grad_ref[block + 1]], axis=1)
        term = mm_bf16(attn, right, 0, 0)
        send_ref[:, :, block * WIDTH : (block + 2) * WIDTH] = term.reshape(
            dests, part, 2 * WIDTH
        ).astype(BF16)


def gradient_kernel(
    q_ref, k_ref, state_ref, end_ref, cot_ref, tmat_ref, mix_ref, ratio_ref, uw_ref, cols_ref,
    q_grad_ref, k_grad_ref, v_grad_ref,
):
    length = q_ref.shape[0]
    group = tmat_ref.shape[0]
    share = state_ref.shape[0] // group
    q = q_ref[...].astype(F32)
    k = k_ref[...].astype(F32)
    q_inv = inverse_norm(q)
    k_inv = inverse_norm(k)
    qn = q * q_inv * WIDTH ** (-0.5)
    kn = k * k_inv
    rows, cols = ids(length)
    dq = jnp.zeros((length, WIDTH), F32)
    dk = jnp.zeros((length, WIDTH), F32)
    for head in range(group):
        span = slice(head * WIDTH, (head + 1) * WIDTH)
        state_t = state_ref[head * share : (head + 1) * share].reshape(WIDTH, WIDTH)
        end_t = end_ref[head * share : (head + 1) * share].reshape(WIDTH, WIDTH)
        cot = cot_ref[:, span]
        ratio = ratio_ref[head]
        decay = cols_ref[head, 0]
        weight = cols_ref[head, 1]
        new_values = uw_ref[head, :, :WIDTH] - mm(uw_ref[head, :, WIDTH:], state_t, 1, 1)
        d_new = mm(mix_ref[head], cot, 0, 0) + mm(weight * kn, end_t, 1, 1)
        d_value = mm(tmat_ref[head], d_new, 0, 0)
        v_grad_ref[:, span] = d_value
        d_mix = mm(cot, new_values, 1, 1) * ratio
        d_gram = jnp.where(rows > cols, -mm(d_value, new_values, 1, 1) * ratio, 0.0)
        dq += decay * mm(cot, state_t) + mm(d_mix, kn)
        dk += (
            weight * mm(new_values, end_t)
            - decay * mm(d_value, state_t)
            + mm(d_mix, qn, 0, 0)
            + mm(d_gram + d_gram.T, kn)
        )
    dq = dq * WIDTH ** (-0.5)
    q_grad_ref[...] = q_inv * dq - q * (
        q_inv * q_inv * q_inv * jnp.sum(q * dq, axis=-1, keepdims=True)
    )
    k_grad_ref[...] = k_inv * dk - k * (
        k_inv * k_inv * k_inv * jnp.sum(k * dk, axis=-1, keepdims=True)
    )


def call(kernel, outs, flops, *operands):
    moved = sum(x.size * x.dtype.itemsize for x in operands) + sum(
        x.size * x.dtype.itemsize for x in outs
    )
    return pl.pallas_call(
        kernel,
        out_shape=outs,
        name=kernel.__name__,
        cost_estimate=pl.CostEstimate(flops=flops, bytes_accessed=moved, transcendentals=0),
        compiler_params=pltpu.CompilerParams(vmem_limit_bytes=48 << 20),
    )(*operands)


def shape(dims, dtype=F32):
    return jax.ShapeDtypeStruct(dims, dtype)


def swap(value, axis):
    return lax.all_to_all(value, axis, 0, 0, tiled=True)


def per_device(queries, keys, values, gate_code, beta_code, out_grad, w_out):
    length = queries.shape[0]
    group = values.shape[1] // queries.shape[1]
    slabs = lax.axis_size("seq")
    heads = lax.axis_size("head")
    share = slabs // group
    part = WIDTH // share
    square = (group, length, WIDTH)
    full_grad = swap(jnp.broadcast_to(out_grad[None], (heads, length, WIDTH)), "head")
    send, tmat, mix, ratio, uw, probe, local, columns = call(
        prepare_kernel,
        [
            shape((slabs, WIDTH + part, WIDTH)),
            shape(square),
            shape(square),
            shape(square),
            shape((group, length, 2 * WIDTH)),
            shape(square),
            shape((length, group * WIDTH)),
            shape((group, 2, length, WIDTH)),
        ],
        1 << 30,
        queries, keys, values, gate_code, beta_code,
    )
    got = swap(send, "seq")
    cot, cot_send = call(
        cotangent_kernel,
        [shape((length, group * WIDTH)), shape((slabs, part, WIDTH))],
        1 << 28,
        full_grad, w_out, probe,
    )
    cot_got = swap(cot_send, "seq")
    (start_send,) = call(forward_scan_kernel, [shape((slabs, part, WIDTH))], 1 << 29, got)
    start = swap(start_send, "seq")
    (end_send,) = call(
        backward_scan_kernel, [shape((slabs, part, WIDTH))], 1 << 29, got, cot_got
    )
    end = swap(end_send, "seq")
    attn_out, grad_send = call(
        output_kernel,
        [shape((length, group * WIDTH), BF16), shape((slabs, part, heads * WIDTH), BF16)],
        1 << 28,
        start, probe, local, full_grad,
    )
    grad_got = swap(grad_send, "seq")
    q_grad, k_grad, v_grad = call(
        gradient_kernel,
        [shape((length, WIDTH)), shape((length, WIDTH)), shape((length, group * WIDTH))],
        1 << 29,
        queries, keys, start, end, cot, tmat, mix, ratio, uw, columns,
    )
    scaling = (length * slabs) ** (-0.5)
    weight_grad = jnp.sum(grad_got.astype(F32), axis=0) * scaling
    return (attn_out, q_grad, k_grad, v_grad, weight_grad)


def solution(mesh):
    in_specs = (
        P("seq", "head"),
        P("seq", "head"),
        P("seq", "head"),
        P("seq", "head"),
        P("seq", "head"),
        P("seq", "head"),
        P("head", None),
    )
    out_specs = (
        P("seq", "head"),
        P("seq", "head"),
        P("seq", "head"),
        P("seq", "head"),
        P(("head", "seq"), None),
    )
    return jax.shard_map(
        per_device, mesh=mesh, in_specs=in_specs, out_specs=out_specs, check_vma=False
    )
```

time: 709 us -> 153 us (0.22)
  the two profiles are of different devices: /device:TPU:7 before, /device:TPU:1 now
where the time goes in v1:
time: 153 us; the launch traced here: 152 us
  waiting for transfers between devices  55.3 us (36%)
  starting transfers between devices  54.4 us (36%)
  Pallas kernels  30.8 us (20%)
  local copies, waits for them, and re-layouts  9.61 us (6%)
    all_to_all x6, waiting for transfers between devices, swap(): return lax.all_to_all(value, axis, 0, 0, tiled=True)  55.3 us
    all_to_all x6, starting transfers between devices, swap(): return lax.all_to_all(value, axis, 0, 0, tiled=True)  54.4 us
    pallas_call x6, Pallas kernels, call(): pl.pallas_call(kernel, out_shape=outs, name=kernel.__name__, cost_estimat...  30.8 us
    unnamed x32, local copies, waits for them, and re-layouts  7.95 us
  transfers between devices with their start and end apart: 6, of which 5 were waited for; matrix products, arithmetic and copies ran while one was open for 1% of the time, Pallas kernels for 20%

profile of v1, /device:TPU:1, one launch (start us, length us, event | category | flops | bytes accessed | tf_op | source)
XLA Modules:
  0.0 151.7 jit_solution(1462343218217414738)
XLA Ops:
  0.6 1.7 %broadcast_in_dim.2 = bf16[16,128,128]{2,1,0:T(8,128)(2,1)} broadcast(bf16[128,128]{1,0:T(8,128)(2,1)} %param.12), dimensions={1,2} | broadcast | bytes 557056 | tf_op jit(solution)/shard_map/broadcast_in_dim | solution.py:236
  2.3 15.7 %all-to-all-start.2 = ((bf16[16,128,128]{2,1,0:T(8,128)(2,1)}), bf16[16,128,128]{2,1,0:T(8,128)(2,1)S(1)}, u32[]{:S(2)}, u32[]{:S(2)}) async-start(bf16[16,128,128]{2,1,0:T(8,128)(2,1)} %broadcast_in_dim.2), calls=%async_computation.2 | async-start | bytes 1048576 | tf_op jit(solution)/shard_map/all_to_all | solution.py:225
  18.0 0.8 copy.12.gate_ref
  18.8 0.8 copy.13.beta_ref
  19.6 0.0 copy-start.2
  19.6 0.8 copy-done.2
  20.5 0.0 copy-start.3
  20.5 0.8 copy-done.3
  21.2 0.0 copy-start.5
  21.2 0.8 copy-done.5
  22.0 7.6 %prepare_kernel.1 = (f32[32,136,128]{2,1,0:T(8,128)S(1)}, f32[2,128,128]{2,1,0:T(8,128)S(1)}, f32[2,128,128]{2,1,0:T(8,128)S(1)}, f32[2,128,128]{2,1,0:T(8,128)S...) custom-call(bf16[128,128]{1,0:T(8,128)(2,1)S(1)} %copy-done.3, ...), custom_call_target="tpu_custom_call" | custom-call | flops 1073741824 | bytes 3540992 | tf_op jit(solution)/shard_map/prepare_kernel/pallas_call | solution.py:211
  29.6 0.0 copy-start
  29.6 1.4 copy-done
  30.9 0.0 copy-start.7
  30.9 0.7 copy-done.7
  31.6 0.0 copy-start.9
  31.6 0.7 copy-done.9
  32.3 0.0 copy-start.11
  32.3 8.5 %all-to-all-done.2.grad_ref = bf16[16,128,128]{2,1,0:T(8,128)(2,1)S(1)} async-done(((bf16[16,128,128]{2,1,0:T(8,128)(2,1)}), bf16[16,128,128]{2,1,0:T(8,128)(2,1)S(1)}, u32[]{:S(2)}, u32[]{:S(2)}) %all-to-all-start.2) | async-done | bytes 524320 | tf_op jit(solution)/shard_map/all_to_all | solution.py:225
  40.9 0.0 copy-done.11
  40.9 0.0 copy-done.13
  40.9 14.3 %all-to-all-start = ((f32[32,136,128]{2,1,0:T(8,128)}), f32[32,136,128]{2,1,0:T(8,128)S(1)}, u32[]{:S(2)}, u32[]{:S(2)}) async-start(f32[32,136,128]{2,1,0:T(8,128)} %copy-done), calls=%async_computation | async-start | bytes 4456448 | tf_op jit(solution)/shard_map/all_to_all | solution.py:225
  55.2 0.0 copy-start.1
  55.2 1.2 copy-done.1
  56.4 1.6 %cotangent_kernel.1 = (f32[128,256]{1,0:T(8,128)S(1)}, f32[32,8,128]{2,1,0:T(8,128)}) custom-call(bf16[16,128,128]{2,1,0:T(8,128)(2,1)S(1)} %all-to-all-done.2.grad_ref, bf16[256,2048]{1,0:T(8,128)(2,1)S(1)} %copy-done.1, f32[2,128,128]{2,1,0:T(8,128)S(1)} %get-tuple-element.21.probe_ref), custom_call_target="tpu_custom_call" | custom-call | flops 268435456 | bytes 1966080 | tf_op jit(solution)/shard_map/cotangent_kernel/pallas_call | solution.py:211
  58.0 26.4 %all-to-all-done.got_ref = f32[32,136,128]{2,1,0:T(8,128)S(1)} async-done(((f32[32,136,128]{2,1,0:T(8,128)}), f32[32,136,128]{2,1,0:T(8,128)S(1)}, u32[]{:S(2)}, u32[]{:S(2)}) %all-to-all-start) | async-done | bytes 2228256 | tf_op jit(solution)/shard_map/all_to_all | solution.py:225
  84.5 6.0 %all-to-all-start.3 = ((f32[32,8,128]{2,1,0:T(8,128)}), f32[32,8,128]{2,1,0:T(8,128)S(1)}, u32[]{:S(2)}, u32[]{:S(2)}) async-start(f32[32,8,128]{2,1,0:T(8,128)} %get-tuple-element.24), calls=%async_computation.3 | async-start | bytes 262144 | tf_op jit(solution)/shard_map/all_to_all | solution.py:225
  90.5 9.5 %forward_scan_kernel.1 = f32[32,8,128]{2,1,0:T(8,128)} custom-call(f32[32,136,128]{2,1,0:T(8,128)S(1)} %all-to-all-done.got_ref), custom_call_target="tpu_custom_call" | custom-call | flops 536870912 | bytes 2359296 | tf_op jit(solution)/shard_map/forward_scan_kernel/pallas_call | solution.py:211
  100.0 0.0 all-to-all-done.3.cot_ref
  100.0 7.5 %all-to-all-start.1 = ((f32[32,8,128]{2,1,0:T(8,128)}), f32[32,8,128]{2,1,0:T(8,128)S(1)}, u32[]{:S(2)}, u32[]{:S(2)}) async-start(f32[32,8,128]{2,1,0:T(8,128)} %forward_scan_kernel.1), calls=%async_computation.1 | async-start | bytes 262144 | tf_op jit(solution)/shard_map/all_to_all | solution.py:225
  107.5 6.9 %backward_scan_kernel.1 = f32[32,8,128]{2,1,0:T(8,128)} custom-call(f32[32,136,128]{2,1,0:T(8,128)S(1)} %all-to-all-done.got_ref, f32[32,8,128]{2,1,0:T(8,128)S(1)} %all-to-all-done.3.cot_ref), custom_call_target="tpu_custom_call" | custom-call | flops 536870912 | bytes 2490368 | tf_op jit(solution)/shard_map/backward_scan_kernel/pallas_call | solution.py:211
  114.4 0.0 copy-start.12
  114.4 0.0 copy-start.14
  114.4 0.7 all-to-all-done.1.state_ref
  115.1 6.8 %all-to-all-start.4 = ((f32[32,8,128]{2,1,0:T(8,128)}), f32[32,8,128]{2,1,0:T(8,128)S(1)}, u32[]{:S(2)}, u32[]{:S(2)}) async-start(f32[32,8,128]{2,1,0:T(8,128)} %backward_scan_kernel.1), calls=%async_computation.4 | async-start | bytes 262144 | tf_op jit(solution)/shard_map/all_to_all | solution.py:225
  122.0 1.8 %output_kernel.1 = (bf16[128,256]{1,0:T(8,128)(2,1)}, bf16[32,8,2048]{2,1,0:T(8,128)(2,1)}) custom-call(f32[32,8,128]{2,1,0:T(8,128)S(1)} %all-to-all-done.1.state_ref, f32[2,128,128]{2,1,0:T(8,128)S(1)} %get-tuple-element.21.probe_ref, f32[128,256]{1,0:T(8,128)S(1)} %get-tuple-element.22.local_ref, bf16[16,128,128]{2,1,0:T(8,128)(2,1)S(1)} %all-to-all-done.2.grad_ref), custom_call_target="tpu_custom_call" | custom-call | flops 268435456 | bytes 2031616 | tf_op jit(solution)/shard_map/output_kernel/pallas_call | solution.py:211
  123.8 5.8 %all-to-all-done.4.end_ref = f32[32,8,128]{2,1,0:T(8,128)S(1)} async-done(((f32[32,8,128]{2,1,0:T(8,128)}), f32[32,8,128]{2,1,0:T(8,128)S(1)}, u32[]{:S(2)}, u32[]{:S(2)}) %all-to-all-start.4) | async-done | bytes 131104 | tf_op jit(solution)/shard_map/all_to_all | solution.py:225
  129.6 4.0 %all-to-all-start.5 = ((bf16[32,8,2048]{2,1,0:T(8,128)(2,1)}), bf16[32,8,2048]{2,1,0:T(8,128)(2,1)S(1)}, u32[]{:S(2)}, u32[]{:S(2)}) async-start(bf16[32,8,2048]{2,1,0:T(8,128)(2,1)} %get-tuple-element.34), calls=%async_computation.5 | async-start | bytes 2097152 | tf_op jit(solution)/shard_map/all_to_all | solution.py:225
  133.6 0.0 copy-done.4
  133.6 0.0 copy-done.6
  133.6 0.0 copy-done.8
  133.6 0.0 copy-done.10
  133.6 0.0 copy-done.12
  133.6 0.0 copy-done.14
  133.6 3.4 %gradient_kernel.1 = (f32[128,128]{1,0:T(8,128)}, f32[128,128]{1,0:T(8,128)}, f32[128,256]{1,0:T(8,128)}) custom-call(bf16[128,128]{1,0:T(8,128)(2,1)S(1)} %copy-done.4, bf16[128,128]{1,0:T(8,128)(2,1)S(1)} %copy-done.6, f32[32,8,128]{2,1,0:T(8,128)S(1)} %all-to-all-done.1.state_ref, f32[32,8,128]{2,1,0:T(8,128)S(1)} %all-to-all-done.4.end_ref, ...), custom_call_target="tpu_custom_call" | custom-call | flops 536870912 | bytes 1638400 | tf_op jit(solution)/shard_map/gradient_kernel/pallas_call | solution.py:211
  137.0 13.9 %all-to-all-done.5 = bf16[32,8,2048]{2,1,0:T(8,128)(2,1)S(1)} async-done(((bf16[32,8,2048]{2,1,0:T(8,128)(2,1)}), bf16[32,8,2048]{2,1,0:T(8,128)(2,1)S(1)}, u32[]{:S(2)}, u32[]{:S(2)}) %all-to-all-start.5) | async-done | bytes 1048608 | tf_op jit(solution)/shard_map/all_to_all | solution.py:225
  150.9 0.2 convert_reduce_fusion
  151.0 0.6 broadcast_multiply_fusion
  (5 shorter events, 0.0 us)
Async XLA Ops:
  2.3 38.6 %all-to-all-start.2 = ((bf16[16,128,128]{2,1,0:T(8,128)(2,1)}), bf16[16,128,128]{2,1,0:T(8,128)(2,1)S(1)}, u32[]{:S(2)}, u32[]{:S(2)}) async-start(bf16[16,128,128]{2,1,0:T(8,128)(2,1)} %broadcast_in_dim.2), calls=%async_computation.2 | async-start | bytes 1048576 | tf_op jit(solution)/shard_map/all_to_all | solution.py:225
  19.6 0.8 copy-start.2
  20.5 0.8 copy-start.3
  21.2 0.8 copy-start.5
  29.6 1.4 copy-start
  30.9 0.7 copy-start.7
  31.6 0.7 copy-start.9
  32.3 8.5 %copy-start.11 = (f32[2,128,128]{2,1,0:T(8,128)}, f32[2,128,128]{2,1,0:T(8,128)S(1)}, u32[]{:S(2)}) copy-start(f32[2,128,128]{2,1,0:T(8,128)S(1)} %get-tuple-element.27.mix_ref) | copy-start | bytes 393220
  32.3 8.5 %copy-start.13 = (f32[2,128,128]{2,1,0:T(8,128)}, f32[2,128,128]{2,1,0:T(8,128)S(1)}, u32[]{:S(2)}) copy-start(f32[2,128,128]{2,1,0:T(8,128)S(1)} %get-tuple-element.28.ratio_ref) | copy-start | bytes 393220
  40.9 43.6 %all-to-all-start = ((f32[32,136,128]{2,1,0:T(8,128)}), f32[32,136,128]{2,1,0:T(8,128)S(1)}, u32[]{:S(2)}, u32[]{:S(2)}) async-start(f32[32,136,128]{2,1,0:T(8,128)} %copy-done), calls=%async_computation | async-start | bytes 4456448 | tf_op jit(solution)/shard_map/all_to_all | solution.py:225
  55.2 1.2 copy-start.1
  84.5 15.5 %all-to-all-start.3 = ((f32[32,8,128]{2,1,0:T(8,128)}), f32[32,8,128]{2,1,0:T(8,128)S(1)}, u32[]{:S(2)}, u32[]{:S(2)}) async-start(f32[32,8,128]{2,1,0:T(8,128)} %get-tuple-element.24), calls=%async_computation.3 | async-start | bytes 262144 | tf_op jit(solution)/shard_map/all_to_all | solution.py:225
  100.0 15.1 %all-to-all-start.1 = ((f32[32,8,128]{2,1,0:T(8,128)}), f32[32,8,128]{2,1,0:T(8,128)S(1)}, u32[]{:S(2)}, u32[]{:S(2)}) async-start(f32[32,8,128]{2,1,0:T(8,128)} %forward_scan_kernel.1), calls=%async_computation.1 | async-start | bytes 262144 | tf_op jit(solution)/shard_map/all_to_all | solution.py:225
  114.4 19.2 %copy-start.4 = (bf16[128,128]{1,0:T(8,128)(2,1)S(1)}, bf16[128,128]{1,0:T(8,128)(2,1)}, u32[]{:S(2)}) copy-start(bf16[128,128]{1,0:T(8,128)(2,1)} %q_ref.3) | copy-start | bytes 98308
  114.4 19.2 %copy-start.6 = (bf16[128,128]{1,0:T(8,128)(2,1)S(1)}, bf16[128,128]{1,0:T(8,128)(2,1)}, u32[]{:S(2)}) copy-start(bf16[128,128]{1,0:T(8,128)(2,1)} %k_ref.3) | copy-start | bytes 98308
  114.4 19.2 %copy-start.8 = (f32[2,128,256]{2,1,0:T(8,128)S(1)}, f32[2,128,256]{2,1,0:T(8,128)}, u32[]{:S(2)}) copy-start(f32[2,128,256]{2,1,0:T(8,128)} %copy-done.7) | copy-start | bytes 786436
  114.4 19.2 %copy-start.10 = (f32[2,2,128,128]{3,2,1,0:T(8,128)S(1)}, f32[2,2,128,128]{3,2,1,0:T(8,128)}, u32[]{:S(2)}) copy-start(f32[2,2,128,128]{3,2,1,0:T(8,128)} %copy-done.9) | copy-start | bytes 786436
  114.4 19.2 %copy-start.12 = (f32[2,128,128]{2,1,0:T(8,128)S(1)}, f32[2,128,128]{2,1,0:T(8,128)}, u32[]{:S(2)}) copy-start(f32[2,128,128]{2,1,0:T(8,128)} %copy-done.11) | copy-start | bytes 393220
  114.4 19.2 %copy-start.14 = (f32[2,128,128]{2,1,0:T(8,128)S(1)}, f32[2,128,128]{2,1,0:T(8,128)}, u32[]{:S(2)}) copy-start(f32[2,128,128]{2,1,0:T(8,128)} %copy-done.13) | copy-start | bytes 393220
  115.1 14.5 %all-to-all-start.4 = ((f32[32,8,128]{2,1,0:T(8,128)}), f32[32,8,128]{2,1,0:T(8,128)S(1)}, u32[]{:S(2)}, u32[]{:S(2)}) async-start(f32[32,8,128]{2,1,0:T(8,128)} %backward_scan_kernel.1), calls=%async_computation.4 | async-start | bytes 262144 | tf_op jit(solution)/shard_map/all_to_all | solution.py:225
  129.6 21.3 %all-to-all-start.5 = ((bf16[32,8,2048]{2,1,0:T(8,128)(2,1)}), bf16[32,8,2048]{2,1,0:T(8,128)(2,1)S(1)}, u32[]{:S(2)}, u32[]{:S(2)}) async-start(bf16[32,8,2048]{2,1,0:T(8,128)(2,1)} %get-tuple-element.34), calls=%async_computation.5 | async-start | bytes 2097152 | tf_op jit(solution)/shard_map/all_to_all | solution.py:225

commit v2 on v1

--- a/solution.py
+++ b/solution.py
@@ -56,15 +56,17 @@
     return lax.rsqrt(jnp.sum(block * block, axis=-1, keepdims=True) + norm_eps)
 
 
+def split_bf16(value):
+    high = value.astype(BF16)
+    return high, (value - high.astype(F32)).astype(BF16)
+
+
 def prepare_kernel(
     q_ref, k_ref, v_ref, gate_ref, beta_ref,
-    send_ref, tmat_ref, mix_ref, ratio_ref, uw_ref, probe_ref, local_ref, cols_ref,
+    pair_ref, tmat_ref, mix_ref, ratio_ref, uw_ref, probe_ref, local_ref, cols_ref,
 ):
     length = q_ref.shape[0]
-    group = gate_ref.shape[1]
-    dests = send_ref.shape[0]
-    share = dests // group
-    part = WIDTH // share
+    group = gate_ref.shape[0]
     q = q_ref[...].astype(F32)
     k = k_ref[...].astype(F32)
     qn = q * inverse_norm(q) * WIDTH ** (-0.5)
@@ -77,9 +79,9 @@
     betas = beta_ref[...].astype(F32) / beta_steps
     for head in range(group):
         span = slice(head * WIDTH, (head + 1) * WIDTH)
-        log_cum = mm(tri, jnp.broadcast_to(logs[:, head : head + 1], (length, length)))
-        beta_col = jnp.broadcast_to(betas[:, head : head + 1], (length, length))
-        ratio = jnp.exp(log_cum - log_cum.T) * beta_col.T
+        log_cum = mm(tri, jnp.broadcast_to(logs[head : head + 1, :], (length, length)), 1, 1)
+        beta_row = jnp.broadcast_to(betas[head : head + 1, :], (length, length))
+        ratio = jnp.exp(log_cum - log_cum.T) * beta_row
         ratio = jnp.where(rows >= cols, ratio, 0.0)
         lower = jnp.where(rows > cols, ratio * gram, 0.0)
         mix = ratio * query_key
@@ -89,14 +91,11 @@
         uw = mm(inverse, jnp.concatenate([value, decay * kn], axis=1))
         mixed = mm(mix, uw)
         last = log_cum[length - 1 :, :]
-        weight = beta_col * jnp.exp(last - log_cum)
+        weight = beta_row.T * jnp.exp(last - log_cum)
         weighted = weight * kn
         uv, wk = uw[:, :WIDTH], uw[:, WIDTH:]
-        transition = jnp.where(rows == cols, jnp.exp(last), 0.0) - mm(weighted, wk, 0, 0)
-        state_t = mm(uv, weighted, 0, 0)
-        for dest in range(share):
-            send_ref[head * share + dest, :WIDTH, :] = transition
-            send_ref[head * share + dest, WIDTH:, :] = state_t[dest * part : (dest + 1) * part, :]
+        pair_ref[head] = jnp.where(rows == cols, jnp.exp(last), 0.0) - mm(weighted, wk, 0, 0)
+        pair_ref[group + head] = mm(uv, weighted, 0, 0)
         tmat_ref[head] = inverse
         mix_ref[head] = mix
         ratio_ref[head] = ratio
@@ -107,47 +106,108 @@
         cols_ref[head, 1] = weight
 
 
-def cotangent_kernel(grad_ref, w_ref, probe_ref, cot_ref, send_ref):
+def compose_kernel(
+    odd_ref, own_ref, other_ref, probe_ref, local_ref,
+    trans_ref, state_ref, diag_ref, probe_out_ref, local_out_ref,
+):
+    group = probe_ref.shape[0]
+    is_odd = odd_ref[0] == 1
+    rows, cols = ids(WIDTH)
+    half = WIDTH // 2
+    for head in range(group):
+        span = slice(head * WIDTH, (head + 1) * WIDTH)
+        own, other = own_ref[head], other_ref[head]
+        own_state, other_state = own_ref[group + head], other_ref[group + head]
+        first = jnp.where(is_odd, other, own)
+        second = jnp.where(is_odd, own, other)
+        first_state = jnp.where(is_odd, other_state, own_state)
+        second_state = jnp.where(is_odd, own_state, other_state)
+        transition = mm(second, first)
+        state_t = mm(first_state, second, 1, 1) + second_state
+        rounded = transition.astype(BF16)
+        rest = jnp.where(rows == cols, transition - rounded.astype(F32), 0.0)
+        diag_ref[head] = jnp.broadcast_to(
+            jnp.sum(rest, axis=0, keepdims=True), (diag_ref.shape[1], WIDTH)
+        ).astype(BF16)
+        trans_ref[head] = jnp.where(is_odd, transition[half:], transition[:half]).astype(BF16)
+        high, low = split_bf16(state_t)
+        state_ref[head] = jnp.where(is_odd, low, high)
+        probe = probe_ref[head]
+        local = local_ref[:, span]
+        probe_out_ref[head] = jnp.where(is_odd, mm(probe, other), probe)
+        local_out_ref[:, span] = jnp.where(is_odd, local + mm(probe, other_state, 1, 1), local)
+
+
+def cotangent_kernel(
+    grad_ref, w_ref, probe_ref, trans_ref, state_ref, diag_ref, cot_ref, send_ref
+):
     blocks = grad_ref.shape[0]
     group = probe_ref.shape[0]
+    half = WIDTH // 2
     total = jnp.zeros(cot_ref.shape, F32)
     for block in range(0, blocks, 2):
         left = jnp.concatenate([grad_ref[block], grad_ref[block + 1]], axis=1)
         total += mm_bf16(left, w_ref[:, block * WIDTH : (block + 2) * WIDTH], 1, 1)
     cot_ref[...] = total
-    dests, part, _ = send_ref.shape
-    share = dests // group
+    chips = send_ref.shape[0]
+    part = WIDTH // chips
     for head in range(group):
         carried_t = mm(total[:, head * WIDTH : (head + 1) * WIDTH], probe_ref[head], 0, 0)
-        send_ref[head * share : (head + 1) * share] = carried_t.reshape(share, part, WIDTH)
-
-
-def forward_scan_kernel(got_ref, send_ref):
-    slabs, part = send_ref.shape[0], send_ref.shape[1]
-    state = jnp.zeros((part, WIDTH), F32)
-    for slab in range(slabs):
-        send_ref[slab] = state
-        if slab < slabs - 1:
-            state = mm(state, got_ref[slab, :WIDTH, :], 1, 1) + got_ref[slab, WIDTH:, :]
-
-
-def backward_scan_kernel(got_ref, cot_ref, send_ref):
-    slabs, part = send_ref.shape[0], send_ref.shape[1]
-    state = jnp.zeros((part, WIDTH), F32)
-    for slab in reversed(range(slabs)):
-        send_ref[slab] = state
-        if slab > 0:
-            state = mm(state, got_ref[slab, :WIDTH, :], 1, 0) + cot_ref[slab]
-
-
-def output_kernel(state_ref, probe_ref, local_ref, grad_ref, attn_ref, send_ref):
+        high = carried_t.astype(BF16).astype(F32)
+        low = carried_t - high
+        state = state_ref[head].astype(F32)
+        diag = diag_ref[head].astype(F32)
+        trans = trans_ref[head]
+        for chip in range(chips):
+            mine = slice(chip * part, (chip + 1) * part)
+            send_ref[chip, head, :half, :] = trans
+            send_ref[chip, head, half:, :] = jnp.concatenate(
+                [state[mine], high[mine], low[mine], diag], axis=0
+            ).astype(BF16)
+
+
+def scan_kernel(got_ref, send_ref):
+    chips = got_ref.shape[0]
+    half = WIDTH // 2
+    part = WIDTH // chips
+
+    def step(state, chip, dim):
+        high, low = split_bf16(state)
+        both = jnp.concatenate([high.astype(F32), low.astype(F32)], axis=0).astype(BF16)
+        trans = jnp.concatenate([got_ref[chip, 0, :half, :], got_ref[chip, 1, :half, :]], axis=0)
+        rest = got_ref[chip, 0, half:, :].astype(F32)
+        other = got_ref[chip, 1, half:, :].astype(F32)
+        product = mm_bf16(both, trans, 1, dim)
+        moved = product[:part] + product[part:] + state * rest[3 * part :]
+        if dim == 1:
+            return moved + rest[:part] + other[:part]
+        return moved + (
+            (rest[part : 2 * part] + other[part : 2 * part])
+            + (rest[2 * part : 3 * part] + other[2 * part : 3 * part])
+        )
+
+    ahead = jnp.zeros((part, WIDTH), F32)
+    back = jnp.zeros((part, WIDTH), F32)
+    for turn in range(chips):
+        late = chips - 1 - turn
+        for core in range(2):
+            send_ref[turn, core, :part, :] = ahead
+            send_ref[late, core, part:, :] = back
+        if turn < chips - 1:
+            ahead = step(ahead, turn, 1)
+            back = step(back, late, 0)
+
+
+def gather_rows(got_ref, head, which):
+    chips, _, rows, _ = got_ref.shape
+    part = rows // 2
+    return got_ref[:, head, which * part : (which + 1) * part, :].reshape(chips * part, WIDTH)
+
+
+def output_kernel(got_ref, probe_ref, local_ref, grad_ref, attn_ref, send_ref):
     group = probe_ref.shape[0]
     dests, part, _ = send_ref.shape
-    share = dests // group
-    outs = []
-    for head in range(group):
-        state_t = state_ref[head * share : (head + 1) * share].reshape(WIDTH, WIDTH)
-        outs.append(mm(probe_ref[head], state_t, 1, 1))
+    outs = [mm(probe_ref[head], gather_rows(got_ref, head, 0), 1, 1) for head in range(group)]
     attn = (jnp.concatenate(outs, axis=1) + local_ref[...]).astype(BF16)
     attn_ref[...] = attn
     for block in range(0, grad_ref.shape[0], 2):
@@ -158,13 +218,20 @@
         ).astype(BF16)
 
 
+def carried_kernel(cot_ref, probe_ref, carried_ref):
+    for head in range(probe_ref.shape[0]):
+        carried_ref[head] = mm(
+            cot_ref[:, head * WIDTH : (head + 1) * WIDTH], probe_ref[head], 0, 0
+        )
+
+
 def gradient_kernel(
-    q_ref, k_ref, state_ref, end_ref, cot_ref, tmat_ref, mix_ref, ratio_ref, uw_ref, cols_ref,
-    q_grad_ref, k_grad_ref, v_grad_ref,
+    odd_ref, q_ref, k_ref, got_ref, other_ref, carried_ref, cot_ref, tmat_ref, mix_ref,
+    ratio_ref, uw_ref, cols_ref, q_grad_ref, k_grad_ref, v_grad_ref,
 ):
     length = q_ref.shape[0]
     group = tmat_ref.shape[0]
-    share = state_ref.shape[0] // group
+    is_odd = odd_ref[0] == 1
     q = q_ref[...].astype(F32)
     k = k_ref[...].astype(F32)
     q_inv = inverse_norm(q)
@@ -176,8 +243,13 @@
     dk = jnp.zeros((length, WIDTH), F32)
     for head in range(group):
         span = slice(head * WIDTH, (head + 1) * WIDTH)
-        state_t = state_ref[head * share : (head + 1) * share].reshape(WIDTH, WIDTH)
-        end_t = end_ref[head * share : (head + 1) * share].reshape(WIDTH, WIDTH)
+        state_t = gather_rows(got_ref, head, 0)
+        end_t = gather_rows(got_ref, head, 1)
+        other = other_ref[head]
+        through_state = mm(state_t, other, 1, 1) + other_ref[group + head]
+        through_end = mm(end_t, other) + carried_ref[head]
+        state_t = jnp.where(is_odd, through_state, state_t)
+        end_t = jnp.where(is_odd, end_t, through_end)
         cot = cot_ref[:, span]
         ratio = ratio_ref[head]
         decay = cols_ref[head, 0]
@@ -208,9 +280,14 @@
     moved = sum(x.size * x.dtype.itemsize for x in operands) + sum(
         x.size * x.dtype.itemsize for x in outs
     )
+    scalars = [x.ndim == 1 for x in operands]
+    vmem = pl.BlockSpec(memory_space=pltpu.VMEM)
+    smem = pl.BlockSpec(memory_space=pltpu.SMEM)
     return pl.pallas_call(
         kernel,
         out_shape=outs,
+        in_specs=[smem if scalar else vmem for scalar in scalars],
+        out_specs=[vmem] * len(outs),
         name=kernel.__name__,
         cost_estimate=pl.CostEstimate(flops=flops, bytes_accessed=moved, transcendentals=0),
         compiler_params=pltpu.CompilerParams(vmem_limit_bytes=48 << 20),
@@ -230,51 +307,65 @@
     group = values.shape[1] // queries.shape[1]
     slabs = lax.axis_size("seq")
     heads = lax.axis_size("head")
-    share = slabs // group
-    part = WIDTH // share
+    chips = slabs // 2
+    part = WIDTH // chips
     square = (group, length, WIDTH)
+    flat = (length, group * WIDTH)
+    odd = (lax.axis_index("seq") % 2).astype(jnp.int32).reshape(1)
     full_grad = swap(jnp.broadcast_to(out_grad[None], (heads, length, WIDTH)), "head")
-    send, tmat, mix, ratio, uw, probe, local, columns = call(
+    pair, tmat, mix, ratio, uw, probe, local, columns = call(
         prepare_kernel,
         [
-            shape((slabs, WIDTH + part, WIDTH)),
+            shape((2 * group, WIDTH, WIDTH)),
             shape(square),
             shape(square),
             shape(square),
             shape((group, length, 2 * WIDTH)),
             shape(square),
-            shape((length, group * WIDTH)),
+            shape(flat),
             shape((group, 2, length, WIDTH)),
         ],
         1 << 30,
-        queries, keys, values, gate_code, beta_code,
-    )
-    got = swap(send, "seq")
-    cot, cot_send = call(
+        queries, keys, values, gate_code.T, beta_code.T,
+    )
+    other = lax.ppermute(pair, "seq", [(slab, slab ^ 1) for slab in range(slabs)])
+    trans, state, diag, chip_probe, chip_local = call(
+        compose_kernel,
+        [
+            shape((group, WIDTH // 2, WIDTH), BF16),
+            shape((group, WIDTH, WIDTH), BF16),
+            shape((group, part, WIDTH), BF16),
+            shape(square),
+            shape(flat),
+        ],
+        1 << 28,
+        odd, pair, other, probe, local,
+    )
+    cot, send = call(
         cotangent_kernel,
-        [shape((length, group * WIDTH)), shape((slabs, part, WIDTH))],
+        [shape(flat), shape((chips, group, WIDTH // 2 + 4 * part, WIDTH), BF16)],
         1 << 28,
-        full_grad, w_out, probe,
-    )
-    cot_got = swap(cot_send, "seq")
-    (start_send,) = call(forward_scan_kernel, [shape((slabs, part, WIDTH))], 1 << 29, got)
-    start = swap(start_send, "seq")
-    (end_send,) = call(
-        backward_scan_kernel, [shape((slabs, part, WIDTH))], 1 << 29, got, cot_got
-    )
-    end = swap(end_send, "seq")
+        full_grad, w_out, chip_probe, trans, state, diag,
+    )
+    got = swap(send.reshape((slabs,) + send.shape[2:]), "seq")
+    (carried,) = call(carried_kernel, [shape((group, WIDTH, WIDTH))], 1 << 26, cot, probe)
+    carried = lax.ppermute(carried, "seq", [(slab, slab ^ 1) for slab in range(slabs)])
+    (back,) = call(
+        scan_kernel, [shape((chips, 2, 2 * part, WIDTH))], 1 << 27, got.reshape(send.shape)
+    )
+    states = swap(back.reshape(slabs, 2 * part, WIDTH), "seq").reshape(back.shape)
     attn_out, grad_send = call(
         output_kernel,
-        [shape((length, group * WIDTH), BF16), shape((slabs, part, heads * WIDTH), BF16)],
+        [shape(flat, BF16), shape((slabs, part, heads * WIDTH), BF16)],
         1 << 28,
-        start, probe, local, full_grad,
+        states, chip_probe, chip_local, full_grad,
     )
     grad_got = swap(grad_send, "seq")
     q_grad, k_grad, v_grad = call(
         gradient_kernel,
-        [shape((length, WIDTH)), shape((length, WIDTH)), shape((length, group * WIDTH))],
+        [shape((length, WIDTH)), shape((length, WIDTH)), shape(flat)],
         1 << 29,
-        queries, keys, start, end, cot, tmat, mix, ratio, uw, columns,
+        odd, queries, keys, states, other, carried, cot, tmat, mix, ratio, uw, columns,
     )
     scaling = (length * slabs) ** (-0.5)
     weight_grad = jnp.sum(grad_got.astype(F32), axis=0) * scaling

time: 153 us -> 111 us (0.73)
  blocking collectives: 0 us -> 40.9 us
  waiting for transfers between devices: 55.3 us -> 20.6 us
  starting transfers between devices: 54.4 us -> 25.5 us
  Pallas kernels: 30.8 us -> 17.6 us
  local copies, waits for them, and re-layouts: 9.61 us -> 3.04 us
    all_to_all x0 -> x2, blocking collectives: none -> 40.9 us  [swap(): return lax.all_to_all(value, axis, 0, 0, tiled=True)]
    all_to_all x6 -> x2, waiting for transfers between devices: 55.3 us -> 18.5 us  [swap(): return lax.all_to_all(value, axis, 0, 0, tiled=True)]
    all_to_all x6 -> x2, starting transfers between devices: 54.4 us -> 20.4 us  [swap(): return lax.all_to_all(value, axis, 0, 0, tiled=True)]
    pallas_call x6 -> x7, Pallas kernels: 30.8 us -> 17.6 us  [call(): pl.pallas_call(kernel, out_shape=outs, in_specs=[smem if scalar else vmem...]
    unnamed x32 -> x20, local copies, waits for them, and re-layouts: 7.95 us -> 1.34 us
    ppermute x0 -> x2, starting transfers between devices: none -> 5.18 us  [the longest x1 2.85 us: per_device(): lax.ppermute(pair, 'seq', [(slab, slab ^ 1) for slab in range(slabs)])]
    ppermute x0 -> x2, waiting for transfers between devices: none -> 2.09 us  [the longest x1 1.13 us: per_device(): lax.ppermute(pair, 'seq', [(slab, slab ^ 1) for slab in range(slabs)])]
  transfers between devices with their start and end apart: 6 -> 4, of which waited for: 5 -> 4; matrix products, arithmetic and copies ran while one was open for 1% -> 0% of each run, Pallas kernels for 20% -> 12%
where the time goes in v2:
time: 111 us; the launch traced here: 110 us
  blocking collectives  40.9 us (37%)
  starting transfers between devices  25.5 us (23%)
  waiting for transfers between devices  20.6 us (19%)
  Pallas kernels  17.6 us (16%)
  local copies, waits for them, and re-layouts  3.04 us (3%)
  other arithmetic  2.02 us (2%)
    all_to_all x2, blocking collectives, swap(): return lax.all_to_all(value, axis, 0, 0, tiled=True)  40.9 us
    all_to_all x2, starting transfers between devices, swap(): return lax.all_to_all(value, axis, 0, 0, tiled=True)  20.4 us
    all_to_all x2, waiting for transfers between devices, swap(): return lax.all_to_all(value, axis, 0, 0, tiled=True)  18.5 us
    pallas_call x7, Pallas kernels, call(): pl.pallas_call(kernel, out_shape=outs, in_specs=[smem if scalar else vmem...  17.6 us
    ppermute x1, starting transfers between devices, per_device(): lax.ppermute(pair, 'seq', [(slab, slab ^ 1) for slab in range(slabs)])  2.85 us
    ppermute x1, starting transfers between devices, per_device(): lax.ppermute(carried, 'seq', [(slab, slab ^ 1) for slab in range(slabs)])  2.33 us
  transfers between devices with their start and end apart: 4, of which 4 were waited for; matrix products, arithmetic and copies ran while one was open for 0% of the time, Pallas kernels for 12%

profile of v2, /device:TPU:1, one launch (start us, length us, event | category | flops | bytes accessed | tf_op | source)
XLA Modules:
  0.0 110.5 jit_solution(6877200964513326170)
XLA Ops:
  0.6 0.0 copy-start.3
  0.6 0.0 copy-start.2
  0.7 0.0 copy-start.5
  0.7 0.0 copy-start.4
  0.7 0.0 copy-start.1
  0.7 1.7 %broadcast_in_dim.2 = bf16[16,128,128]{2,1,0:T(8,128)(2,1)} broadcast(bf16[128,128]{1,0:T(8,128)(2,1)} %param.12), dimensions={1,2} | broadcast | bytes 557056 | tf_op jit(solution)/shard_map/broadcast_in_dim | solution.py:315
  2.4 15.7 %all-to-all-start = ((bf16[16,128,128]{2,1,0:T(8,128)(2,1)}), bf16[16,128,128]{2,1,0:T(8,128)(2,1)S(1)}, u32[]{:S(2)}, u32[]{:S(2)}) async-start(bf16[16,128,128]{2,1,0:T(8,128)(2,1)} %broadcast_in_dim.2), calls=%async_computation | async-start | bytes 1048576 | tf_op jit(solution)/shard_map/all_to_all | solution.py:302
  18.1 0.0 copy-done.3
  18.2 0.0 copy-done.2
  18.2 0.0 copy-done.5
  18.2 0.0 copy-done.4
  18.2 0.0 copy-done.1
  18.2 0.0 copy-start
  18.2 7.7 %prepare_kernel.1 = (f32[4,128,128]{2,1,0:T(8,128)S(1)}, f32[2,128,128]{2,1,0:T(8,128)S(1)}, f32[2,128,128]{2,1,0:T(8,128)S(1)}, f32[2,128,128]{2,1,0:T(8,128)S(...) custom-call(bf16[128,128]{1,0:T(8,128)(2,1)S(1)} %copy-done.2, ...), custom_call_target="tpu_custom_call" | custom-call | flops 1073741824 | bytes 1574912 | tf_op jit(solution)/shard_map/prepare_kernel/pallas_call | solution.py:286
  25.9 0.0 copy-start.6
  25.9 0.6 copy-done.6
  26.6 0.0 copy-start.8
  26.6 0.7 copy-done.8
  27.2 2.9 %collective-permute-start = (f32[4,128,128]{2,1,0:T(8,128)S(1)}, f32[4,128,128]{2,1,0:T(8,128)S(1)}, u32[]{:S(2)}, u32[]{:S(2)}) collective-permute-start(f32[4,128,128]{2,1,0:T(8,128)S(1)} %get-tuple-element.25.own_ref), channel_id=1, source_target_pairs={{0,16},{16,0},{32,48},{48,32},{64,80},{80,64},{96,112},{112,96},{1... | collective-permute-start | bytes 786440 | tf_op jit(solution)/shard_map/ppermute | solution.py:331
  30.1 1.1 %collective-permute-done.other_ref = f32[4,128,128]{2,1,0:T(8,128)S(1)} collective-permute-done((f32[4,128,128]{2,1,0:T(8,128)S(1)}, f32[4,128,128]{2,1,0:T(8,128)S(1)}, u32[]{:S(2)}, u32[]{:S(2)}) %collective-permute-start) | collective-permute-done | bytes 262176 | tf_op jit(solution)/shard_map/ppermute | solution.py:331
  31.2 0.9 compose_kernel.1
  32.1 8.9 %all-to-all-done.grad_ref = bf16[16,128,128]{2,1,0:T(8,128)(2,1)S(1)} async-done(((bf16[16,128,128]{2,1,0:T(8,128)(2,1)}), bf16[16,128,128]{2,1,0:T(8,128)(2,1)S(1)}, u32[]{:S(2)}, u32[]{:S(2)}) %all-to-all-start) | async-done | bytes 524320 | tf_op jit(solution)/shard_map/all_to_all | solution.py:302
  41.0 0.0 copy-done
  41.0 0.9 cotangent_kernel.1
  41.9 28.3 %all_to_all.20 = bf16[32,96,128]{2,1,0:T(8,128)(2,1)S(1)} all-to-all(bf16[32,96,128]{2,1,0:T(8,128)(2,1)S(1)} %bitcast.11), channel_id=1, replica_groups=mesh['seq'=32,'head'=16] {'seq'}, dimensions={0} | all-to-all | bytes 1572864 | tf_op jit(solution)/shard_map/all_to_all | solution.py:302
  70.3 1.9 %scan_kernel.1 = f32[16,2,16,128]{3,2,1,0:T(8,128)S(1)} custom-call(bf16[16,2,96,128]{3,2,1,0:T(8,128)(2,1)S(1)} %bitcast.7), custom_call_target="tpu_custom_call" | custom-call | flops 134217728 | bytes 1048576 | tf_op jit(solution)/shard_map/scan_kernel/pallas_call | solution.py:286
  72.1 12.6 %all_to_all.21 = f32[32,16,128]{2,1,0:T(8,128)S(1)} all-to-all(f32[32,16,128]{2,1,0:T(8,128)S(1)} %bitcast.10), channel_id=1, replica_groups=mesh['seq'=32,'head'=16] {'seq'}, dimensions={0} | all-to-all | bytes 524288 | tf_op jit(solution)/shard_map/all_to_all | solution.py:302
  84.7 1.8 %output_kernel.1 = (bf16[128,256]{1,0:T(8,128)(2,1)}, bf16[32,8,2048]{2,1,0:T(8,128)(2,1)}) custom-call(f32[16,2,16,128]{3,2,1,0:T(8,128)S(1)} %bitcast.8, f32[2,128,128]{2,1,0:T(8,128)S(1)} %get-tuple-element.28.probe_ref, f32[128,256]{1,0:T(8,128)S(1)} %get-tuple-element.33.local_ref, bf16[16,128,128]{2,1,0:T(8,128)(2,1)S(1)} %all-to-all-done.grad_ref), custom_call_target="tpu_custom_call" | custom-call | flops 268435456 | bytes 2162688 | tf_op jit(solution)/shard_map/output_kernel/pallas_call | solution.py:286
  86.5 0.0 copy-start.7
  86.5 0.0 copy-start.9
  86.5 4.6 %all-to-all-start.3 = ((bf16[32,8,2048]{2,1,0:T(8,128)(2,1)}), bf16[32,8,2048]{2,1,0:T(8,128)(2,1)}, u32[]{:S(2)}, u32[]{:S(2)}) async-start(bf16[32,8,2048]{2,1,0:T(8,128)(2,1)} %get-tuple-element.44), calls=%async_computation.3 | async-start | bytes 2097152 | tf_op jit(solution)/shard_map/all_to_all | solution.py:302
  91.1 0.3 carried_kernel.1
  91.5 2.3 %collective-permute-start.1 = (f32[2,128,128]{2,1,0:T(8,128)S(1)}, f32[2,128,128]{2,1,0:T(8,128)S(1)}, u32[]{:S(2)}, u32[]{:S(2)}) collective-permute-start(f32[2,128,128]{2,1,0:T(8,128)S(1)} %carried_kernel.1), channel_id=1, source_target_pairs={{0,16},{16,0},{32,48},{48,32},{64,80},{80,64},{96,112},{112,96},{1... | collective-permute-start | bytes 393224 | tf_op jit(solution)/shard_map/ppermute | solution.py:352
  93.8 1.0 collective-permute-done.1.carried_ref
  94.8 0.0 copy-done.7
  94.8 0.0 copy-done.9
  94.8 4.1 %gradient_kernel.1 = (f32[128,128]{1,0:T(8,128)}, f32[128,128]{1,0:T(8,128)}, f32[128,256]{1,0:T(8,128)}) custom-call(s32[1]{0:T(128)} %bitcast.odd_ref, bf16[128,128]{1,0:T(8,128)(2,1)S(1)} %copy-done.2, bf16[128,128]{1,0:T(8,128)(2,1)S(1)} %copy-done.3, f32[16,2,16,128]{3,2,1,0:T(8,128)S(1)} %bitcast.9, f32[4,128,128]{2,1,0:T(8,128)S(1)} %collective-permute-done.other_ref, ...), custom_call_target="tpu_custom_call" | custom-call | flops 536870912 | bytes 2031620 | tf_op jit(solution)/shard_map/gradient_kernel/pallas_call | solution.py:286
  98.9 9.6 %all-to-all-done.3 = bf16[32,8,2048]{2,1,0:T(8,128)(2,1)} async-done(((bf16[32,8,2048]{2,1,0:T(8,128)(2,1)}), bf16[32,8,2048]{2,1,0:T(8,128)(2,1)}, u32[]{:S(2)}, u32[]{:S(2)}) %all-to-all-start.3) | async-done | bytes 1048608 | tf_op jit(solution)/shard_map/all_to_all | solution.py:302
  108.5 1.4 %convert_reduce_fusion = f32[8,2048]{1,0:T(8,128)S(1)} fusion(bf16[32,8,2048]{2,1,0:T(8,128)(2,1)} %all-to-all-done.3), kind=kLoop, calls=%fused_computation | loop fusion | flops 1032192 | bytes 1114112 | tf_op jit(solution)/shard_map/reduce_sum | solution.py:371
  109.9 0.6 broadcast_multiply_fusion
Async XLA Ops:
  0.6 17.5 %copy-start.3 = (bf16[128,128]{1,0:T(8,128)(2,1)S(1)}, bf16[128,128]{1,0:T(8,128)(2,1)}, u32[]{:S(2)}) copy-start(bf16[128,128]{1,0:T(8,128)(2,1)} %k_ref.3) | copy-start | bytes 98308
  0.6 17.5 %copy-start.2 = (bf16[128,128]{1,0:T(8,128)(2,1)S(1)}, bf16[128,128]{1,0:T(8,128)(2,1)}, u32[]{:S(2)}) copy-start(bf16[128,128]{1,0:T(8,128)(2,1)} %q_ref.3) | copy-start | bytes 98308
  0.7 17.5 %copy-start.5 = (s32[128,2]{0,1:T(2,128)S(1)}, s32[128,2]{0,1:T(2,128)}, u32[]{:S(2)}) copy-start(s32[128,2]{0,1:T(2,128)} %param.11) | copy-start | bytes 3076
  0.7 17.5 %copy-start.4 = (s32[128,2]{0,1:T(2,128)S(1)}, s32[128,2]{0,1:T(2,128)}, u32[]{:S(2)}) copy-start(s32[128,2]{0,1:T(2,128)} %param.10) | copy-start | bytes 3076
  0.7 17.5 %copy-start.1 = (bf16[128,256]{1,0:T(8,128)(2,1)S(1)}, bf16[128,256]{1,0:T(8,128)(2,1)}, u32[]{:S(2)}) copy-start(bf16[128,256]{1,0:T(8,128)(2,1)} %v_ref.1) | copy-start | bytes 196612
  2.4 38.6 %all-to-all-start = ((bf16[16,128,128]{2,1,0:T(8,128)(2,1)}), bf16[16,128,128]{2,1,0:T(8,128)(2,1)S(1)}, u32[]{:S(2)}, u32[]{:S(2)}) async-start(bf16[16,128,128]{2,1,0:T(8,128)(2,1)} %broadcast_in_dim.2), calls=%async_computation | async-start | bytes 1048576 | tf_op jit(solution)/shard_map/all_to_all | solution.py:302
  18.2 22.8 %copy-start = (bf16[256,2048]{1,0:T(8,128)(2,1)S(1)}, bf16[256,2048]{1,0:T(8,128)(2,1)}, u32[]{:S(2)}) copy-start(bf16[256,2048]{1,0:T(8,128)(2,1)} %w_ref.1) | copy-start | bytes 3145732
  25.9 0.7 copy-start.6
  26.6 0.7 copy-start.8
  27.2 4.0 %collective-permute-start = (f32[4,128,128]{2,1,0:T(8,128)S(1)}, f32[4,128,128]{2,1,0:T(8,128)S(1)}, u32[]{:S(2)}, u32[]{:S(2)}) collective-permute-start(f32[4,128,128]{2,1,0:T(8,128)S(1)} %get-tuple-element.25.own_ref), channel_id=1, source_target_pairs={{0,16},{16,0},{32,48},{48,32},{64,80},{80,64},{96,112},{112,96},{1... | collective-permute-start | bytes 786440 | tf_op jit(solution)/shard_map/ppermute | solution.py:331
  86.5 8.3 %copy-start.7 = (f32[2,128,128]{2,1,0:T(8,128)S(1)}, f32[2,128,128]{2,1,0:T(8,128)}, u32[]{:S(2)}) copy-start(f32[2,128,128]{2,1,0:T(8,128)} %copy-done.6) | copy-start | bytes 393220
  86.5 8.3 %copy-start.9 = (f32[2,128,128]{2,1,0:T(8,128)S(1)}, f32[2,128,128]{2,1,0:T(8,128)}, u32[]{:S(2)}) copy-start(f32[2,128,128]{2,1,0:T(8,128)} %copy-done.8) | copy-start | bytes 393220
  86.5 22.0 %all-to-all-start.3 = ((bf16[32,8,2048]{2,1,0:T(8,128)(2,1)}), bf16[32,8,2048]{2,1,0:T(8,128)(2,1)}, u32[]{:S(2)}, u32[]{:S(2)}) async-start(bf16[32,8,2048]{2,1,0:T(8,128)(2,1)} %get-tuple-element.44), calls=%async_computation.3 | async-start | bytes 2097152 | tf_op jit(solution)/shard_map/all_to_all | solution.py:302
  91.5 3.3 %collective-permute-start.1 = (f32[2,128,128]{2,1,0:T(8,128)S(1)}, f32[2,128,128]{2,1,0:T(8,128)S(1)}, u32[]{:S(2)}, u32[]{:S(2)}) collective-permute-start(f32[2,128,128]{2,1,0:T(8,128)S(1)} %carried_kernel.1), channel_id=1, source_target_pairs={{0,16},{16,0},{32,48},{48,32},{64,80},{80,64},{96,112},{112,96},{1... | collective-permute-start | bytes 393224 | tf_op jit(solution)/shard_map/ppermute | solution.py:352

commit v3 on v2

--- a/solution.py
+++ b/solution.py
@@ -108,7 +108,7 @@
 
 def compose_kernel(
     odd_ref, own_ref, other_ref, probe_ref, local_ref,
-    trans_ref, state_ref, diag_ref, probe_out_ref, local_out_ref,
+    trans_ref, state_ref, diag_ref, maps_ref,
 ):
     group = probe_ref.shape[0]
     is_odd = odd_ref[0] == 1
@@ -134,15 +134,15 @@
         state_ref[head] = jnp.where(is_odd, low, high)
         probe = probe_ref[head]
         local = local_ref[:, span]
-        probe_out_ref[head] = jnp.where(is_odd, mm(probe, other), probe)
-        local_out_ref[:, span] = jnp.where(is_odd, local + mm(probe, other_state, 1, 1), local)
+        maps_ref[head] = jnp.where(is_odd, mm(probe, other), probe)
+        maps_ref[group + head] = jnp.where(is_odd, local + mm(probe, other_state, 1, 1), local)
 
 
 def cotangent_kernel(
-    grad_ref, w_ref, probe_ref, trans_ref, state_ref, diag_ref, cot_ref, send_ref
+    grad_ref, w_ref, maps_ref, trans_ref, state_ref, diag_ref, cot_ref, send_ref
 ):
     blocks = grad_ref.shape[0]
-    group = probe_ref.shape[0]
+    group = trans_ref.shape[0]
     half = WIDTH // 2
     total = jnp.zeros(cot_ref.shape, F32)
     for block in range(0, blocks, 2):
@@ -152,7 +152,7 @@
     chips = send_ref.shape[0]
     part = WIDTH // chips
     for head in range(group):
-        carried_t = mm(total[:, head * WIDTH : (head + 1) * WIDTH], probe_ref[head], 0, 0)
+        carried_t = mm(total[:, head * WIDTH : (head + 1) * WIDTH], maps_ref[head], 0, 0)
         high = carried_t.astype(BF16).astype(F32)
         low = carried_t - high
         state = state_ref[head].astype(F32)
@@ -204,18 +204,48 @@
     return got_ref[:, head, which * part : (which + 1) * part, :].reshape(chips * part, WIDTH)
 
 
-def output_kernel(got_ref, probe_ref, local_ref, grad_ref, attn_ref, send_ref):
-    group = probe_ref.shape[0]
+def output_kernel(
+    odd_ref, got_ref, maps_ref, other_maps_ref, grad_ref, other_grad_ref, attn_ref, send_ref
+):
+    group = maps_ref.shape[0] // 2
     dests, part, _ = send_ref.shape
-    outs = [mm(probe_ref[head], gather_rows(got_ref, head, 0), 1, 1) for head in range(group)]
-    attn = (jnp.concatenate(outs, axis=1) + local_ref[...]).astype(BF16)
-    attn_ref[...] = attn
-    for block in range(0, grad_ref.shape[0], 2):
-        right = jnp.concatenate([grad_ref[block], grad_ref[block + 1]], axis=1)
-        term = mm_bf16(attn, right, 0, 0)
+    blocks = other_grad_ref.shape[0]
+    first = odd_ref[0] * blocks
+    own, other = [], []
+    for head in range(group):
+        state_t = gather_rows(got_ref, head, 0)
+        own.append(mm(maps_ref[head], state_t, 1, 1) + maps_ref[group + head])
+        other.append(mm(other_maps_ref[head], state_t, 1, 1) + other_maps_ref[group + head])
+    own = jnp.concatenate(own, axis=1).astype(BF16)
+    other = jnp.concatenate(other, axis=1).astype(BF16)
+    attn_ref[...] = own
+    left = jnp.concatenate([own, other], axis=0)
+    for block in range(0, blocks, 2):
+        right = jnp.concatenate(
+            [
+                jnp.concatenate([grad_ref[first + block], grad_ref[first + block + 1]], axis=1),
+                jnp.concatenate([other_grad_ref[block], other_grad_ref[block + 1]], axis=1),
+            ],
+            axis=0,
+        )
+        term = mm_bf16(left, right, 0, 0)
         send_ref[:, :, block * WIDTH : (block + 2) * WIDTH] = term.reshape(
             dests, part, 2 * WIDTH
         ).astype(BF16)
+
+
+def sum_kernel(got_ref, out_ref, *, scaling):
+    chips, cores, _, width = got_ref.shape
+    for core in range(cores):
+        total = got_ref[0, core].astype(F32)
+        for chip in range(1, chips):
+            total = total + got_ref[chip, core].astype(F32)
+        out_ref[:, core * width : (core + 1) * width] = total * scaling
+
+
+def half_kernel(odd_ref, grad_ref, half_ref):
+    blocks = half_ref.shape[0]
+    half_ref[...] = grad_ref[pl.ds((1 - odd_ref[0]) * blocks, blocks)]
 
 
 def carried_kernel(cot_ref, probe_ref, carried_ref):
@@ -288,7 +318,7 @@
         out_shape=outs,
         in_specs=[smem if scalar else vmem for scalar in scalars],
         out_specs=[vmem] * len(outs),
-        name=kernel.__name__,
+        name=getattr(kernel, "func", kernel).__name__,
         cost_estimate=pl.CostEstimate(flops=flops, bytes_accessed=moved, transcendentals=0),
         compiler_params=pltpu.CompilerParams(vmem_limit_bytes=48 << 20),
     )(*operands)
@@ -300,6 +330,11 @@
 
 def swap(value, axis):
     return lax.all_to_all(value, axis, 0, 0, tiled=True)
+
+
+def across(value):
+    slabs = lax.axis_size("seq")
+    return lax.ppermute(value, "seq", [(slab, slab ^ 1) for slab in range(slabs)])
 
 
 def per_device(queries, keys, values, gate_code, beta_code, out_grad, w_out):
@@ -328,37 +363,41 @@
         1 << 30,
         queries, keys, values, gate_code.T, beta_code.T,
     )
-    other = lax.ppermute(pair, "seq", [(slab, slab ^ 1) for slab in range(slabs)])
-    trans, state, diag, chip_probe, chip_local = call(
+    other = across(pair)
+    trans, state, diag, maps = call(
         compose_kernel,
         [
             shape((group, WIDTH // 2, WIDTH), BF16),
             shape((group, WIDTH, WIDTH), BF16),
             shape((group, part, WIDTH), BF16),
-            shape(square),
-            shape(flat),
+            shape((2 * group, length, WIDTH)),
         ],
         1 << 28,
         odd, pair, other, probe, local,
     )
+    other_maps = across(maps)
     cot, send = call(
         cotangent_kernel,
         [shape(flat), shape((chips, group, WIDTH // 2 + 4 * part, WIDTH), BF16)],
         1 << 28,
-        full_grad, w_out, chip_probe, trans, state, diag,
-    )
+        full_grad, w_out, maps, trans, state, diag,
+    )
+    (half,) = call(
+        half_kernel, [shape((heads // 2, length, WIDTH), BF16)], 1 << 20, odd, full_grad
+    )
+    other_half = across(half)
     got = swap(send.reshape((slabs,) + send.shape[2:]), "seq")
     (carried,) = call(carried_kernel, [shape((group, WIDTH, WIDTH))], 1 << 26, cot, probe)
-    carried = lax.ppermute(carried, "seq", [(slab, slab ^ 1) for slab in range(slabs)])
+    carried = across(carried)
     (back,) = call(
         scan_kernel, [shape((chips, 2, 2 * part, WIDTH))], 1 << 27, got.reshape(send.shape)
     )
     states = swap(back.reshape(slabs, 2 * part, WIDTH), "seq").reshape(back.shape)
     attn_out, grad_send = call(
         output_kernel,
-        [shape(flat, BF16), shape((slabs, part, heads * WIDTH), BF16)],
+        [shape(flat, BF16), shape((slabs, part, heads // 2 * WIDTH), BF16)],
         1 << 28,
-        states, chip_probe, chip_local, full_grad,
+        odd, states, maps, other_maps, full_grad, other_half,
     )
     grad_got = swap(grad_send, "seq")
     q_grad, k_grad, v_grad = call(
@@ -368,7 +407,12 @@
         odd, queries, keys, states, other, carried, cot, tmat, mix, ratio, uw, columns,
     )
     scaling = (length * slabs) ** (-0.5)
-    weight_grad = jnp.sum(grad_got.astype(F32), axis=0) * scaling
+    (weight_grad,) = call(
+        functools.partial(sum_kernel, scaling=scaling),
+        [shape((part, heads * WIDTH))],
+        1 << 20,
+        grad_got.reshape((chips, 2) + grad_got.shape[1:]),
+    )
     return (attn_out, q_grad, k_grad, v_grad, weight_grad)
 
 

time: 111 us -> 106 us (0.955)
  blocking collectives: 40.9 us -> 0 us
  starting transfers between devices: 25.5 us -> 47.5 us
  waiting for transfers between devices: 20.6 us -> 32.5 us
  Pallas kernels: 17.6 us -> 19.9 us
  other arithmetic: 2.02 us -> 0 us
  local copies, waits for them, and re-layouts: 3.04 us -> 4.29 us
    all_to_all x2 -> x0, blocking collectives: 40.9 us -> none  [swap(): return lax.all_to_all(value, axis, 0, 0, tiled=True)]
    all_to_all x2 -> x4, starting transfers between devices: 20.4 us -> 38.1 us  [swap(): return lax.all_to_all(value, axis, 0, 0, tiled=True)]
    all_to_all x2 -> x4, waiting for transfers between devices: 18.5 us -> 30.4 us  [swap(): return lax.all_to_all(value, axis, 0, 0, tiled=True)]
    ppermute x2 -> x4, starting transfers between devices: 5.18 us -> 9.44 us  [across(): lax.ppermute(value, 'seq', [(slab, slab ^ 1) for slab in range(slabs)])]
    pallas_call x7 -> x9, Pallas kernels: 17.6 us -> 19.9 us  [call(): pl.pallas_call(kernel, out_shape=outs, in_specs=[smem if scalar else vmem...]
    reduce_sum x1 -> x0, other arithmetic: 1.38 us -> none  [per_device(): weight_grad = jnp.sum(grad_got.astype(F32), axis=0) * scaling]
    unnamed x20 -> x24, local copies, waits for them, and re-layouts: 1.34 us -> 2.61 us
  transfers between devices with their start and end apart: 4 -> 8, of which waited for: 4 -> 6; matrix products, arithmetic and copies ran while one was open for 0% -> 0% of each run, Pallas kernels for 12% -> 15%
where the time goes in v3:
time: 106 us; the launch traced here: 105 us
  starting transfers between devices  47.5 us (45%)
  waiting for transfers between devices  32.5 us (31%)
  Pallas kernels  19.9 us (19%)
  local copies, waits for them, and re-layouts  4.29 us (4%)
    all_to_all x4, starting transfers between devices, swap(): return lax.all_to_all(value, axis, 0, 0, tiled=True)  38.1 us
    all_to_all x4, waiting for transfers between devices, swap(): return lax.all_to_all(value, axis, 0, 0, tiled=True)  30.4 us
    pallas_call x9, Pallas kernels, call(): pl.pallas_call(kernel, out_shape=outs, in_specs=[smem if scalar else vmem...  19.9 us
    ppermute x4, starting transfers between devices, across(): lax.ppermute(value, 'seq', [(slab, slab ^ 1) for slab in range(slabs)])  9.44 us
    unnamed x24, local copies, waits for them, and re-layouts  2.61 us
  transfers between devices with their start and end apart: 8, of which 6 were waited for; matrix products, arithmetic and copies ran while one was open for 0% of the time, Pallas kernels for 15%

profile of v3, /device:TPU:1, one launch (start us, length us, event | category | flops | bytes accessed | tf_op | source)
XLA Modules:
  0.0 105.0 jit_solution(5250258552600281920)
XLA Ops:
  0.6 1.7 %broadcast_in_dim.2 = bf16[16,128,128]{2,1,0:T(8,128)(2,1)} broadcast(bf16[128,128]{1,0:T(8,128)(2,1)} %param.12), dimensions={1,2} | broadcast | bytes 557056 | tf_op jit(solution)/shard_map/broadcast_in_dim | solution.py:350
  2.3 0.0 copy-start.1
  2.3 0.0 copy-start.2
  2.3 0.0 copy-start.3
  2.3 0.0 copy-start.5
  2.3 15.9 %all-to-all-start = ((bf16[16,128,128]{2,1,0:T(8,128)(2,1)}), bf16[16,128,128]{2,1,0:T(8,128)(2,1)S(1)}, u32[]{:S(2)}, u32[]{:S(2)}) async-start(bf16[16,128,128]{2,1,0:T(8,128)(2,1)} %broadcast_in_dim.2), calls=%async_computation | async-start | bytes 1048576 | tf_op jit(solution)/shard_map/all_to_all | solution.py:332
  18.2 0.0 copy-start.4
  18.2 0.0 copy-done.1
  18.2 0.0 copy-done.2
  18.2 0.0 copy-done.3
  18.3 0.0 copy-done.5
  18.3 0.6 copy-done.4
  18.9 0.0 copy-start
  18.9 7.7 %prepare_kernel.1 = (f32[4,128,128]{2,1,0:T(8,128)S(1)}, f32[2,128,128]{2,1,0:T(8,128)S(1)}, f32[2,128,128]{2,1,0:T(8,128)S(1)}, f32[2,128,128]{2,1,0:T(8,128)S(...) custom-call(bf16[128,128]{1,0:T(8,128)(2,1)S(1)} %copy-done.2, ...), custom_call_target="tpu_custom_call" | custom-call | flops 1073741824 | bytes 1574912 | tf_op jit(solution)/shard_map/prepare_kernel/pallas_call | solution.py:316
  26.6 0.0 copy-start.6
  26.6 0.6 copy-done.6
  27.3 0.0 copy-start.8
  27.3 0.6 copy-done.8
  27.9 0.7 copy-done.10
  28.6 2.8 %collective-permute-start = (f32[4,128,128]{2,1,0:T(8,128)S(1)}, f32[4,128,128]{2,1,0:T(8,128)S(1)}, u32[]{:S(2)}, u32[]{:S(2)}) collective-permute-start(f32[4,128,128]{2,1,0:T(8,128)S(1)} %get-tuple-element.24.own_ref), channel_id=1, source_target_pairs={{0,16},{16,0},{32,48},{48,32},{64,80},{80,64},{96,112},{112,96},{1... | collective-permute-start | bytes 786440 | tf_op jit(solution)/shard_map/ppermute | solution.py:337
  31.4 1.1 %collective-permute-done.other_ref = f32[4,128,128]{2,1,0:T(8,128)S(1)} collective-permute-done((f32[4,128,128]{2,1,0:T(8,128)S(1)}, f32[4,128,128]{2,1,0:T(8,128)S(1)}, u32[]{:S(2)}, u32[]{:S(2)}) %collective-permute-start) | collective-permute-done | bytes 262176 | tf_op jit(solution)/shard_map/ppermute | solution.py:337
  32.6 0.9 compose_kernel.1
  33.4 7.6 %all-to-all-done.grad_ref = bf16[16,128,128]{2,1,0:T(8,128)(2,1)S(1)} async-done(((bf16[16,128,128]{2,1,0:T(8,128)(2,1)}), bf16[16,128,128]{2,1,0:T(8,128)(2,1)S(1)}, u32[]{:S(2)}, u32[]{:S(2)}) %all-to-all-start) | async-done | bytes 524320 | tf_op jit(solution)/shard_map/all_to_all | solution.py:332
  41.0 0.0 copy-done
  41.0 1.8 %cotangent_kernel.1 = (f32[128,256]{1,0:T(8,128)S(1)}, bf16[16,2,96,128]{3,2,1,0:T(8,128)(2,1)}) custom-call(bf16[16,128,128]{2,1,0:T(8,128)(2,1)S(1)} %all-to-all-done.grad_ref, bf16[256,2048]{1,0:T(8,128)(2,1)S(1)} %copy-done, f32[4,128,128]{2,1,0:T(8,128)S(1)} %get-tuple-element.27.maps_ref, bf16[2,64,128]{2,1,0:T(8,128)(2,1)S(1)} %get-tuple-element.28.trans_ref, ...), custom_call_target="tpu_custom_call" | custom-call | flops 268435456 | bytes 2854912 | tf_op jit(solution)/shard_map/cotangent_kernel/pallas_call | solution.py:316
  42.9 14.3 %all-to-all-start.1 = ((bf16[32,96,128]{2,1,0:T(8,128)(2,1)}), bf16[32,96,128]{2,1,0:T(8,128)(2,1)S(1)}, u32[]{:S(2)}, u32[]{:S(2)}) async-start(bf16[32,96,128]{2,1,0:T(8,128)(2,1)} %bitcast.3), calls=%async_computation.1 | async-start | bytes 1572864 | tf_op jit(solution)/shard_map/all_to_all | solution.py:332
  57.2 2.1 %collective-permute-start.1 = (f32[4,128,128]{2,1,0:T(8,128)S(1)}, f32[4,128,128]{2,1,0:T(8,128)S(1)}, u32[]{:S(2)}, u32[]{:S(2)}) collective-permute-start(f32[4,128,128]{2,1,0:T(8,128)S(1)} %get-tuple-element.27.maps_ref), channel_id=1, source_target_pairs={{0,16},{16,0},{32,48},{48,32},{64,80},{80,64},{96,112},{112,96},{1... | collective-permute-start | bytes 786440 | tf_op jit(solution)/shard_map/ppermute | solution.py:337
  59.4 2.2 %collective-permute-start.2 = (bf16[8,128,128]{2,1,0:T(8,128)(2,1)S(1)}, bf16[8,128,128]{2,1,0:T(8,128)(2,1)S(1)}, u32[]{:S(2)}, u32[]{:S(2)}) collective-permute-start(bf16[8,128,128]{2,1,0:T(8,128)(2,1)S(1)} %half_kernel.1), channel_id=1, source_target_pairs={{0,16},{16,0},{32,48},{48,32},{64,80},{80,64},{96,112},{112,96},{1... | collective-permute-start | bytes 786440 | tf_op jit(solution)/shard_map/ppermute | solution.py:337
  61.6 9.9 %all-to-all-done.1 = bf16[32,96,128]{2,1,0:T(8,128)(2,1)S(1)} async-done(((bf16[32,96,128]{2,1,0:T(8,128)(2,1)}), bf16[32,96,128]{2,1,0:T(8,128)(2,1)S(1)}, u32[]{:S(2)}, u32[]{:S(2)}) %all-to-all-start.1) | async-done | bytes 786464 | tf_op jit(solution)/shard_map/all_to_all | solution.py:332
  71.4 2.6 %scan_kernel.1 = f32[16,2,16,128]{3,2,1,0:T(8,128)} custom-call(bf16[16,2,96,128]{3,2,1,0:T(8,128)(2,1)S(1)} %bitcast.8), custom_call_target="tpu_custom_call" | custom-call | flops 134217728 | bytes 1048576 | tf_op jit(solution)/shard_map/scan_kernel/pallas_call | solution.py:316
  74.0 4.1 %all-to-all-start.2 = ((f32[32,16,128]{2,1,0:T(8,128)}), f32[32,16,128]{2,1,0:T(8,128)S(1)}, u32[]{:S(2)}, u32[]{:S(2)}) async-start(f32[32,16,128]{2,1,0:T(8,128)} %bitcast.5), calls=%async_computation.2 | async-start | bytes 524288 | tf_op jit(solution)/shard_map/all_to_all | solution.py:332
  78.1 0.0 collective-permute-done.1.other_maps_ref
  78.1 0.0 collective-permute-done.2.other_grad_ref
  78.1 9.0 %all-to-all-done.2 = f32[32,16,128]{2,1,0:T(8,128)S(1)} async-done(((f32[32,16,128]{2,1,0:T(8,128)}), f32[32,16,128]{2,1,0:T(8,128)S(1)}, u32[]{:S(2)}, u32[]{:S(2)}) %all-to-all-start.2) | async-done | bytes 262176 | tf_op jit(solution)/shard_map/all_to_all | solution.py:332
  87.1 1.8 %output_kernel.1 = (bf16[128,256]{1,0:T(8,128)(2,1)}, bf16[32,8,1024]{2,1,0:T(8,128)(2,1)}) custom-call(s32[1]{0:T(128)} %bitcast.odd_ref, f32[16,2,16,128]{3,2,1,0:T(8,128)S(1)} %bitcast.10, f32[4,128,128]{2,1,0:T(8,128)S(1)} %get-tuple-element.27.maps_ref, f32[4,128,128]{2,1,0:T(8,128)S(1)} %collective-permute-done.1.other_maps_ref, ...), custom_call_target="tpu_custom_call" | custom-call | flops 268435456 | bytes 2162692 | tf_op jit(solution)/shard_map/output_kernel/pallas_call | solution.py:316
  88.9 3.8 %all-to-all-start.3 = ((bf16[32,8,1024]{2,1,0:T(8,128)(2,1)}), bf16[32,8,1024]{2,1,0:T(8,128)(2,1)S(1)}, u32[]{:S(2)}, u32[]{:S(2)}) async-start(bf16[32,8,1024]{2,1,0:T(8,128)(2,1)} %get-tuple-element.42), calls=%async_computation.3 | async-start | bytes 1048576 | tf_op jit(solution)/shard_map/all_to_all | solution.py:332
  92.7 0.0 copy-start.7
  92.7 0.0 copy-start.9
  92.7 0.0 copy-start.11
  92.7 0.3 carried_kernel.1
  93.0 2.3 %collective-permute-start.3 = (f32[2,128,128]{2,1,0:T(8,128)S(1)}, f32[2,128,128]{2,1,0:T(8,128)S(1)}, u32[]{:S(2)}, u32[]{:S(2)}) collective-permute-start(f32[2,128,128]{2,1,0:T(8,128)S(1)} %carried_kernel.1), channel_id=1, source_target_pairs={{0,16},{16,0},{32,48},{48,32},{64,80},{80,64},{96,112},{112,96},{1... | collective-permute-start | bytes 393224 | tf_op jit(solution)/shard_map/ppermute | solution.py:337
  95.3 1.0 collective-permute-done.3.carried_ref
  96.2 0.0 copy-done.7
  96.2 0.0 copy-done.9
  96.2 0.0 copy-done.11
  96.3 4.1 %gradient_kernel.1 = (f32[128,128]{1,0:T(8,128)}, f32[128,128]{1,0:T(8,128)}, f32[128,256]{1,0:T(8,128)}) custom-call(s32[1]{0:T(128)} %bitcast.odd_ref, bf16[128,128]{1,0:T(8,128)(2,1)S(1)} %copy-done.2, bf16[128,128]{1,0:T(8,128)(2,1)S(1)} %copy-done.3, f32[16,2,16,128]{3,2,1,0:T(8,128)S(1)} %bitcast.11, ...), custom_call_target="tpu_custom_call" | custom-call | flops 536870912 | bytes 2031620 | tf_op jit(solution)/shard_map/gradient_kernel/pallas_call | solution.py:316
  100.3 4.0 %all-to-all-done.3 = bf16[32,8,1024]{2,1,0:T(8,128)(2,1)S(1)} async-done(((bf16[32,8,1024]{2,1,0:T(8,128)(2,1)}), bf16[32,8,1024]{2,1,0:T(8,128)(2,1)S(1)}, u32[]{:S(2)}, u32[]{:S(2)}) %all-to-all-start.3) | async-done | bytes 524320 | tf_op jit(solution)/shard_map/all_to_all | solution.py:332
  104.3 0.7 sum_kernel.1
  (2 shorter events, 0.0 us)
Async XLA Ops:
  2.3 15.9 %copy-start.1 = (bf16[128,256]{1,0:T(8,128)(2,1)S(1)}, bf16[128,256]{1,0:T(8,128)(2,1)}, u32[]{:S(2)}) copy-start(bf16[128,256]{1,0:T(8,128)(2,1)} %v_ref.1) | copy-start | bytes 196612
  2.3 15.9 %copy-start.2 = (bf16[128,128]{1,0:T(8,128)(2,1)S(1)}, bf16[128,128]{1,0:T(8,128)(2,1)}, u32[]{:S(2)}) copy-start(bf16[128,128]{1,0:T(8,128)(2,1)} %q_ref.3) | copy-start | bytes 98308
  2.3 15.9 %copy-start.3 = (bf16[128,128]{1,0:T(8,128)(2,1)S(1)}, bf16[128,128]{1,0:T(8,128)(2,1)}, u32[]{:S(2)}) copy-start(bf16[128,128]{1,0:T(8,128)(2,1)} %k_ref.3) | copy-start | bytes 98308
  2.3 15.9 %copy-start.5 = (s32[128,2]{0,1:T(2,128)S(1)}, s32[128,2]{0,1:T(2,128)}, u32[]{:S(2)}) copy-start(s32[128,2]{0,1:T(2,128)} %param.11) | copy-start | bytes 3076
  2.3 38.7 %all-to-all-start = ((bf16[16,128,128]{2,1,0:T(8,128)(2,1)}), bf16[16,128,128]{2,1,0:T(8,128)(2,1)S(1)}, u32[]{:S(2)}, u32[]{:S(2)}) async-start(bf16[16,128,128]{2,1,0:T(8,128)(2,1)} %broadcast_in_dim.2), calls=%async_computation | async-start | bytes 1048576 | tf_op jit(solution)/shard_map/all_to_all | solution.py:332
  18.2 0.7 copy-start.4
  18.9 22.1 %copy-start = (bf16[256,2048]{1,0:T(8,128)(2,1)S(1)}, bf16[256,2048]{1,0:T(8,128)(2,1)}, u32[]{:S(2)}) copy-start(bf16[256,2048]{1,0:T(8,128)(2,1)} %w_ref.1) | copy-start | bytes 3145732
  26.6 0.7 copy-start.6
  27.3 0.6 copy-start.8
  27.9 0.7 copy-start.10
  28.6 4.0 %collective-permute-start = (f32[4,128,128]{2,1,0:T(8,128)S(1)}, f32[4,128,128]{2,1,0:T(8,128)S(1)}, u32[]{:S(2)}, u32[]{:S(2)}) collective-permute-start(f32[4,128,128]{2,1,0:T(8,128)S(1)} %get-tuple-element.24.own_ref), channel_id=1, source_target_pairs={{0,16},{16,0},{32,48},{48,32},{64,80},{80,64},{96,112},{112,96},{1... | collective-permute-start | bytes 786440 | tf_op jit(solution)/shard_map/ppermute | solution.py:337
  42.9 28.5 %all-to-all-start.1 = ((bf16[32,96,128]{2,1,0:T(8,128)(2,1)}), bf16[32,96,128]{2,1,0:T(8,128)(2,1)S(1)}, u32[]{:S(2)}, u32[]{:S(2)}) async-start(bf16[32,96,128]{2,1,0:T(8,128)(2,1)} %bitcast.3), calls=%async_computation.1 | async-start | bytes 1572864 | tf_op jit(solution)/shard_map/all_to_all | solution.py:332
  57.2 20.9 %collective-permute-start.1 = (f32[4,128,128]{2,1,0:T(8,128)S(1)}, f32[4,128,128]{2,1,0:T(8,128)S(1)}, u32[]{:S(2)}, u32[]{:S(2)}) collective-permute-start(f32[4,128,128]{2,1,0:T(8,128)S(1)} %get-tuple-element.27.maps_ref), channel_id=1, source_target_pairs={{0,16},{16,0},{32,48},{48,32},{64,80},{80,64},{96,112},{112,96},{1... | collective-permute-start | bytes 786440 | tf_op jit(solution)/shard_map/ppermute | solution.py:337
  59.4 18.7 %collective-permute-start.2 = (bf16[8,128,128]{2,1,0:T(8,128)(2,1)S(1)}, bf16[8,128,128]{2,1,0:T(8,128)(2,1)S(1)}, u32[]{:S(2)}, u32[]{:S(2)}) collective-permute-start(bf16[8,128,128]{2,1,0:T(8,128)(2,1)S(1)} %half_kernel.1), channel_id=1, source_target_pairs={{0,16},{16,0},{32,48},{48,32},{64,80},{80,64},{96,112},{112,96},{1... | collective-permute-start | bytes 786440 | tf_op jit(solution)/shard_map/ppermute | solution.py:337
  74.0 13.1 %all-to-all-start.2 = ((f32[32,16,128]{2,1,0:T(8,128)}), f32[32,16,128]{2,1,0:T(8,128)S(1)}, u32[]{:S(2)}, u32[]{:S(2)}) async-start(f32[32,16,128]{2,1,0:T(8,128)} %bitcast.5), calls=%async_computation.2 | async-start | bytes 524288 | tf_op jit(solution)/shard_map/all_to_all | solution.py:332
  88.9 15.4 %all-to-all-start.3 = ((bf16[32,8,1024]{2,1,0:T(8,128)(2,1)}), bf16[32,8,1024]{2,1,0:T(8,128)(2,1)S(1)}, u32[]{:S(2)}, u32[]{:S(2)}) async-start(bf16[32,8,1024]{2,1,0:T(8,128)(2,1)} %get-tuple-element.42), calls=%async_computation.3 | async-start | bytes 1048576 | tf_op jit(solution)/shard_map/all_to_all | solution.py:332
  92.7 3.6 %copy-start.7 = (f32[2,128,128]{2,1,0:T(8,128)S(1)}, f32[2,128,128]{2,1,0:T(8,128)}, u32[]{:S(2)}) copy-start(f32[2,128,128]{2,1,0:T(8,128)} %copy-done.6) | copy-start | bytes 393220
  92.7 3.6 %copy-start.9 = (f32[2,128,128]{2,1,0:T(8,128)S(1)}, f32[2,128,128]{2,1,0:T(8,128)}, u32[]{:S(2)}) copy-start(f32[2,128,128]{2,1,0:T(8,128)} %copy-done.8) | copy-start | bytes 393220
  92.7 3.6 %copy-start.11 = (f32[2,128,128]{2,1,0:T(8,128)S(1)}, f32[2,128,128]{2,1,0:T(8,128)}, u32[]{:S(2)}) copy-start(f32[2,128,128]{2,1,0:T(8,128)} %copy-done.10) | copy-start | bytes 393220
  93.0 3.2 %collective-permute-start.3 = (f32[2,128,128]{2,1,0:T(8,128)S(1)}, f32[2,128,128]{2,1,0:T(8,128)S(1)}, u32[]{:S(2)}, u32[]{:S(2)}) collective-permute-start(f32[2,128,128]{2,1,0:T(8,128)S(1)} %carried_kernel.1), channel_id=1, source_target_pairs={{0,16},{16,0},{32,48},{48,32},{64,80},{80,64},{96,112},{112,96},{1... | collective-permute-start | bytes 393224 | tf_op jit(solution)/shard_map/ppermute | solution.py:337

commit v4 on v3

--- a/solution.py
+++ b/solution.py
@@ -106,44 +106,69 @@
         cols_ref[head, 1] = weight
 
 
-def compose_kernel(
-    odd_ref, own_ref, other_ref, probe_ref, local_ref,
-    trans_ref, state_ref, diag_ref, maps_ref,
+def in_order(late, own, other):
+    return jnp.where(late, other, own), jnp.where(late, own, other)
+
+
+def compose_heads(late, own_ref, other_ref, head, group):
+    own, other = own_ref[head], other_ref[head]
+    first, second = in_order(late, own, other)
+    first_state, second_state = in_order(late, own_ref[group + head], other_ref[group + head])
+    return mm(second, first), mm(first_state, second, 1, 1) + second_state
+
+
+def compose_maps(late, other_ref, head, group, probe, local):
+    moved = jnp.where(late, mm(probe, other_ref[head]), probe)
+    return moved, jnp.where(late, local + mm(probe, other_ref[group + head], 1, 1), local)
+
+
+def chip_kernel(flags_ref, own_ref, other_ref, probe_ref, local_ref, chip_ref, maps_ref):
+    group = probe_ref.shape[0]
+    late = flags_ref[0] == 1
+    for head in range(group):
+        span = slice(head * WIDTH, (head + 1) * WIDTH)
+        chip_ref[head], chip_ref[group + head] = compose_heads(
+            late, own_ref, other_ref, head, group
+        )
+        maps_ref[head], maps_ref[group + head] = compose_maps(
+            late, other_ref, head, group, probe_ref[head], local_ref[:, span]
+        )
+
+
+def quad_kernel(
+    flags_ref, own_ref, other_ref, chip_maps_ref, trans_ref, state_ref, diag_ref, maps_ref
 ):
-    group = probe_ref.shape[0]
-    is_odd = odd_ref[0] == 1
+    group = trans_ref.shape[0]
+    core = flags_ref[0] == 1
+    late = flags_ref[1] == 1
     rows, cols = ids(WIDTH)
-    half = WIDTH // 2
-    for head in range(group):
-        span = slice(head * WIDTH, (head + 1) * WIDTH)
-        own, other = own_ref[head], other_ref[head]
-        own_state, other_state = own_ref[group + head], other_ref[group + head]
-        first = jnp.where(is_odd, other, own)
-        second = jnp.where(is_odd, own, other)
-        first_state = jnp.where(is_odd, other_state, own_state)
-        second_state = jnp.where(is_odd, own_state, other_state)
-        transition = mm(second, first)
-        state_t = mm(first_state, second, 1, 1) + second_state
+    share = WIDTH // 4
+    for head in range(group):
+        transition, state_t = compose_heads(late, own_ref, other_ref, head, group)
         rounded = transition.astype(BF16)
         rest = jnp.where(rows == cols, transition - rounded.astype(F32), 0.0)
         diag_ref[head] = jnp.broadcast_to(
             jnp.sum(rest, axis=0, keepdims=True), (diag_ref.shape[1], WIDTH)
         ).astype(BF16)
-        trans_ref[head] = jnp.where(is_odd, transition[half:], transition[:half]).astype(BF16)
-        high, low = split_bf16(state_t)
-        state_ref[head] = jnp.where(is_odd, low, high)
-        probe = probe_ref[head]
-        local = local_ref[:, span]
-        maps_ref[head] = jnp.where(is_odd, mm(probe, other), probe)
-        maps_ref[group + head] = jnp.where(is_odd, local + mm(probe, other_state, 1, 1), local)
+        quarters = [transition[at * share : (at + 1) * share] for at in range(4)]
+        trans_ref[head] = jnp.where(
+            late,
+            jnp.where(core, quarters[3], quarters[2]),
+            jnp.where(core, quarters[1], quarters[0]),
+        ).astype(BF16)
+        high = state_t.astype(BF16).astype(F32)
+        part = jnp.where(core, state_t - high, high)
+        state_ref[head] = jnp.where(late, 0.0, part).astype(BF16)
+        maps_ref[head], maps_ref[group + head] = compose_maps(
+            late, other_ref, head, group, chip_maps_ref[head], chip_maps_ref[group + head]
+        )
 
 
 def cotangent_kernel(
     grad_ref, w_ref, maps_ref, trans_ref, state_ref, diag_ref, cot_ref, send_ref
 ):
     blocks = grad_ref.shape[0]
-    group = trans_ref.shape[0]
-    half = WIDTH // 2
+    group, share, _ = trans_ref.shape
     total = jnp.zeros(cot_ref.shape, F32)
     for block in range(0, blocks, 2):
         left = jnp.concatenate([grad_ref[block], grad_ref[block + 1]], axis=1)
@@ -160,40 +185,40 @@
         trans = trans_ref[head]
         for chip in range(chips):
             mine = slice(chip * part, (chip + 1) * part)
-            send_ref[chip, head, :half, :] = trans
-            send_ref[chip, head, half:, :] = jnp.concatenate(
-                [state[mine], high[mine], low[mine], diag], axis=0
+            send_ref[chip, head, :share, :] = trans
+            send_ref[chip, head, share:, :] = jnp.concatenate(
+                [state[mine], diag, high[mine], low[mine]], axis=0
             ).astype(BF16)
 
 
 def scan_kernel(got_ref, send_ref):
-    chips = got_ref.shape[0]
-    half = WIDTH // 2
-    part = WIDTH // chips
-
-    def step(state, chip, dim):
+    quads, members = got_ref.shape[:2]
+    share = WIDTH // members
+    part = send_ref.shape[2] // 2
+
+    def step(state, quad, dim):
         high, low = split_bf16(state)
         both = jnp.concatenate([high.astype(F32), low.astype(F32)], axis=0).astype(BF16)
-        trans = jnp.concatenate([got_ref[chip, 0, :half, :], got_ref[chip, 1, :half, :]], axis=0)
-        rest = got_ref[chip, 0, half:, :].astype(F32)
-        other = got_ref[chip, 1, half:, :].astype(F32)
+        trans = jnp.concatenate(
+            [got_ref[quad, member, :share, :] for member in range(members)], axis=0
+        )
+        rest = [got_ref[quad, member, share:, :].astype(F32) for member in range(members)]
         product = mm_bf16(both, trans, 1, dim)
-        moved = product[:part] + product[part:] + state * rest[3 * part :]
+        moved = product[:part] + product[part:] + state * rest[0][part : 2 * part]
         if dim == 1:
-            return moved + rest[:part] + other[:part]
-        return moved + (
-            (rest[part : 2 * part] + other[part : 2 * part])
-            + (rest[2 * part : 3 * part] + other[2 * part : 3 * part])
-        )
+            return moved + rest[0][:part] + rest[1][:part]
+        for piece in rest:
+            moved = moved + (piece[2 * part : 3 * part] + piece[3 * part :])
+        return moved
 
     ahead = jnp.zeros((part, WIDTH), F32)
     back = jnp.zeros((part, WIDTH), F32)
-    for turn in range(chips):
-        late = chips - 1 - turn
-        for core in range(2):
-            send_ref[turn, core, :part, :] = ahead
-            send_ref[late, core, part:, :] = back
-        if turn < chips - 1:
+    for turn in range(quads):
+        late = quads - 1 - turn
+        for member in range(members):
+            send_ref[turn, member, :part, :] = ahead
+            send_ref[late, member, part:, :] = back
+        if turn < quads - 1:
             ahead = step(ahead, turn, 1)
             back = step(back, late, 0)
 
@@ -205,12 +230,12 @@
 
 
 def output_kernel(
-    odd_ref, got_ref, maps_ref, other_maps_ref, grad_ref, other_grad_ref, attn_ref, send_ref
+    flags_ref, got_ref, maps_ref, other_maps_ref, grad_ref, other_grad_ref, attn_ref, send_ref
 ):
     group = maps_ref.shape[0] // 2
     dests, part, _ = send_ref.shape
     blocks = other_grad_ref.shape[0]
-    first = odd_ref[0] * blocks
+    first = flags_ref[0] * blocks
     own, other = [], []
     for head in range(group):
         state_t = gather_rows(got_ref, head, 0)
@@ -243,25 +268,32 @@
         out_ref[:, core * width : (core + 1) * width] = total * scaling
 
 
-def half_kernel(odd_ref, grad_ref, half_ref):
+def half_kernel(flags_ref, grad_ref, half_ref):
     blocks = half_ref.shape[0]
-    half_ref[...] = grad_ref[pl.ds((1 - odd_ref[0]) * blocks, blocks)]
-
-
-def carried_kernel(cot_ref, probe_ref, carried_ref):
-    for head in range(probe_ref.shape[0]):
-        carried_ref[head] = mm(
-            cot_ref[:, head * WIDTH : (head + 1) * WIDTH], probe_ref[head], 0, 0
-        )
+    half_ref[...] = grad_ref[pl.ds((1 - flags_ref[0]) * blocks, blocks)]
+
+
+def carried_kernel(cot_ref, probe_ref, chip_maps_ref, carried_ref):
+    group = probe_ref.shape[0]
+    for head in range(group):
+        cot = cot_ref[:, head * WIDTH : (head + 1) * WIDTH]
+        carried_ref[head] = mm(cot, probe_ref[head], 0, 0)
+        carried_ref[group + head] = mm(cot, chip_maps_ref[head], 0, 0)
+
+
+def add_kernel(own_ref, other_ref, total_ref):
+    group = total_ref.shape[0]
+    total_ref[...] = own_ref[group:] + other_ref[group:]
 
 
 def gradient_kernel(
-    odd_ref, q_ref, k_ref, got_ref, other_ref, carried_ref, cot_ref, tmat_ref, mix_ref,
-    ratio_ref, uw_ref, cols_ref, q_grad_ref, k_grad_ref, v_grad_ref,
+    flags_ref, q_ref, k_ref, got_ref, other_ref, other_chip_ref, carried_ref, chip_carried_ref,
+    cot_ref, tmat_ref, mix_ref, ratio_ref, uw_ref, cols_ref, q_grad_ref, k_grad_ref, v_grad_ref,
 ):
     length = q_ref.shape[0]
     group = tmat_ref.shape[0]
-    is_odd = odd_ref[0] == 1
+    core = flags_ref[0] == 1
+    late = flags_ref[1] == 1
     q = q_ref[...].astype(F32)
     k = k_ref[...].astype(F32)
     q_inv = inverse_norm(q)
@@ -275,11 +307,14 @@
         span = slice(head * WIDTH, (head + 1) * WIDTH)
         state_t = gather_rows(got_ref, head, 0)
         end_t = gather_rows(got_ref, head, 1)
-        other = other_ref[head]
-        through_state = mm(state_t, other, 1, 1) + other_ref[group + head]
-        through_end = mm(end_t, other) + carried_ref[head]
-        state_t = jnp.where(is_odd, through_state, state_t)
-        end_t = jnp.where(is_odd, end_t, through_end)
+        for after, other, term, carried in (
+            (late, other_chip_ref[head], other_chip_ref[group + head], chip_carried_ref[head]),
+            (core, other_ref[head], other_ref[group + head], carried_ref[head]),
+        ):
+            through_state = mm(state_t, other, 1, 1) + term
+            through_end = mm(end_t, other) + carried
+            state_t = jnp.where(after, through_state, state_t)
+            end_t = jnp.where(after, end_t, through_end)
         cot = cot_ref[:, span]
         ratio = ratio_ref[head]
         decay = cols_ref[head, 0]
@@ -332,9 +367,9 @@
     return lax.all_to_all(value, axis, 0, 0, tiled=True)
 
 
-def across(value):
+def across(value, step):
     slabs = lax.axis_size("seq")
-    return lax.ppermute(value, "seq", [(slab, slab ^ 1) for slab in range(slabs)])
+    return lax.ppermute(value, "seq", [(slab, slab ^ step) for slab in range(slabs)])
 
 
 def per_device(queries, keys, values, gate_code, beta_code, out_grad, w_out):
@@ -345,13 +380,15 @@
     chips = slabs // 2
     part = WIDTH // chips
     square = (group, length, WIDTH)
+    states_shape = (2 * group, WIDTH, WIDTH)
     flat = (length, group * WIDTH)
-    odd = (lax.axis_index("seq") % 2).astype(jnp.int32).reshape(1)
+    place = lax.axis_index("seq").astype(jnp.int32)
+    flags = jnp.stack([place & 1, (place >> 1) & 1])
     full_grad = swap(jnp.broadcast_to(out_grad[None], (heads, length, WIDTH)), "head")
     pair, tmat, mix, ratio, uw, probe, local, columns = call(
         prepare_kernel,
         [
-            shape((2 * group, WIDTH, WIDTH)),
+            shape(states_shape),
             shape(square),
             shape(square),
             shape(square),
@@ -363,48 +400,66 @@
         1 << 30,
         queries, keys, values, gate_code.T, beta_code.T,
     )
-    other = across(pair)
+    other = across(pair, 1)
+    chip, chip_maps = call(
+        chip_kernel,
+        [shape(states_shape), shape((2 * group, length, WIDTH))],
+        1 << 28,
+        flags, pair, other, probe, local,
+    )
+    other_chip = across(chip, 2)
     trans, state, diag, maps = call(
-        compose_kernel,
+        quad_kernel,
         [
-            shape((group, WIDTH // 2, WIDTH), BF16),
+            shape((group, WIDTH // 4, WIDTH), BF16),
             shape((group, WIDTH, WIDTH), BF16),
             shape((group, part, WIDTH), BF16),
             shape((2 * group, length, WIDTH)),
         ],
         1 << 28,
-        odd, pair, other, probe, local,
-    )
-    other_maps = across(maps)
+        flags, chip, other_chip, chip_maps,
+    )
+    other_maps = across(maps, 1)
     cot, send = call(
         cotangent_kernel,
-        [shape(flat), shape((chips, group, WIDTH // 2 + 4 * part, WIDTH), BF16)],
+        [shape(flat), shape((chips, group, WIDTH // 4 + 4 * part, WIDTH), BF16)],
         1 << 28,
         full_grad, w_out, maps, trans, state, diag,
     )
+    got = swap(send.reshape((slabs,) + send.shape[2:]), "seq")
     (half,) = call(
-        half_kernel, [shape((heads // 2, length, WIDTH), BF16)], 1 << 20, odd, full_grad
-    )
-    other_half = across(half)
-    got = swap(send.reshape((slabs,) + send.shape[2:]), "seq")
-    (carried,) = call(carried_kernel, [shape((group, WIDTH, WIDTH))], 1 << 26, cot, probe)
-    carried = across(carried)
+        half_kernel, [shape((heads // 2, length, WIDTH), BF16)], 1 << 20, flags, full_grad
+    )
+    other_half = across(half, 1)
+    (own_carried,) = call(
+        carried_kernel, [shape(states_shape)], 1 << 26, cot, probe, chip_maps
+    )
+    carried = across(own_carried, 1)
+    got, carried = lax.optimization_barrier((got, carried))
     (back,) = call(
-        scan_kernel, [shape((chips, 2, 2 * part, WIDTH))], 1 << 27, got.reshape(send.shape)
-    )
-    states = swap(back.reshape(slabs, 2 * part, WIDTH), "seq").reshape(back.shape)
+        scan_kernel,
+        [shape((slabs // 4, 4, 2 * part, WIDTH))],
+        1 << 27,
+        got.reshape((slabs // 4, 4) + got.shape[1:]),
+    )
+    states = swap(back.reshape(slabs, 2 * part, WIDTH), "seq").reshape(
+        chips, group, 2 * part, WIDTH
+    )
+    (chip_carried,) = call(add_kernel, [shape(square)], 1 << 20, own_carried, carried)
+    chip_carried = across(chip_carried, 2)
+    states, chip_carried = lax.optimization_barrier((states, chip_carried))
     attn_out, grad_send = call(
         output_kernel,
         [shape(flat, BF16), shape((slabs, part, heads // 2 * WIDTH), BF16)],
         1 << 28,
-        odd, states, maps, other_maps, full_grad, other_half,
+        flags, states, maps, other_maps, full_grad, other_half,
     )
     grad_got = swap(grad_send, "seq")
     q_grad, k_grad, v_grad = call(
         gradient_kernel,
         [shape((length, WIDTH)), shape((length, WIDTH)), shape(flat)],
         1 << 29,
-        odd, queries, keys, states, other, carried, cot, tmat, mix, ratio, uw, columns,
+        flags, queries, keys, states, other, other_chip, carried, chip_carried, cot, tmat, mix, ratio, uw, columns,
     )
     scaling = (length * slabs) ** (-0.5)
     (weight_grad,) = call(

time: 106 us -> 105 us (level)
  waiting for transfers between devices: 32.5 us -> 23 us
  starting transfers between devices: 47.5 us -> 52.6 us
  Pallas kernels: 19.9 us -> 23.5 us
    all_to_all x4, waiting for transfers between devices: 30.4 us -> 11.1 us  [swap(): return lax.all_to_all(value, axis, 0, 0, tiled=True)]
    ppermute x4 -> x6, waiting for transfers between devices: 2.11 us -> 11.9 us  [across(): lax.ppermute(value, 'seq', [(slab, slab ^ step) for slab in range(slabs)])]
    ppermute x4 -> x6, starting transfers between devices: 9.44 us -> 15.8 us  [across(): lax.ppermute(value, 'seq', [(slab, slab ^ step) for slab in range(slabs)])]
    pallas_call x9 -> x11, Pallas kernels: 19.9 us -> 23.5 us  [call(): pl.pallas_call(kernel, out_shape=outs, in_specs=[smem if scalar else vmem...]
    all_to_all x4, starting transfers between devices: 38.1 us -> 36.8 us  [swap(): return lax.all_to_all(value, axis, 0, 0, tiled=True)]
    unnamed x24 -> x28, local copies, waits for them, and re-layouts: 2.61 us -> 2.62 us
  transfers between devices with their start and end apart: 8 -> 10, of which waited for: 6 -> 6; matrix products, arithmetic and copies ran while one was open for 0% -> 0% of each run, Pallas kernels for 15% -> 18%
where the time goes in v4:
time: 105 us; the launch traced here: 104 us
  starting transfers between devices  52.6 us (50%)
  Pallas kernels  23.5 us (22%)
  waiting for transfers between devices  23 us (22%)
  local copies, waits for them, and re-layouts  4.27 us (4%)
    all_to_all x4, starting transfers between devices, swap(): return lax.all_to_all(value, axis, 0, 0, tiled=True)  36.8 us
    pallas_call x11, Pallas kernels, call(): pl.pallas_call(kernel, out_shape=outs, in_specs=[smem if scalar else vmem...  23.5 us
    ppermute x6, starting transfers between devices, across(): lax.ppermute(value, 'seq', [(slab, slab ^ step) for slab in range(slabs)])  15.8 us
    ppermute x6, waiting for transfers between devices, across(): lax.ppermute(value, 'seq', [(slab, slab ^ step) for slab in range(slabs)])  11.9 us
    all_to_all x4, waiting for transfers between devices, swap(): return lax.all_to_all(value, axis, 0, 0, tiled=True)  11.1 us
    unnamed x28, local copies, waits for them, and re-layouts  2.62 us
  transfers between devices with their start and end apart: 10, of which 6 were waited for; matrix products, arithmetic and copies ran while one was open for 0% of the time, Pallas kernels for 18%

profile of v4, /device:TPU:1, one launch (start us, length us, event | category | flops | bytes accessed | tf_op | source)
XLA Modules:
  0.0 104.3 jit_solution(10109255344469596023)
XLA Ops:
  0.6 1.6 %broadcast_in_dim.2 = bf16[16,128,128]{2,1,0:T(8,128)(2,1)} broadcast(bf16[128,128]{1,0:T(8,128)(2,1)} %param.12), dimensions={1,2} | broadcast | bytes 557056 | tf_op jit(solution)/shard_map/broadcast_in_dim | solution.py:387
  2.3 15.9 %all-to-all-start = ((bf16[16,128,128]{2,1,0:T(8,128)(2,1)}), bf16[16,128,128]{2,1,0:T(8,128)(2,1)S(1)}, u32[]{:S(2)}, u32[]{:S(2)}) async-start(bf16[16,128,128]{2,1,0:T(8,128)(2,1)} %broadcast_in_dim.2), calls=%async_computation | async-start | bytes 1048576 | tf_op jit(solution)/shard_map/all_to_all | solution.py:367
  18.2 0.0 copy-start.12
  18.2 0.0 copy-done.7
  18.2 0.0 copy-done.9
  18.2 0.0 copy-done.11
  18.2 0.0 copy-done.13
  18.2 0.6 copy-done.12
  18.9 7.7 %prepare_kernel.1 = (f32[4,128,128]{2,1,0:T(8,128)S(1)}, f32[2,128,128]{2,1,0:T(8,128)S(1)}, f32[2,128,128]{2,1,0:T(8,128)S(1)}, f32[2,128,128]{2,1,0:T(8,128)S(...) custom-call(bf16[128,128]{1,0:T(8,128)(2,1)S(1)} %copy-done.7, ...), custom_call_target="tpu_custom_call" | custom-call | flops 1073741824 | bytes 1574912 | tf_op jit(solution)/shard_map/prepare_kernel/pallas_call | solution.py:351
  26.6 0.0 copy-start.1
  26.6 0.6 copy-done.1
  27.2 0.6 copy-done.3
  27.9 0.6 copy-done.5
  28.5 3.0 %collective-permute-start = (f32[4,128,128]{2,1,0:T(8,128)S(1)}, f32[4,128,128]{2,1,0:T(8,128)S(1)}, u32[]{:S(2)}, u32[]{:S(2)}) collective-permute-start(f32[4,128,128]{2,1,0:T(8,128)S(1)} %get-tuple-element.30.own_ref), channel_id=1, source_target_pairs={{0,16},{16,0},{32,48},{48,32},{64,80},{80,64},{96,112},{112,96},{1... | collective-permute-start | bytes 786440 | tf_op jit(solution)/shard_map/ppermute | solution.py:372
  31.5 0.1 pad_add_fusion.flags_ref
  31.6 1.1 %collective-permute-done.other_ref = f32[4,128,128]{2,1,0:T(8,128)S(1)} collective-permute-done((f32[4,128,128]{2,1,0:T(8,128)S(1)}, f32[4,128,128]{2,1,0:T(8,128)S(1)}, u32[]{:S(2)}, u32[]{:S(2)}) %collective-permute-start) | collective-permute-done | bytes 262176 | tf_op jit(solution)/shard_map/ppermute | solution.py:372
  32.7 1.4 %chip_kernel.1 = (f32[4,128,128]{2,1,0:T(8,128)S(1)}, f32[4,128,128]{2,1,0:T(8,128)S(1)}) custom-call(s32[2]{0:T(128)S(1)} %pad_add_fusion.flags_ref, f32[4,128,128]{2,1,0:T(8,128)S(1)} %get-tuple-element.30.own_ref, f32[4,128,128]{2,1,0:T(8,128)S(1)} %collective-permute-done.other_ref, f32[2,128,128]{2,1,0:T(8,128)S(1)} %get-tuple-element.31.probe_ref, ...), custom_call_target="tpu_custom_call" | custom-call | flops 268435456 | bytes 1310728 | tf_op jit(solution)/shard_map/chip_kernel/pallas_call | solution.py:351
  34.1 3.1 %collective-permute-start.1 = (f32[4,128,128]{2,1,0:T(8,128)S(1)}, f32[4,128,128]{2,1,0:T(8,128)S(1)}, u32[]{:S(2)}, u32[]{:S(2)}) collective-permute-start(f32[4,128,128]{2,1,0:T(8,128)S(1)} %get-tuple-element.33.own_ref), channel_id=1, source_target_pairs={{0,32},{16,48},{32,0},{48,16},{64,96},{80,112},{96,64},{112,80},{1... | collective-permute-start | bytes 786440 | tf_op jit(solution)/shard_map/ppermute | solution.py:372
  37.2 6.3 %collective-permute-done.1.other_ref.other_chip_ref = f32[4,128,128]{2,1,0:T(8,128)S(1)} collective-permute-done((f32[4,128,128]{2,1,0:T(8,128)S(1)}, f32[4,128,128]{2,1,0:T(8,128)S(1)}, u32[]{:S(2)}, u32[]{:S(2)}) %collective-permute-start.1) | collective-permute-done | bytes 262176 | tf_op jit(solution)/shard_map/ppermute | solution.py:372
  43.5 1.4 %quad_kernel.1 = (bf16[2,32,128]{2,1,0:T(8,128)(2,1)S(1)}, bf16[2,128,128]{2,1,0:T(8,128)(2,1)S(1)}, bf16[2,8,128]{2,1,0:T(8,128)(2,1)S(1)}, f32[4,128,128]{2,1,0:T(8,128)S(1)}) custom-call(s32[2]{0:T(128)S(1)} %pad_add_fusion.flags_ref, f32[4,128,128]{2,1,0:T(8,128)S(1)} %get-tuple-element.33.own_ref, ...), custom_call_target="tpu_custom_call" | custom-call | flops 268435456 | bytes 1134600 | tf_op jit(solution)/shard_map/quad_kernel/pallas_call | solution.py:351
  44.9 0.0 all-to-all-done.grad_ref
  44.9 0.0 copy-done
  44.9 1.7 %cotangent_kernel.1 = (f32[128,256]{1,0:T(8,128)S(1)}, bf16[16,2,64,128]{3,2,1,0:T(8,128)(2,1)}) custom-call(bf16[16,128,128]{2,1,0:T(8,128)(2,1)S(1)} %all-to-all-done.grad_ref, bf16[256,2048]{1,0:T(8,128)(2,1)S(1)} %copy-done, f32[4,128,128]{2,1,0:T(8,128)S(1)} %get-tuple-element.35.maps_ref, bf16[2,32,128]{2,1,0:T(8,128)(2,1)S(1)} %get-tuple-element.36.trans_ref, ...), custom_call_target="tpu_custom_call" | custom-call | flops 268435456 | bytes 2576384 | tf_op jit(solution)/shard_map/cotangent_kernel/pallas_call | solution.py:351
  46.7 10.4 %all-to-all-start.1 = ((bf16[32,64,128]{2,1,0:T(8,128)(2,1)}), bf16[32,64,128]{2,1,0:T(8,128)(2,1)S(1)}, u32[]{:S(2)}, u32[]{:S(2)}) async-start(bf16[32,64,128]{2,1,0:T(8,128)(2,1)} %bitcast.4), calls=%async_computation.1 | async-start | bytes 1048576 | tf_op jit(solution)/shard_map/all_to_all | solution.py:367
  57.1 0.4 carried_kernel.1.own_ref
  57.5 2.1 %collective-permute-start.2 = (f32[4,128,128]{2,1,0:T(8,128)S(1)}, f32[4,128,128]{2,1,0:T(8,128)S(1)}, u32[]{:S(2)}, u32[]{:S(2)}) collective-permute-start(f32[4,128,128]{2,1,0:T(8,128)S(1)} %carried_kernel.1.own_ref), channel_id=1, source_target_pairs={{0,16},{16,0},{32,48},{48,32},{64,80},{80,64},{96,112},{112,96},{1... | collective-permute-start | bytes 786440 | tf_op jit(solution)/shard_map/ppermute | solution.py:372
  59.6 2.2 %collective-permute-start.4 = (f32[4,128,128]{2,1,0:T(8,128)S(1)}, f32[4,128,128]{2,1,0:T(8,128)S(1)}, u32[]{:S(2)}, u32[]{:S(2)}) collective-permute-start(f32[4,128,128]{2,1,0:T(8,128)S(1)} %get-tuple-element.35.maps_ref), channel_id=1, source_target_pairs={{0,16},{16,0},{32,48},{48,32},{64,80},{80,64},{96,112},{112,96},{1... | collective-permute-start | bytes 786440 | tf_op jit(solution)/shard_map/ppermute | solution.py:372
  61.8 1.3 %half_kernel.1 = bf16[8,128,128]{2,1,0:T(8,128)(2,1)} custom-call(s32[2]{0:T(128)S(1)} %pad_add_fusion.flags_ref, bf16[16,128,128]{2,1,0:T(8,128)(2,1)S(1)} %all-to-all-done.grad_ref), custom_call_target="tpu_custom_call" | custom-call | flops 1048576 | bytes 786440 | tf_op jit(solution)/shard_map/half_kernel/pallas_call | solution.py:351
  63.1 2.1 %collective-permute-start.5 = (bf16[8,128,128]{2,1,0:T(8,128)(2,1)}, bf16[8,128,128]{2,1,0:T(8,128)(2,1)S(1)}, u32[]{:S(2)}, u32[]{:S(2)}) collective-permute-start(bf16[8,128,128]{2,1,0:T(8,128)(2,1)} %half_kernel.1), channel_id=1, source_target_pairs={{0,16},{16,0},{32,48},{48,32},{64,80},{80,64},{96,112},{112,96},{1... | collective-permute-start | bytes 786440 | tf_op jit(solution)/shard_map/ppermute | solution.py:372
  65.3 0.0 collective-permute-done.2.other_ref.carried_ref
  65.3 3.3 %all-to-all-done.1 = bf16[32,64,128]{2,1,0:T(8,128)(2,1)S(1)} async-done(((bf16[32,64,128]{2,1,0:T(8,128)(2,1)}), bf16[32,64,128]{2,1,0:T(8,128)(2,1)S(1)}, u32[]{:S(2)}, u32[]{:S(2)}) %all-to-all-start.1) | async-done | bytes 524320 | tf_op jit(solution)/shard_map/all_to_all | solution.py:367
  68.6 1.6 %scan_kernel.1 = f32[8,4,16,128]{3,2,1,0:T(8,128)} custom-call(bf16[8,4,64,128]{3,2,1,0:T(8,128)(2,1)S(1)} %bitcast.11), custom_call_target="tpu_custom_call" | custom-call | flops 134217728 | bytes 786432 | tf_op jit(solution)/shard_map/scan_kernel/pallas_call | solution.py:351
  70.2 4.0 %all-to-all-start.2 = ((f32[32,16,128]{2,1,0:T(8,128)}), f32[32,16,128]{2,1,0:T(8,128)S(1)}, u32[]{:S(2)}, u32[]{:S(2)}) async-start(f32[32,16,128]{2,1,0:T(8,128)} %bitcast.6), calls=%async_computation.2 | async-start | bytes 524288 | tf_op jit(solution)/shard_map/all_to_all | solution.py:367
  74.2 3.3 %collective-permute-start.3 = (f32[2,128,128]{2,1,0:T(8,128)S(1)}, f32[2,128,128]{2,1,0:T(8,128)S(1)}, u32[]{:S(2)}, u32[]{:S(2)}) collective-permute-start(f32[2,128,128]{2,1,0:T(8,128)S(1)} %add_kernel.1), channel_id=1, source_target_pairs={{0,32},{16,48},{32,0},{48,16},{64,96},{80,112},{96,64},{112,80},{1... | collective-permute-start | bytes 393224 | tf_op jit(solution)/shard_map/ppermute | solution.py:372
  77.5 4.5 %collective-permute-done.3.chip_carried_ref = f32[2,128,128]{2,1,0:T(8,128)S(1)} collective-permute-done((f32[2,128,128]{2,1,0:T(8,128)S(1)}, f32[2,128,128]{2,1,0:T(8,128)S(1)}, u32[]{:S(2)}, u32[]{:S(2)}) %collective-permute-start.3) | collective-permute-done | bytes 131104 | tf_op jit(solution)/shard_map/ppermute | solution.py:372
  82.0 1.1 %all-to-all-done.2 = f32[32,16,128]{2,1,0:T(8,128)S(1)} async-done(((f32[32,16,128]{2,1,0:T(8,128)}), f32[32,16,128]{2,1,0:T(8,128)S(1)}, u32[]{:S(2)}, u32[]{:S(2)}) %all-to-all-start.2) | async-done | bytes 262176 | tf_op jit(solution)/shard_map/all_to_all | solution.py:367
  83.2 0.0 collective-permute-done.4.other_maps_ref
  83.2 0.0 collective-permute-done.5.other_grad_ref
  83.2 2.3 %output_kernel.1 = (bf16[128,256]{1,0:T(8,128)(2,1)}, bf16[32,8,1024]{2,1,0:T(8,128)(2,1)}) custom-call(s32[2]{0:T(128)S(1)} %pad_add_fusion.flags_ref, f32[16,2,16,128]{3,2,1,0:T(8,128)S(1)} %bitcast.9, f32[4,128,128]{2,1,0:T(8,128)S(1)} %get-tuple-element.35.maps_ref, f32[4,128,128]{2,1,0:T(8,128)S(1)} %collective-permute-done.4.other_maps_ref, ...), custom_call_target="tpu_custom_call" | custom-call | flops 268435456 | bytes 2162696 | tf_op jit(solution)/shard_map/output_kernel/pallas_call | solution.py:351
  85.5 0.0 copy-start.10
  85.5 6.5 %all-to-all-start.3 = ((bf16[32,8,1024]{2,1,0:T(8,128)(2,1)}), bf16[32,8,1024]{2,1,0:T(8,128)(2,1)S(1)}, u32[]{:S(2)}, u32[]{:S(2)}) async-start(bf16[32,8,1024]{2,1,0:T(8,128)(2,1)} %get-tuple-element.54), calls=%async_computation.3 | async-start | bytes 1048576 | tf_op jit(solution)/shard_map/all_to_all | solution.py:367
  92.0 0.0 copy-done.2
  92.0 0.0 copy-done.4
  92.0 0.0 copy-done.6
  92.1 0.0 copy-done.8
  92.1 4.9 %gradient_kernel.1 = (f32[128,128]{1,0:T(8,128)}, f32[128,128]{1,0:T(8,128)}, f32[128,256]{1,0:T(8,128)}) custom-call(s32[2]{0:T(128)S(1)} %pad_add_fusion.flags_ref, bf16[128,128]{1,0:T(8,128)(2,1)S(1)} %copy-done.8, bf16[128,128]{1,0:T(8,128)(2,1)S(1)} %copy-done.10, f32[16,2,16,128]{3,2,1,0:T(8,128)S(1)} %bitcast.10, ...), custom_call_target="tpu_custom_call" | custom-call | flops 536870912 | bytes 2555912 | tf_op jit(solution)/shard_map/gradient_kernel/pallas_call | solution.py:351
  97.0 6.6 %all-to-all-done.3 = bf16[32,8,1024]{2,1,0:T(8,128)(2,1)S(1)} async-done(((bf16[32,8,1024]{2,1,0:T(8,128)(2,1)}), bf16[32,8,1024]{2,1,0:T(8,128)(2,1)S(1)}, u32[]{:S(2)}, u32[]{:S(2)}) %all-to-all-start.3) | async-done | bytes 524320 | tf_op jit(solution)/shard_map/all_to_all | solution.py:367
  103.6 0.7 sum_kernel.1
  (13 shorter events, 0.0 us)
Async XLA Ops:
  2.3 15.9 %copy-start.7 = (bf16[128,128]{1,0:T(8,128)(2,1)S(1)}, bf16[128,128]{1,0:T(8,128)(2,1)}, u32[]{:S(2)}) copy-start(bf16[128,128]{1,0:T(8,128)(2,1)} %q_ref.3) | copy-start | bytes 98308
  2.3 15.9 %copy-start.9 = (bf16[128,128]{1,0:T(8,128)(2,1)S(1)}, bf16[128,128]{1,0:T(8,128)(2,1)}, u32[]{:S(2)}) copy-start(bf16[128,128]{1,0:T(8,128)(2,1)} %k_ref.3) | copy-start | bytes 98308
  2.3 15.9 %copy-start.11 = (bf16[128,256]{1,0:T(8,128)(2,1)S(1)}, bf16[128,256]{1,0:T(8,128)(2,1)}, u32[]{:S(2)}) copy-start(bf16[128,256]{1,0:T(8,128)(2,1)} %v_ref.1) | copy-start | bytes 196612
  2.3 15.9 %copy-start.13 = (s32[128,2]{0,1:T(2,128)S(1)}, s32[128,2]{0,1:T(2,128)}, u32[]{:S(2)}) copy-start(s32[128,2]{0,1:T(2,128)} %param.11) | copy-start | bytes 3076
  2.3 42.6 %all-to-all-start = ((bf16[16,128,128]{2,1,0:T(8,128)(2,1)}), bf16[16,128,128]{2,1,0:T(8,128)(2,1)S(1)}, u32[]{:S(2)}, u32[]{:S(2)}) async-start(bf16[16,128,128]{2,1,0:T(8,128)(2,1)} %broadcast_in_dim.2), calls=%async_computation | async-start | bytes 1048576 | tf_op jit(solution)/shard_map/all_to_all | solution.py:367
  18.2 0.7 copy-start.12
  26.6 0.7 copy-start.1
  27.2 0.7 copy-start.3
  27.9 0.6 copy-start.5
  28.5 16.4 %copy-start = (bf16[256,2048]{1,0:T(8,128)(2,1)S(1)}, bf16[256,2048]{1,0:T(8,128)(2,1)}, u32[]{:S(2)}) copy-start(bf16[256,2048]{1,0:T(8,128)(2,1)} %w_ref.1) | copy-start | bytes 3145732
  28.5 4.1 %collective-permute-start = (f32[4,128,128]{2,1,0:T(8,128)S(1)}, f32[4,128,128]{2,1,0:T(8,128)S(1)}, u32[]{:S(2)}, u32[]{:S(2)}) collective-permute-start(f32[4,128,128]{2,1,0:T(8,128)S(1)} %get-tuple-element.30.own_ref), channel_id=1, source_target_pairs={{0,16},{16,0},{32,48},{48,32},{64,80},{80,64},{96,112},{112,96},{1... | collective-permute-start | bytes 786440 | tf_op jit(solution)/shard_map/ppermute | solution.py:372
  34.1 9.4 %collective-permute-start.1 = (f32[4,128,128]{2,1,0:T(8,128)S(1)}, f32[4,128,128]{2,1,0:T(8,128)S(1)}, u32[]{:S(2)}, u32[]{:S(2)}) collective-permute-start(f32[4,128,128]{2,1,0:T(8,128)S(1)} %get-tuple-element.33.own_ref), channel_id=1, source_target_pairs={{0,32},{16,48},{32,0},{48,16},{64,96},{80,112},{96,64},{112,80},{1... | collective-permute-start | bytes 786440 | tf_op jit(solution)/shard_map/ppermute | solution.py:372
  46.7 21.9 %all-to-all-start.1 = ((bf16[32,64,128]{2,1,0:T(8,128)(2,1)}), bf16[32,64,128]{2,1,0:T(8,128)(2,1)S(1)}, u32[]{:S(2)}, u32[]{:S(2)}) async-start(bf16[32,64,128]{2,1,0:T(8,128)(2,1)} %bitcast.4), calls=%async_computation.1 | async-start | bytes 1048576 | tf_op jit(solution)/shard_map/all_to_all | solution.py:367
  57.5 7.8 %collective-permute-start.2 = (f32[4,128,128]{2,1,0:T(8,128)S(1)}, f32[4,128,128]{2,1,0:T(8,128)S(1)}, u32[]{:S(2)}, u32[]{:S(2)}) collective-permute-start(f32[4,128,128]{2,1,0:T(8,128)S(1)} %carried_kernel.1.own_ref), channel_id=1, source_target_pairs={{0,16},{16,0},{32,48},{48,32},{64,80},{80,64},{96,112},{112,96},{1... | collective-permute-start | bytes 786440 | tf_op jit(solution)/shard_map/ppermute | solution.py:372
  59.6 23.5 %collective-permute-start.4 = (f32[4,128,128]{2,1,0:T(8,128)S(1)}, f32[4,128,128]{2,1,0:T(8,128)S(1)}, u32[]{:S(2)}, u32[]{:S(2)}) collective-permute-start(f32[4,128,128]{2,1,0:T(8,128)S(1)} %get-tuple-element.35.maps_ref), channel_id=1, source_target_pairs={{0,16},{16,0},{32,48},{48,32},{64,80},{80,64},{96,112},{112,96},{1... | collective-permute-start | bytes 786440 | tf_op jit(solution)/shard_map/ppermute | solution.py:372
  63.1 20.1 %collective-permute-start.5 = (bf16[8,128,128]{2,1,0:T(8,128)(2,1)}, bf16[8,128,128]{2,1,0:T(8,128)(2,1)S(1)}, u32[]{:S(2)}, u32[]{:S(2)}) collective-permute-start(bf16[8,128,128]{2,1,0:T(8,128)(2,1)} %half_kernel.1), channel_id=1, source_target_pairs={{0,16},{16,0},{32,48},{48,32},{64,80},{80,64},{96,112},{112,96},{1... | collective-permute-start | bytes 786440 | tf_op jit(solution)/shard_map/ppermute | solution.py:372
  70.2 13.0 %all-to-all-start.2 = ((f32[32,16,128]{2,1,0:T(8,128)}), f32[32,16,128]{2,1,0:T(8,128)S(1)}, u32[]{:S(2)}, u32[]{:S(2)}) async-start(f32[32,16,128]{2,1,0:T(8,128)} %bitcast.6), calls=%async_computation.2 | async-start | bytes 524288 | tf_op jit(solution)/shard_map/all_to_all | solution.py:367
  74.2 7.8 %collective-permute-start.3 = (f32[2,128,128]{2,1,0:T(8,128)S(1)}, f32[2,128,128]{2,1,0:T(8,128)S(1)}, u32[]{:S(2)}, u32[]{:S(2)}) collective-permute-start(f32[2,128,128]{2,1,0:T(8,128)S(1)} %add_kernel.1), channel_id=1, source_target_pairs={{0,32},{16,48},{32,0},{48,16},{64,96},{80,112},{96,64},{112,80},{1... | collective-permute-start | bytes 393224 | tf_op jit(solution)/shard_map/ppermute | solution.py:372
  85.5 6.6 %copy-start.2 = (f32[2,128,128]{2,1,0:T(8,128)S(1)}, f32[2,128,128]{2,1,0:T(8,128)}, u32[]{:S(2)}) copy-start(f32[2,128,128]{2,1,0:T(8,128)} %copy-done.1) | copy-start | bytes 393220
  85.5 6.6 %copy-start.4 = (f32[2,128,128]{2,1,0:T(8,128)S(1)}, f32[2,128,128]{2,1,0:T(8,128)}, u32[]{:S(2)}) copy-start(f32[2,128,128]{2,1,0:T(8,128)} %copy-done.3) | copy-start | bytes 393220
  85.5 6.6 %copy-start.6 = (f32[2,128,128]{2,1,0:T(8,128)S(1)}, f32[2,128,128]{2,1,0:T(8,128)}, u32[]{:S(2)}) copy-start(f32[2,128,128]{2,1,0:T(8,128)} %copy-done.5) | copy-start | bytes 393220
  85.5 6.6 %copy-start.8 = (bf16[128,128]{1,0:T(8,128)(2,1)S(1)}, bf16[128,128]{1,0:T(8,128)(2,1)}, u32[]{:S(2)}) copy-start(bf16[128,128]{1,0:T(8,128)(2,1)} %q_ref.3) | copy-start | bytes 98308
  85.5 6.6 %copy-start.10 = (bf16[128,128]{1,0:T(8,128)(2,1)S(1)}, bf16[128,128]{1,0:T(8,128)(2,1)}, u32[]{:S(2)}) copy-start(bf16[128,128]{1,0:T(8,128)(2,1)} %k_ref.3) | copy-start | bytes 98308
  85.5 18.1 %all-to-all-start.3 = ((bf16[32,8,1024]{2,1,0:T(8,128)(2,1)}), bf16[32,8,1024]{2,1,0:T(8,128)(2,1)S(1)}, u32[]{:S(2)}, u32[]{:S(2)}) async-start(bf16[32,8,1024]{2,1,0:T(8,128)(2,1)} %get-tuple-element.54), calls=%async_computation.3 | async-start | bytes 1048576 | tf_op jit(solution)/shard_map/all_to_all | solution.py:367

commit v5 on v4

--- a/solution.py
+++ b/solution.py
@@ -136,9 +136,9 @@
 
 
 def quad_kernel(
-    flags_ref, own_ref, other_ref, chip_maps_ref, trans_ref, state_ref, diag_ref, maps_ref
-):
-    group = trans_ref.shape[0]
+    flags_ref, own_ref, other_ref, chip_maps_ref, maps_ref
+):
+    group = chip_maps_ref.shape[0] // 2
     core = flags_ref[0] == 1
     late = flags_ref[1] == 1
     rows, cols = ids(WIDTH)
@@ -147,28 +147,29 @@
         transition, state_t = compose_heads(late, own_ref, other_ref, head, group)
         rounded = transition.astype(BF16)
         rest = jnp.where(rows == cols, transition - rounded.astype(F32), 0.0)
-        diag_ref[head] = jnp.broadcast_to(
-            jnp.sum(rest, axis=0, keepdims=True), (diag_ref.shape[1], WIDTH)
-        ).astype(BF16)
+        maps_ref[3 * group + head, share : 2 * share] = jnp.broadcast_to(
+            jnp.sum(rest, axis=0, keepdims=True), (share, WIDTH)
+        )
         quarters = [transition[at * share : (at + 1) * share] for at in range(4)]
-        trans_ref[head] = jnp.where(
+        maps_ref[3 * group + head, :share] = jnp.where(
             late,
             jnp.where(core, quarters[3], quarters[2]),
             jnp.where(core, quarters[1], quarters[0]),
-        ).astype(BF16)
+        )
         high = state_t.astype(BF16).astype(F32)
         part = jnp.where(core, state_t - high, high)
-        state_ref[head] = jnp.where(late, 0.0, part).astype(BF16)
+        maps_ref[2 * group + head] = jnp.where(late, 0.0, part)
         maps_ref[head], maps_ref[group + head] = compose_maps(
             late, other_ref, head, group, chip_maps_ref[head], chip_maps_ref[group + head]
         )
 
 
 def cotangent_kernel(
-    grad_ref, w_ref, maps_ref, trans_ref, state_ref, diag_ref, cot_ref, send_ref
+    grad_ref, w_ref, maps_ref, cot_ref, send_ref
 ):
     blocks = grad_ref.shape[0]
-    group, share, _ = trans_ref.shape
+    group = send_ref.shape[1]
+    share = WIDTH // 4
     total = jnp.zeros(cot_ref.shape, F32)
     for block in range(0, blocks, 2):
         left = jnp.concatenate([grad_ref[block], grad_ref[block + 1]], axis=1)
@@ -180,9 +181,9 @@
         carried_t = mm(total[:, head * WIDTH : (head + 1) * WIDTH], maps_ref[head], 0, 0)
         high = carried_t.astype(BF16).astype(F32)
         low = carried_t - high
-        state = state_ref[head].astype(F32)
-        diag = diag_ref[head].astype(F32)
-        trans = trans_ref[head]
+        state = maps_ref[2 * group + head]
+        diag = maps_ref[3 * group + head, share : share + part, :]
+        trans = maps_ref[3 * group + head, :share, :].astype(BF16)
         for chip in range(chips):
             mine = slice(chip * part, (chip + 1) * part)
             send_ref[chip, head, :share, :] = trans
@@ -232,7 +233,7 @@
 def output_kernel(
     flags_ref, got_ref, maps_ref, other_maps_ref, grad_ref, other_grad_ref, attn_ref, send_ref
 ):
-    group = maps_ref.shape[0] // 2
+    group = maps_ref.shape[0] // 4
     dests, part, _ = send_ref.shape
     blocks = other_grad_ref.shape[0]
     first = flags_ref[0] * blocks
@@ -273,21 +274,19 @@
     half_ref[...] = grad_ref[pl.ds((1 - flags_ref[0]) * blocks, blocks)]
 
 
-def carried_kernel(cot_ref, probe_ref, chip_maps_ref, carried_ref):
+def sibling_kernel(
+    maps_ref, cot_ref, probe_ref, chip_maps_ref, pack_ref, term_ref
+):
     group = probe_ref.shape[0]
+    pack_ref[: 2 * group] = maps_ref[: 2 * group]
     for head in range(group):
         cot = cot_ref[:, head * WIDTH : (head + 1) * WIDTH]
-        carried_ref[head] = mm(cot, probe_ref[head], 0, 0)
-        carried_ref[group + head] = mm(cot, chip_maps_ref[head], 0, 0)
-
-
-def add_kernel(own_ref, other_ref, total_ref):
-    group = total_ref.shape[0]
-    total_ref[...] = own_ref[group:] + other_ref[group:]
+        pack_ref[2 * group + head] = mm(cot, probe_ref[head], 0, 0)
+        term_ref[head] = mm(cot, chip_maps_ref[head], 0, 0)
 
 
 def gradient_kernel(
-    flags_ref, q_ref, k_ref, got_ref, other_ref, other_chip_ref, carried_ref, chip_carried_ref,
+    flags_ref, q_ref, k_ref, got_ref, other_ref, other_chip_ref, other_pack_ref, near_ref, far_ref,
     cot_ref, tmat_ref, mix_ref, ratio_ref, uw_ref, cols_ref, q_grad_ref, k_grad_ref, v_grad_ref,
 ):
     length = q_ref.shape[0]
@@ -308,8 +307,8 @@
         state_t = gather_rows(got_ref, head, 0)
         end_t = gather_rows(got_ref, head, 1)
         for after, other, term, carried in (
-            (late, other_chip_ref[head], other_chip_ref[group + head], chip_carried_ref[head]),
-            (core, other_ref[head], other_ref[group + head], carried_ref[head]),
+            (late, other_chip_ref[head], other_chip_ref[group + head], near_ref[head] + far_ref[head]),
+            (core, other_ref[head], other_ref[group + head], other_pack_ref[2 * group + head]),
         ):
             through_state = mm(state_t, other, 1, 1) + term
             through_end = mm(end_t, other) + carried
@@ -408,58 +407,54 @@
         flags, pair, other, probe, local,
     )
     other_chip = across(chip, 2)
-    trans, state, diag, maps = call(
+    (maps,) = call(
         quad_kernel,
-        [
-            shape((group, WIDTH // 4, WIDTH), BF16),
-            shape((group, WIDTH, WIDTH), BF16),
-            shape((group, part, WIDTH), BF16),
-            shape((2 * group, length, WIDTH)),
-        ],
+        [shape((4 * group, WIDTH, WIDTH))],
         1 << 28,
         flags, chip, other_chip, chip_maps,
     )
-    other_maps = across(maps, 1)
     cot, send = call(
         cotangent_kernel,
         [shape(flat), shape((chips, group, WIDTH // 4 + 4 * part, WIDTH), BF16)],
         1 << 28,
-        full_grad, w_out, maps, trans, state, diag,
+        full_grad, w_out, maps,
     )
     got = swap(send.reshape((slabs,) + send.shape[2:]), "seq")
-    (half,) = call(
-        half_kernel, [shape((heads // 2, length, WIDTH), BF16)], 1 << 20, flags, full_grad
-    )
-    other_half = across(half, 1)
-    (own_carried,) = call(
-        carried_kernel, [shape(states_shape)], 1 << 26, cot, probe, chip_maps
-    )
-    carried = across(own_carried, 1)
-    got, carried = lax.optimization_barrier((got, carried))
+    pack, term = call(
+        sibling_kernel,
+        [shape((3 * group, length, WIDTH)), shape(square)],
+        1 << 26,
+        maps, cot, probe, chip_maps,
+    )
+    near_term = across(term, 2)
+    other_pack = across(pack, 1)
     (back,) = call(
         scan_kernel,
         [shape((slabs // 4, 4, 2 * part, WIDTH))],
         1 << 27,
         got.reshape((slabs // 4, 4) + got.shape[1:]),
     )
+    back, near_term = lax.optimization_barrier((back, near_term))
+    far_term = across(near_term, 1)
+    (half,) = call(
+        half_kernel, [shape((heads // 2, length, WIDTH), BF16)], 1 << 20, flags, full_grad
+    )
+    other_half = across(half, 1)
     states = swap(back.reshape(slabs, 2 * part, WIDTH), "seq").reshape(
         chips, group, 2 * part, WIDTH
     )
-    (chip_carried,) = call(add_kernel, [shape(square)], 1 << 20, own_carried, carried)
-    chip_carried = across(chip_carried, 2)
-    states, chip_carried = lax.optimization_barrier((states, chip_carried))
     attn_out, grad_send = call(
         output_kernel,
         [shape(flat, BF16), shape((slabs, part, heads // 2 * WIDTH), BF16)],
         1 << 28,
-        flags, states, maps, other_maps, full_grad, other_half,
+        flags, states, maps, other_pack, full_grad, other_half,
     )
     grad_got = swap(grad_send, "seq")
     q_grad, k_grad, v_grad = call(
         gradient_kernel,
         [shape((length, WIDTH)), shape((length, WIDTH)), shape(flat)],
         1 << 29,
-        flags, queries, keys, states, other, other_chip, carried, chip_carried, cot, tmat, mix, ratio, uw, columns,
+        flags, queries, keys, states, other, other_chip, other_pack, near_term, far_term, cot, tmat, mix, ratio, uw, columns,
     )
     scaling = (length * slabs) ** (-0.5)
     (weight_grad,) = call(

time: 105 us -> 104 us (level)
    ppermute x6, waiting for transfers between devices: 11.9 us -> 8.14 us  [across(): lax.ppermute(value, 'seq', [(slab, slab ^ step) for slab in range(slabs)])]
    all_to_all x4, waiting for transfers between devices: 11.1 us -> 14.2 us  [swap(): return lax.all_to_all(value, axis, 0, 0, tiled=True)]
    all_to_all x4, starting transfers between devices: 36.8 us -> 35.7 us  [swap(): return lax.all_to_all(value, axis, 0, 0, tiled=True)]
    pallas_call x11 -> x10, Pallas kernels: 23.5 us -> 23.5 us  [call(): pl.pallas_call(kernel, out_shape=outs, in_specs=[smem if scalar else vmem...]
    unnamed x28 -> x32, local copies, waits for them, and re-layouts: 2.62 us -> 2.64 us
where the time goes in v5:
time: 104 us; the launch traced here: 103 us
  starting transfers between devices  52 us (50%)
  Pallas kernels  23.5 us (23%)
  waiting for transfers between devices  22.4 us (22%)
  local copies, waits for them, and re-layouts  4.28 us (4%)
    all_to_all x4, starting transfers between devices, swap(): return lax.all_to_all(value, axis, 0, 0, tiled=True)  35.7 us
    pallas_call x10, Pallas kernels, call(): pl.pallas_call(kernel, out_shape=outs, in_specs=[smem if scalar else vmem...  23.5 us
    ppermute x6, starting transfers between devices, across(): lax.ppermute(value, 'seq', [(slab, slab ^ step) for slab in range(slabs)])  16.3 us
    all_to_all x4, waiting for transfers between devices, swap(): return lax.all_to_all(value, axis, 0, 0, tiled=True)  14.2 us
    ppermute x6, waiting for transfers between devices, across(): lax.ppermute(value, 'seq', [(slab, slab ^ step) for slab in range(slabs)])  8.14 us
    unnamed x32, local copies, waits for them, and re-layouts  2.64 us
  transfers between devices with their start and end apart: 10, of which 6 were waited for; matrix products, arithmetic and copies ran while one was open for 0% of the time, Pallas kernels for 18%

profile of v5, /device:TPU:1, one launch (start us, length us, event | category | flops | bytes accessed | tf_op | source)
XLA Modules:
  0.0 103.1 jit_solution(8800768806885236580)
XLA Ops:
  0.6 1.6 %broadcast_in_dim.2 = bf16[16,128,128]{2,1,0:T(8,128)(2,1)} broadcast(bf16[128,128]{1,0:T(8,128)(2,1)} %param.12), dimensions={1,2} | broadcast | bytes 557056 | tf_op jit(solution)/shard_map/broadcast_in_dim | solution.py:386
  2.3 15.9 %all-to-all-start = ((bf16[16,128,128]{2,1,0:T(8,128)(2,1)}), bf16[16,128,128]{2,1,0:T(8,128)(2,1)S(1)}, u32[]{:S(2)}, u32[]{:S(2)}) async-start(bf16[16,128,128]{2,1,0:T(8,128)(2,1)} %broadcast_in_dim.2), calls=%async_computation | async-start | bytes 1048576 | tf_op jit(solution)/shard_map/all_to_all | solution.py:366
  18.2 0.0 copy-start.14
  18.2 0.0 copy-done.9
  18.2 0.0 copy-done.11
  18.2 0.0 copy-done.13
  18.2 0.0 copy-done.15
  18.2 0.6 copy-done.14
  18.9 7.7 %prepare_kernel.1 = (f32[4,128,128]{2,1,0:T(8,128)S(1)}, f32[2,128,128]{2,1,0:T(8,128)S(1)}, f32[2,128,128]{2,1,0:T(8,128)S(1)}, f32[2,128,128]{2,1,0:T(8,128)S(...) custom-call(bf16[128,128]{1,0:T(8,128)(2,1)S(1)} %copy-done.9, ...), custom_call_target="tpu_custom_call" | custom-call | flops 1073741824 | bytes 1574912 | tf_op jit(solution)/shard_map/prepare_kernel/pallas_call | solution.py:350
  26.6 0.0 copy-start.3
  26.6 0.7 copy-done.3
  27.2 0.6 copy-done.5
  27.9 0.6 copy-done.7
  28.5 2.8 %collective-permute-start = (f32[4,128,128]{2,1,0:T(8,128)S(1)}, f32[4,128,128]{2,1,0:T(8,128)S(1)}, u32[]{:S(2)}, u32[]{:S(2)}) collective-permute-start(f32[4,128,128]{2,1,0:T(8,128)S(1)} %get-tuple-element.26.own_ref), channel_id=1, source_target_pairs={{0,16},{16,0},{32,48},{48,32},{64,80},{80,64},{96,112},{112,96},{1... | collective-permute-start | bytes 786440 | tf_op jit(solution)/shard_map/ppermute | solution.py:371
  31.4 0.1 pad_add_fusion.flags_ref
  31.5 1.1 %collective-permute-done.other_ref = f32[4,128,128]{2,1,0:T(8,128)S(1)} collective-permute-done((f32[4,128,128]{2,1,0:T(8,128)S(1)}, f32[4,128,128]{2,1,0:T(8,128)S(1)}, u32[]{:S(2)}, u32[]{:S(2)}) %collective-permute-start) | collective-permute-done | bytes 262176 | tf_op jit(solution)/shard_map/ppermute | solution.py:371
  32.5 1.4 %chip_kernel.1 = (f32[4,128,128]{2,1,0:T(8,128)S(1)}, f32[4,128,128]{2,1,0:T(8,128)S(1)}) custom-call(s32[2]{0:T(128)S(1)} %pad_add_fusion.flags_ref, f32[4,128,128]{2,1,0:T(8,128)S(1)} %get-tuple-element.26.own_ref, f32[4,128,128]{2,1,0:T(8,128)S(1)} %collective-permute-done.other_ref, f32[2,128,128]{2,1,0:T(8,128)S(1)} %get-tuple-element.27.probe_ref, ...), custom_call_target="tpu_custom_call" | custom-call | flops 268435456 | bytes 1310728 | tf_op jit(solution)/shard_map/chip_kernel/pallas_call | solution.py:350
  33.9 0.0 copy-done.1
  34.0 3.1 %collective-permute-start.1 = (f32[4,128,128]{2,1,0:T(8,128)S(1)}, f32[4,128,128]{2,1,0:T(8,128)S(1)}, u32[]{:S(2)}, u32[]{:S(2)}) collective-permute-start(f32[4,128,128]{2,1,0:T(8,128)S(1)} %get-tuple-element.29.own_ref), channel_id=1, source_target_pairs={{0,32},{16,48},{32,0},{48,16},{64,96},{80,112},{96,64},{112,80},{1... | collective-permute-start | bytes 786440 | tf_op jit(solution)/shard_map/ppermute | solution.py:371
  37.1 6.3 %collective-permute-done.1.other_ref.other_chip_ref = f32[4,128,128]{2,1,0:T(8,128)S(1)} collective-permute-done((f32[4,128,128]{2,1,0:T(8,128)S(1)}, f32[4,128,128]{2,1,0:T(8,128)S(1)}, u32[]{:S(2)}, u32[]{:S(2)}) %collective-permute-start.1) | collective-permute-done | bytes 262176 | tf_op jit(solution)/shard_map/ppermute | solution.py:371
  43.4 1.4 %quad_kernel.1.maps_ref = f32[8,128,128]{2,1,0:T(8,128)S(1)} custom-call(s32[2]{0:T(128)S(1)} %pad_add_fusion.flags_ref, f32[4,128,128]{2,1,0:T(8,128)S(1)} %get-tuple-element.29.own_ref, f32[4,128,128]{2,1,0:T(8,128)S(1)} %collective-permute-done.1.other_ref.other_chip_ref, f32[4,128,128]{2,1,0:T(8,128)S(1)} %get-tuple-element.30.chip_maps_ref), custom_call_target="tpu_custom_call" | custom-call | flops 268435456 | bytes 1310728 | tf_op jit(solution)/shard_map/quad_kernel/pallas_call | solution.py:350
  44.8 0.0 all-to-all-done.grad_ref
  44.8 0.0 copy-done
  44.8 1.7 %cotangent_kernel.1 = (f32[128,256]{1,0:T(8,128)S(1)}, bf16[16,2,64,128]{3,2,1,0:T(8,128)(2,1)}) custom-call(bf16[16,128,128]{2,1,0:T(8,128)(2,1)S(1)} %all-to-all-done.grad_ref, bf16[256,2048]{1,0:T(8,128)(2,1)S(1)} %copy-done, f32[8,128,128]{2,1,0:T(8,128)S(1)} %quad_kernel.1.maps_ref), custom_call_target="tpu_custom_call" | custom-call | flops 268435456 | bytes 2752512 | tf_op jit(solution)/shard_map/cotangent_kernel/pallas_call | solution.py:350
  46.5 10.5 %all-to-all-start.1 = ((bf16[32,64,128]{2,1,0:T(8,128)(2,1)}), bf16[32,64,128]{2,1,0:T(8,128)(2,1)S(1)}, u32[]{:S(2)}, u32[]{:S(2)}) async-start(bf16[32,64,128]{2,1,0:T(8,128)(2,1)} %bitcast.4), calls=%async_computation.1 | async-start | bytes 1048576 | tf_op jit(solution)/shard_map/all_to_all | solution.py:366
  57.0 1.2 %sibling_kernel.1 = (f32[6,128,128]{2,1,0:T(8,128)}, f32[2,128,128]{2,1,0:T(8,128)}) custom-call(f32[8,128,128]{2,1,0:T(8,128)S(1)} %quad_kernel.1.maps_ref, f32[128,256]{1,0:T(8,128)S(1)} %get-tuple-element.32.cot_ref, f32[2,128,128]{2,1,0:T(8,128)S(1)} %get-tuple-element.27.probe_ref, f32[4,128,128]{2,1,0:T(8,128)S(1)} %get-tuple-element.30.chip_maps_ref), custom_call_target="tpu_custom_call" | custom-call | flops 67108864 | bytes 1572864 | tf_op jit(solution)/shard_map/sibling_kernel/pallas_call | solution.py:350
  58.3 2.1 %collective-permute-start.3 = (f32[6,128,128]{2,1,0:T(8,128)}, f32[6,128,128]{2,1,0:T(8,128)S(1)}, u32[]{:S(2)}, u32[]{:S(2)}) collective-permute-start(f32[6,128,128]{2,1,0:T(8,128)} %get-tuple-element.35), channel_id=1, source_target_pairs={{0,16},{16,0},{32,48},{48,32},{64,80},{80,64},{96,112},{112,96},{1... | collective-permute-start | bytes 1179656 | tf_op jit(solution)/shard_map/ppermute | solution.py:371
  60.4 3.4 %collective-permute-start.2 = (f32[2,128,128]{2,1,0:T(8,128)}, f32[2,128,128]{2,1,0:T(8,128)S(1)}, u32[]{:S(2)}, u32[]{:S(2)}) collective-permute-start(f32[2,128,128]{2,1,0:T(8,128)} %get-tuple-element.33), channel_id=1, source_target_pairs={{0,32},{16,48},{32,0},{48,16},{64,96},{80,112},{96,64},{112,80},{1... | collective-permute-start | bytes 393224 | tf_op jit(solution)/shard_map/ppermute | solution.py:371
  63.8 0.6 half_kernel.1
  64.4 2.4 %collective-permute-start.4 = (bf16[8,128,128]{2,1,0:T(8,128)(2,1)S(1)}, bf16[8,128,128]{2,1,0:T(8,128)(2,1)S(1)}, u32[]{:S(2)}, u32[]{:S(2)}) collective-permute-start(bf16[8,128,128]{2,1,0:T(8,128)(2,1)S(1)} %half_kernel.1), channel_id=1, source_target_pairs={{0,16},{16,0},{32,48},{48,32},{64,80},{80,64},{96,112},{112,96},{1... | collective-permute-start | bytes 786440 | tf_op jit(solution)/shard_map/ppermute | solution.py:371
  66.8 1.8 %all-to-all-done.1 = bf16[32,64,128]{2,1,0:T(8,128)(2,1)S(1)} async-done(((bf16[32,64,128]{2,1,0:T(8,128)(2,1)}), bf16[32,64,128]{2,1,0:T(8,128)(2,1)S(1)}, u32[]{:S(2)}, u32[]{:S(2)}) %all-to-all-start.1) | async-done | bytes 524320 | tf_op jit(solution)/shard_map/all_to_all | solution.py:366
  68.6 1.6 %scan_kernel.1 = f32[8,4,16,128]{3,2,1,0:T(8,128)} custom-call(bf16[8,4,64,128]{3,2,1,0:T(8,128)(2,1)S(1)} %bitcast.12), custom_call_target="tpu_custom_call" | custom-call | flops 134217728 | bytes 786432 | tf_op jit(solution)/shard_map/scan_kernel/pallas_call | solution.py:350
  70.2 0.0 collective-permute-done.2.near_ref
  70.2 5.4 %all-to-all-start.2 = ((f32[32,16,128]{2,1,0:T(8,128)}), f32[32,16,128]{2,1,0:T(8,128)S(1)}, u32[]{:S(2)}, u32[]{:S(2)}) async-start(f32[32,16,128]{2,1,0:T(8,128)} %bitcast.6), calls=%async_computation.2 | async-start | bytes 524288 | tf_op jit(solution)/shard_map/all_to_all | solution.py:366
  75.6 0.0 collective-permute-done.4.other_grad_ref
  75.6 0.0 collective-permute-done.3.other_maps_ref.other_pack_ref
  75.6 8.9 %all-to-all-done.2 = f32[32,16,128]{2,1,0:T(8,128)S(1)} async-done(((f32[32,16,128]{2,1,0:T(8,128)}), f32[32,16,128]{2,1,0:T(8,128)S(1)}, u32[]{:S(2)}, u32[]{:S(2)}) %all-to-all-start.2) | async-done | bytes 262176 | tf_op jit(solution)/shard_map/all_to_all | solution.py:366
  84.5 2.3 %output_kernel.1 = (bf16[128,256]{1,0:T(8,128)(2,1)}, bf16[32,8,1024]{2,1,0:T(8,128)(2,1)}) custom-call(s32[2]{0:T(128)S(1)} %pad_add_fusion.flags_ref, f32[16,2,16,128]{3,2,1,0:T(8,128)S(1)} %bitcast.9, f32[8,128,128]{2,1,0:T(8,128)S(1)} %quad_kernel.1.maps_ref, f32[6,128,128]{2,1,0:T(8,128)S(1)} %collective-permute-done.3.other_maps_ref.other_pack_ref, ...), custom_call_target="tpu_custom_call" | custom-call | flops 268435456 | bytes 2555912 | tf_op jit(solution)/shard_map/output_kernel/pallas_call | solution.py:350
  86.8 0.0 copy-start.10
  86.8 0.0 copy-start.12
  86.8 3.9 %all-to-all-start.3 = ((bf16[32,8,1024]{2,1,0:T(8,128)(2,1)}), bf16[32,8,1024]{2,1,0:T(8,128)(2,1)S(1)}, u32[]{:S(2)}, u32[]{:S(2)}) async-start(bf16[32,8,1024]{2,1,0:T(8,128)(2,1)} %get-tuple-element.46), calls=%async_computation.3 | async-start | bytes 1048576 | tf_op jit(solution)/shard_map/all_to_all | solution.py:366
  90.7 2.4 %collective-permute-start.5 = (f32[2,128,128]{2,1,0:T(8,128)S(1)}, f32[2,128,128]{2,1,0:T(8,128)S(1)}, u32[]{:S(2)}, u32[]{:S(2)}) collective-permute-start(f32[2,128,128]{2,1,0:T(8,128)S(1)} %collective-permute-done.2.near_ref), channel_id=1, source_target_pairs={{0,16},{16,0},{32,48},{48,32},{64,80},{80,64},{96,112},{112,96},{1... | collective-permute-start | bytes 393224 | tf_op jit(solution)/shard_map/ppermute | solution.py:371
  93.1 0.8 collective-permute-done.5.far_ref
  93.9 0.0 copy-done.2
  94.0 0.0 copy-done.6
  94.0 4.9 %gradient_kernel.1 = (f32[128,128]{1,0:T(8,128)}, f32[128,128]{1,0:T(8,128)}, f32[128,256]{1,0:T(8,128)}) custom-call(s32[2]{0:T(128)S(1)} %pad_add_fusion.flags_ref, bf16[128,128]{1,0:T(8,128)(2,1)S(1)} %copy-done.10, bf16[128,128]{1,0:T(8,128)(2,1)S(1)} %copy-done.12, f32[16,2,16,128]{3,2,1,0:T(8,128)S(1)} %bitcast.10, f32[4,128,128]{2,1,0:T(8,128)S(1)} %copy-done.2, ...), custom_call_target="tpu_custom_call" | custom-call | flops 536870912 | bytes 2818056 | tf_op jit(solution)/shard_map/gradient_kernel/pallas_call | solution.py:350
  98.9 3.5 %all-to-all-done.3 = bf16[32,8,1024]{2,1,0:T(8,128)(2,1)S(1)} async-done(((bf16[32,8,1024]{2,1,0:T(8,128)(2,1)}), bf16[32,8,1024]{2,1,0:T(8,128)(2,1)S(1)}, u32[]{:S(2)}, u32[]{:S(2)}) %all-to-all-start.3) | async-done | bytes 524320 | tf_op jit(solution)/shard_map/all_to_all | solution.py:366
  102.4 0.7 sum_kernel.1
  (16 shorter events, 0.0 us)
Async XLA Ops:
  2.3 15.9 %copy-start.9 = (bf16[128,128]{1,0:T(8,128)(2,1)S(1)}, bf16[128,128]{1,0:T(8,128)(2,1)}, u32[]{:S(2)}) copy-start(bf16[128,128]{1,0:T(8,128)(2,1)} %q_ref.3) | copy-start | bytes 98308
  2.3 15.9 %copy-start.11 = (bf16[128,128]{1,0:T(8,128)(2,1)S(1)}, bf16[128,128]{1,0:T(8,128)(2,1)}, u32[]{:S(2)}) copy-start(bf16[128,128]{1,0:T(8,128)(2,1)} %k_ref.3) | copy-start | bytes 98308
  2.3 15.9 %copy-start.13 = (bf16[128,256]{1,0:T(8,128)(2,1)S(1)}, bf16[128,256]{1,0:T(8,128)(2,1)}, u32[]{:S(2)}) copy-start(bf16[128,256]{1,0:T(8,128)(2,1)} %v_ref.1) | copy-start | bytes 196612
  2.3 15.9 %copy-start.15 = (s32[128,2]{0,1:T(2,128)S(1)}, s32[128,2]{0,1:T(2,128)}, u32[]{:S(2)}) copy-start(s32[128,2]{0,1:T(2,128)} %param.11) | copy-start | bytes 3076
  2.3 42.5 %all-to-all-start = ((bf16[16,128,128]{2,1,0:T(8,128)(2,1)}), bf16[16,128,128]{2,1,0:T(8,128)(2,1)S(1)}, u32[]{:S(2)}, u32[]{:S(2)}) async-start(bf16[16,128,128]{2,1,0:T(8,128)(2,1)} %broadcast_in_dim.2), calls=%async_computation | async-start | bytes 1048576 | tf_op jit(solution)/shard_map/all_to_all | solution.py:366
  18.2 0.7 copy-start.14
  26.6 0.7 copy-start.3
  27.2 0.6 copy-start.5
  27.9 0.7 copy-start.7
  28.5 4.0 %collective-permute-start = (f32[4,128,128]{2,1,0:T(8,128)S(1)}, f32[4,128,128]{2,1,0:T(8,128)S(1)}, u32[]{:S(2)}, u32[]{:S(2)}) collective-permute-start(f32[4,128,128]{2,1,0:T(8,128)S(1)} %get-tuple-element.26.own_ref), channel_id=1, source_target_pairs={{0,16},{16,0},{32,48},{48,32},{64,80},{80,64},{96,112},{112,96},{1... | collective-permute-start | bytes 786440 | tf_op jit(solution)/shard_map/ppermute | solution.py:371
  32.5 1.4 %copy-start.1 = (f32[4,128,128]{2,1,0:T(8,128)}, f32[4,128,128]{2,1,0:T(8,128)S(1)}, u32[]{:S(2)}) copy-start(f32[4,128,128]{2,1,0:T(8,128)S(1)} %collective-permute-done.other_ref) | copy-start | bytes 786436
  32.5 12.3 %copy-start = (bf16[256,2048]{1,0:T(8,128)(2,1)S(1)}, bf16[256,2048]{1,0:T(8,128)(2,1)}, u32[]{:S(2)}) copy-start(bf16[256,2048]{1,0:T(8,128)(2,1)} %w_ref.1) | copy-start | bytes 3145732
  34.0 9.4 %collective-permute-start.1 = (f32[4,128,128]{2,1,0:T(8,128)S(1)}, f32[4,128,128]{2,1,0:T(8,128)S(1)}, u32[]{:S(2)}, u32[]{:S(2)}) collective-permute-start(f32[4,128,128]{2,1,0:T(8,128)S(1)} %get-tuple-element.29.own_ref), channel_id=1, source_target_pairs={{0,32},{16,48},{32,0},{48,16},{64,96},{80,112},{96,64},{112,80},{1... | collective-permute-start | bytes 786440 | tf_op jit(solution)/shard_map/ppermute | solution.py:371
  46.5 22.1 %all-to-all-start.1 = ((bf16[32,64,128]{2,1,0:T(8,128)(2,1)}), bf16[32,64,128]{2,1,0:T(8,128)(2,1)S(1)}, u32[]{:S(2)}, u32[]{:S(2)}) async-start(bf16[32,64,128]{2,1,0:T(8,128)(2,1)} %bitcast.4), calls=%async_computation.1 | async-start | bytes 1048576 | tf_op jit(solution)/shard_map/all_to_all | solution.py:366
  58.3 17.3 %collective-permute-start.3 = (f32[6,128,128]{2,1,0:T(8,128)}, f32[6,128,128]{2,1,0:T(8,128)S(1)}, u32[]{:S(2)}, u32[]{:S(2)}) collective-permute-start(f32[6,128,128]{2,1,0:T(8,128)} %get-tuple-element.35), channel_id=1, source_target_pairs={{0,16},{16,0},{32,48},{48,32},{64,80},{80,64},{96,112},{112,96},{1... | collective-permute-start | bytes 1179656 | tf_op jit(solution)/shard_map/ppermute | solution.py:371
  60.4 9.8 %collective-permute-start.2 = (f32[2,128,128]{2,1,0:T(8,128)}, f32[2,128,128]{2,1,0:T(8,128)S(1)}, u32[]{:S(2)}, u32[]{:S(2)}) collective-permute-start(f32[2,128,128]{2,1,0:T(8,128)} %get-tuple-element.33), channel_id=1, source_target_pairs={{0,32},{16,48},{32,0},{48,16},{64,96},{80,112},{96,64},{112,80},{1... | collective-permute-start | bytes 393224 | tf_op jit(solution)/shard_map/ppermute | solution.py:371
  64.4 11.2 %collective-permute-start.4 = (bf16[8,128,128]{2,1,0:T(8,128)(2,1)S(1)}, bf16[8,128,128]{2,1,0:T(8,128)(2,1)S(1)}, u32[]{:S(2)}, u32[]{:S(2)}) collective-permute-start(bf16[8,128,128]{2,1,0:T(8,128)(2,1)S(1)} %half_kernel.1), channel_id=1, source_target_pairs={{0,16},{16,0},{32,48},{48,32},{64,80},{80,64},{96,112},{112,96},{1... | collective-permute-start | bytes 786440 | tf_op jit(solution)/shard_map/ppermute | solution.py:371
  70.2 14.3 %all-to-all-start.2 = ((f32[32,16,128]{2,1,0:T(8,128)}), f32[32,16,128]{2,1,0:T(8,128)S(1)}, u32[]{:S(2)}, u32[]{:S(2)}) async-start(f32[32,16,128]{2,1,0:T(8,128)} %bitcast.6), calls=%async_computation.2 | async-start | bytes 524288 | tf_op jit(solution)/shard_map/all_to_all | solution.py:366
  86.8 7.2 %copy-start.2 = (f32[4,128,128]{2,1,0:T(8,128)S(1)}, f32[4,128,128]{2,1,0:T(8,128)}, u32[]{:S(2)}) copy-start(f32[4,128,128]{2,1,0:T(8,128)} %copy-done.1) | copy-start | bytes 786436
  86.8 7.2 %copy-start.4 = (f32[2,128,128]{2,1,0:T(8,128)S(1)}, f32[2,128,128]{2,1,0:T(8,128)}, u32[]{:S(2)}) copy-start(f32[2,128,128]{2,1,0:T(8,128)} %copy-done.3) | copy-start | bytes 393220
  86.8 7.2 %copy-start.6 = (f32[2,128,128]{2,1,0:T(8,128)S(1)}, f32[2,128,128]{2,1,0:T(8,128)}, u32[]{:S(2)}) copy-start(f32[2,128,128]{2,1,0:T(8,128)} %copy-done.5) | copy-start | bytes 393220
  86.8 7.2 %copy-start.8 = (f32[2,128,128]{2,1,0:T(8,128)S(1)}, f32[2,128,128]{2,1,0:T(8,128)}, u32[]{:S(2)}) copy-start(f32[2,128,128]{2,1,0:T(8,128)} %copy-done.7) | copy-start | bytes 393220
  86.8 7.2 %copy-start.10 = (bf16[128,128]{1,0:T(8,128)(2,1)S(1)}, bf16[128,128]{1,0:T(8,128)(2,1)}, u32[]{:S(2)}) copy-start(bf16[128,128]{1,0:T(8,128)(2,1)} %q_ref.3) | copy-start | bytes 98308
  86.8 7.2 %copy-start.12 = (bf16[128,128]{1,0:T(8,128)(2,1)S(1)}, bf16[128,128]{1,0:T(8,128)(2,1)}, u32[]{:S(2)}) copy-start(bf16[128,128]{1,0:T(8,128)(2,1)} %k_ref.3) | copy-start | bytes 98308
  86.8 15.6 %all-to-all-start.3 = ((bf16[32,8,1024]{2,1,0:T(8,128)(2,1)}), bf16[32,8,1024]{2,1,0:T(8,128)(2,1)S(1)}, u32[]{:S(2)}, u32[]{:S(2)}) async-start(bf16[32,8,1024]{2,1,0:T(8,128)(2,1)} %get-tuple-element.46), calls=%async_computation.3 | async-start | bytes 1048576 | tf_op jit(solution)/shard_map/all_to_all | solution.py:366
  90.7 3.2 %collective-permute-start.5 = (f32[2,128,128]{2,1,0:T(8,128)S(1)}, f32[2,128,128]{2,1,0:T(8,128)S(1)}, u32[]{:S(2)}, u32[]{:S(2)}) collective-permute-start(f32[2,128,128]{2,1,0:T(8,128)S(1)} %collective-permute-done.2.near_ref), channel_id=1, source_target_pairs={{0,16},{16,0},{32,48},{48,32},{64,80},{80,64},{96,112},{112,96},{1... | collective-permute-start | bytes 393224 | tf_op jit(solution)/shard_map/ppermute | solution.py:371

commit v6 on v5

--- a/solution.py
+++ b/solution.py
@@ -147,9 +147,7 @@
         transition, state_t = compose_heads(late, own_ref, other_ref, head, group)
         rounded = transition.astype(BF16)
         rest = jnp.where(rows == cols, transition - rounded.astype(F32), 0.0)
-        maps_ref[3 * group + head, share : 2 * share] = jnp.broadcast_to(
-            jnp.sum(rest, axis=0, keepdims=True), (share, WIDTH)
-        )
+        diag = jnp.broadcast_to(jnp.sum(rest, axis=0, keepdims=True), (WIDTH, WIDTH))
         quarters = [transition[at * share : (at + 1) * share] for at in range(4)]
         maps_ref[3 * group + head, :share] = jnp.where(
             late,
@@ -158,7 +156,7 @@
         )
         high = state_t.astype(BF16).astype(F32)
         part = jnp.where(core, state_t - high, high)
-        maps_ref[2 * group + head] = jnp.where(late, 0.0, part)
+        maps_ref[2 * group + head] = jnp.where(late, diag, part)
         maps_ref[head], maps_ref[group + head] = compose_maps(
             late, other_ref, head, group, chip_maps_ref[head], chip_maps_ref[group + head]
         )
@@ -182,13 +180,12 @@
         high = carried_t.astype(BF16).astype(F32)
         low = carried_t - high
         state = maps_ref[2 * group + head]
-        diag = maps_ref[3 * group + head, share : share + part, :]
         trans = maps_ref[3 * group + head, :share, :].astype(BF16)
         for chip in range(chips):
             mine = slice(chip * part, (chip + 1) * part)
             send_ref[chip, head, :share, :] = trans
             send_ref[chip, head, share:, :] = jnp.concatenate(
-                [state[mine], diag, high[mine], low[mine]], axis=0
+                [state[mine], high[mine], low[mine]], axis=0
             ).astype(BF16)
 
 
@@ -205,11 +202,11 @@
         )
         rest = [got_ref[quad, member, share:, :].astype(F32) for member in range(members)]
         product = mm_bf16(both, trans, 1, dim)
-        moved = product[:part] + product[part:] + state * rest[0][part : 2 * part]
+        moved = product[:part] + product[part:] + state * rest[2][:part]
         if dim == 1:
             return moved + rest[0][:part] + rest[1][:part]
         for piece in rest:
-            moved = moved + (piece[2 * part : 3 * part] + piece[3 * part :])
+            moved = moved + (piece[part : 2 * part] + piece[2 * part :])
         return moved
 
     ahead = jnp.zeros((part, WIDTH), F32)
@@ -415,7 +412,7 @@
     )
     cot, send = call(
         cotangent_kernel,
-        [shape(flat), shape((chips, group, WIDTH // 4 + 4 * part, WIDTH), BF16)],
+        [shape(flat), shape((chips, group, WIDTH // 4 + 3 * part, WIDTH), BF16)],
         1 << 28,
         full_grad, w_out, maps,
     )

time: 104 us -> 104 us (level)
  no operation moved by 1% of the time
where the time goes in v6:
time: 104 us; the launch traced here: 103 us
  starting transfers between devices  52.7 us (51%)
  Pallas kernels  23.5 us (23%)
  waiting for transfers between devices  21.6 us (21%)
  local copies, waits for them, and re-layouts  4.26 us (4%)
    all_to_all x4, starting transfers between devices, swap(): return lax.all_to_all(value, axis, 0, 0, tiled=True)  36.4 us
    pallas_call x10, Pallas kernels, call(): pl.pallas_call(kernel, out_shape=outs, in_specs=[smem if scalar else vmem...  23.5 us
    ppermute x6, starting transfers between devices, across(): lax.ppermute(value, 'seq', [(slab, slab ^ step) for slab in range(slabs)])  16.3 us
    all_to_all x4, waiting for transfers between devices, swap(): return lax.all_to_all(value, axis, 0, 0, tiled=True)  13.5 us
    ppermute x6, waiting for transfers between devices, across(): lax.ppermute(value, 'seq', [(slab, slab ^ step) for slab in range(slabs)])  8.12 us
    unnamed x32, local copies, waits for them, and re-layouts  2.62 us
  transfers between devices with their start and end apart: 10, of which 6 were waited for; matrix products, arithmetic and copies ran while one was open for 0% of the time, Pallas kernels for 18%

profile of v6, /device:TPU:1, one launch (start us, length us, event | category | flops | bytes accessed | tf_op | source)
XLA Modules:
  0.0 103.1 jit_solution(5362156960543217341)
XLA Ops:
  0.6 1.6 %broadcast_in_dim.2 = bf16[16,128,128]{2,1,0:T(8,128)(2,1)} broadcast(bf16[128,128]{1,0:T(8,128)(2,1)} %param.12), dimensions={1,2} | broadcast | bytes 557056 | tf_op jit(solution)/shard_map/broadcast_in_dim | solution.py:383
  2.3 15.9 %all-to-all-start = ((bf16[16,128,128]{2,1,0:T(8,128)(2,1)}), bf16[16,128,128]{2,1,0:T(8,128)(2,1)S(1)}, u32[]{:S(2)}, u32[]{:S(2)}) async-start(bf16[16,128,128]{2,1,0:T(8,128)(2,1)} %broadcast_in_dim.2), calls=%async_computation | async-start | bytes 1048576 | tf_op jit(solution)/shard_map/all_to_all | solution.py:363
  18.2 0.0 copy-start.14
  18.2 0.0 copy-done.9
  18.2 0.0 copy-done.11
  18.2 0.0 copy-done.13
  18.2 0.0 copy-done.15
  18.2 0.6 copy-done.14
  18.9 7.7 %prepare_kernel.1 = (f32[4,128,128]{2,1,0:T(8,128)S(1)}, f32[2,128,128]{2,1,0:T(8,128)S(1)}, f32[2,128,128]{2,1,0:T(8,128)S(1)}, f32[2,128,128]{2,1,0:T(8,128)S(...) custom-call(bf16[128,128]{1,0:T(8,128)(2,1)S(1)} %copy-done.9, ...), custom_call_target="tpu_custom_call" | custom-call | flops 1073741824 | bytes 1574912 | tf_op jit(solution)/shard_map/prepare_kernel/pallas_call | solution.py:347
  26.6 0.0 copy-start.3
  26.6 0.6 copy-done.3
  27.2 0.6 copy-done.5
  27.9 0.7 copy-done.7
  28.5 2.8 %collective-permute-start = (f32[4,128,128]{2,1,0:T(8,128)S(1)}, f32[4,128,128]{2,1,0:T(8,128)S(1)}, u32[]{:S(2)}, u32[]{:S(2)}) collective-permute-start(f32[4,128,128]{2,1,0:T(8,128)S(1)} %get-tuple-element.26.own_ref), channel_id=1, source_target_pairs={{0,16},{16,0},{32,48},{48,32},{64,80},{80,64},{96,112},{112,96},{1... | collective-permute-start | bytes 786440 | tf_op jit(solution)/shard_map/ppermute | solution.py:368
  31.4 0.1 pad_add_fusion.flags_ref
  31.4 1.1 %collective-permute-done.other_ref = f32[4,128,128]{2,1,0:T(8,128)S(1)} collective-permute-done((f32[4,128,128]{2,1,0:T(8,128)S(1)}, f32[4,128,128]{2,1,0:T(8,128)S(1)}, u32[]{:S(2)}, u32[]{:S(2)}) %collective-permute-start) | collective-permute-done | bytes 262176 | tf_op jit(solution)/shard_map/ppermute | solution.py:368
  32.5 1.4 %chip_kernel.1 = (f32[4,128,128]{2,1,0:T(8,128)S(1)}, f32[4,128,128]{2,1,0:T(8,128)S(1)}) custom-call(s32[2]{0:T(128)S(1)} %pad_add_fusion.flags_ref, f32[4,128,128]{2,1,0:T(8,128)S(1)} %get-tuple-element.26.own_ref, f32[4,128,128]{2,1,0:T(8,128)S(1)} %collective-permute-done.other_ref, f32[2,128,128]{2,1,0:T(8,128)S(1)} %get-tuple-element.27.probe_ref, ...), custom_call_target="tpu_custom_call" | custom-call | flops 268435456 | bytes 1310728 | tf_op jit(solution)/shard_map/chip_kernel/pallas_call | solution.py:347
  33.9 0.0 copy-done.1
  33.9 3.1 %collective-permute-start.1 = (f32[4,128,128]{2,1,0:T(8,128)S(1)}, f32[4,128,128]{2,1,0:T(8,128)S(1)}, u32[]{:S(2)}, u32[]{:S(2)}) collective-permute-start(f32[4,128,128]{2,1,0:T(8,128)S(1)} %get-tuple-element.29.own_ref), channel_id=1, source_target_pairs={{0,32},{16,48},{32,0},{48,16},{64,96},{80,112},{96,64},{112,80},{1... | collective-permute-start | bytes 786440 | tf_op jit(solution)/shard_map/ppermute | solution.py:368
  37.1 6.3 %collective-permute-done.1.other_ref.other_chip_ref = f32[4,128,128]{2,1,0:T(8,128)S(1)} collective-permute-done((f32[4,128,128]{2,1,0:T(8,128)S(1)}, f32[4,128,128]{2,1,0:T(8,128)S(1)}, u32[]{:S(2)}, u32[]{:S(2)}) %collective-permute-start.1) | collective-permute-done | bytes 262176 | tf_op jit(solution)/shard_map/ppermute | solution.py:368
  43.3 1.4 %quad_kernel.1.maps_ref = f32[8,128,128]{2,1,0:T(8,128)S(1)} custom-call(s32[2]{0:T(128)S(1)} %pad_add_fusion.flags_ref, f32[4,128,128]{2,1,0:T(8,128)S(1)} %get-tuple-element.29.own_ref, f32[4,128,128]{2,1,0:T(8,128)S(1)} %collective-permute-done.1.other_ref.other_chip_ref, f32[4,128,128]{2,1,0:T(8,128)S(1)} %get-tuple-element.30.chip_maps_ref), custom_call_target="tpu_custom_call" | custom-call | flops 268435456 | bytes 1310728 | tf_op jit(solution)/shard_map/quad_kernel/pallas_call | solution.py:347
  44.8 0.0 all-to-all-done.grad_ref
  44.8 1.7 %cotangent_kernel.1 = (f32[128,256]{1,0:T(8,128)S(1)}, bf16[16,2,56,128]{3,2,1,0:T(8,128)(2,1)}) custom-call(bf16[16,128,128]{2,1,0:T(8,128)(2,1)S(1)} %all-to-all-done.grad_ref, bf16[256,2048]{1,0:T(8,128)(2,1)S(1)} %copy-done, f32[8,128,128]{2,1,0:T(8,128)S(1)} %quad_kernel.1.maps_ref), custom_call_target="tpu_custom_call" | custom-call | flops 268435456 | bytes 2686976 | tf_op jit(solution)/shard_map/cotangent_kernel/pallas_call | solution.py:347
  46.5 10.5 %all-to-all-start.1 = ((bf16[32,56,128]{2,1,0:T(8,128)(2,1)}), bf16[32,56,128]{2,1,0:T(8,128)(2,1)S(1)}, u32[]{:S(2)}, u32[]{:S(2)}) async-start(bf16[32,56,128]{2,1,0:T(8,128)(2,1)} %bitcast.4), calls=%async_computation.1 | async-start | bytes 917504 | tf_op jit(solution)/shard_map/all_to_all | solution.py:363
  57.0 1.2 %sibling_kernel.1 = (f32[6,128,128]{2,1,0:T(8,128)}, f32[2,128,128]{2,1,0:T(8,128)}) custom-call(f32[8,128,128]{2,1,0:T(8,128)S(1)} %quad_kernel.1.maps_ref, f32[128,256]{1,0:T(8,128)S(1)} %get-tuple-element.32.cot_ref, f32[2,128,128]{2,1,0:T(8,128)S(1)} %get-tuple-element.27.probe_ref, f32[4,128,128]{2,1,0:T(8,128)S(1)} %get-tuple-element.30.chip_maps_ref), custom_call_target="tpu_custom_call" | custom-call | flops 67108864 | bytes 1572864 | tf_op jit(solution)/shard_map/sibling_kernel/pallas_call | solution.py:347
  58.2 2.1 %collective-permute-start.3 = (f32[6,128,128]{2,1,0:T(8,128)}, f32[6,128,128]{2,1,0:T(8,128)S(1)}, u32[]{:S(2)}, u32[]{:S(2)}) collective-permute-start(f32[6,128,128]{2,1,0:T(8,128)} %get-tuple-element.35), channel_id=1, source_target_pairs={{0,16},{16,0},{32,48},{48,32},{64,80},{80,64},{96,112},{112,96},{1... | collective-permute-start | bytes 1179656 | tf_op jit(solution)/shard_map/ppermute | solution.py:368
  60.4 3.4 %collective-permute-start.2 = (f32[2,128,128]{2,1,0:T(8,128)}, f32[2,128,128]{2,1,0:T(8,128)S(1)}, u32[]{:S(2)}, u32[]{:S(2)}) collective-permute-start(f32[2,128,128]{2,1,0:T(8,128)} %get-tuple-element.33), channel_id=1, source_target_pairs={{0,32},{16,48},{32,0},{48,16},{64,96},{80,112},{96,64},{112,80},{1... | collective-permute-start | bytes 393224 | tf_op jit(solution)/shard_map/ppermute | solution.py:368
  63.8 0.6 half_kernel.1
  64.4 2.4 %collective-permute-start.4 = (bf16[8,128,128]{2,1,0:T(8,128)(2,1)S(1)}, bf16[8,128,128]{2,1,0:T(8,128)(2,1)S(1)}, u32[]{:S(2)}, u32[]{:S(2)}) collective-permute-start(bf16[8,128,128]{2,1,0:T(8,128)(2,1)S(1)} %half_kernel.1), channel_id=1, source_target_pairs={{0,16},{16,0},{32,48},{48,32},{64,80},{80,64},{96,112},{112,96},{1... | collective-permute-start | bytes 786440 | tf_op jit(solution)/shard_map/ppermute | solution.py:368
  66.7 1.1 %all-to-all-done.1 = bf16[32,56,128]{2,1,0:T(8,128)(2,1)S(1)} async-done(((bf16[32,56,128]{2,1,0:T(8,128)(2,1)}), bf16[32,56,128]{2,1,0:T(8,128)(2,1)S(1)}, u32[]{:S(2)}, u32[]{:S(2)}) %all-to-all-start.1) | async-done | bytes 458784 | tf_op jit(solution)/shard_map/all_to_all | solution.py:363
  67.9 1.6 %scan_kernel.1 = f32[8,4,16,128]{3,2,1,0:T(8,128)} custom-call(bf16[8,4,56,128]{3,2,1,0:T(8,128)(2,1)S(1)} %bitcast.12), custom_call_target="tpu_custom_call" | custom-call | flops 134217728 | bytes 720896 | tf_op jit(solution)/shard_map/scan_kernel/pallas_call | solution.py:347
  69.5 0.0 collective-permute-done.2.near_ref
  69.5 6.1 %all-to-all-start.2 = ((f32[32,16,128]{2,1,0:T(8,128)}), f32[32,16,128]{2,1,0:T(8,128)S(1)}, u32[]{:S(2)}, u32[]{:S(2)}) async-start(f32[32,16,128]{2,1,0:T(8,128)} %bitcast.6), calls=%async_computation.2 | async-start | bytes 524288 | tf_op jit(solution)/shard_map/all_to_all | solution.py:363
  75.6 0.0 collective-permute-done.4.other_grad_ref
  75.6 0.0 collective-permute-done.3.other_maps_ref.other_pack_ref
  75.6 8.9 %all-to-all-done.2 = f32[32,16,128]{2,1,0:T(8,128)S(1)} async-done(((f32[32,16,128]{2,1,0:T(8,128)}), f32[32,16,128]{2,1,0:T(8,128)S(1)}, u32[]{:S(2)}, u32[]{:S(2)}) %all-to-all-start.2) | async-done | bytes 262176 | tf_op jit(solution)/shard_map/all_to_all | solution.py:363
  84.5 2.3 %output_kernel.1 = (bf16[128,256]{1,0:T(8,128)(2,1)}, bf16[32,8,1024]{2,1,0:T(8,128)(2,1)}) custom-call(s32[2]{0:T(128)S(1)} %pad_add_fusion.flags_ref, f32[16,2,16,128]{3,2,1,0:T(8,128)S(1)} %bitcast.9, f32[8,128,128]{2,1,0:T(8,128)S(1)} %quad_kernel.1.maps_ref, f32[6,128,128]{2,1,0:T(8,128)S(1)} %collective-permute-done.3.other_maps_ref.other_pack_ref, ...), custom_call_target="tpu_custom_call" | custom-call | flops 268435456 | bytes 2555912 | tf_op jit(solution)/shard_map/output_kernel/pallas_call | solution.py:347
  86.8 0.0 copy-start.10
  86.8 0.0 copy-start.12
  86.8 3.9 %all-to-all-start.3 = ((bf16[32,8,1024]{2,1,0:T(8,128)(2,1)}), bf16[32,8,1024]{2,1,0:T(8,128)(2,1)S(1)}, u32[]{:S(2)}, u32[]{:S(2)}) async-start(bf16[32,8,1024]{2,1,0:T(8,128)(2,1)} %get-tuple-element.46), calls=%async_computation.3 | async-start | bytes 1048576 | tf_op jit(solution)/shard_map/all_to_all | solution.py:363
  90.7 2.4 %collective-permute-start.5 = (f32[2,128,128]{2,1,0:T(8,128)S(1)}, f32[2,128,128]{2,1,0:T(8,128)S(1)}, u32[]{:S(2)}, u32[]{:S(2)}) collective-permute-start(f32[2,128,128]{2,1,0:T(8,128)S(1)} %collective-permute-done.2.near_ref), channel_id=1, source_target_pairs={{0,16},{16,0},{32,48},{48,32},{64,80},{80,64},{96,112},{112,96},{1... | collective-permute-start | bytes 393224 | tf_op jit(solution)/shard_map/ppermute | solution.py:368
  93.1 0.8 collective-permute-done.5.far_ref
  93.9 0.0 copy-done.8
  94.0 0.0 copy-done.10
  94.0 0.0 copy-done.12
  94.0 4.9 %gradient_kernel.1 = (f32[128,128]{1,0:T(8,128)}, f32[128,128]{1,0:T(8,128)}, f32[128,256]{1,0:T(8,128)}) custom-call(s32[2]{0:T(128)S(1)} %pad_add_fusion.flags_ref, bf16[128,128]{1,0:T(8,128)(2,1)S(1)} %copy-done.10, bf16[128,128]{1,0:T(8,128)(2,1)S(1)} %copy-done.12, f32[16,2,16,128]{3,2,1,0:T(8,128)S(1)} %bitcast.10, f32[4,128,128]{2,1,0:T(8,128)S(1)} %copy-done.2, ...), custom_call_target="tpu_custom_call" | custom-call | flops 536870912 | bytes 2818056 | tf_op jit(solution)/shard_map/gradient_kernel/pallas_call | solution.py:347
  98.9 3.5 %all-to-all-done.3 = bf16[32,8,1024]{2,1,0:T(8,128)(2,1)S(1)} async-done(((bf16[32,8,1024]{2,1,0:T(8,128)(2,1)}), bf16[32,8,1024]{2,1,0:T(8,128)(2,1)S(1)}, u32[]{:S(2)}, u32[]{:S(2)}) %all-to-all-start.3) | async-done | bytes 524320 | tf_op jit(solution)/shard_map/all_to_all | solution.py:363
  102.4 0.7 sum_kernel.1
  (16 shorter events, 0.0 us)
Async XLA Ops:
  2.3 15.9 %copy-start.9 = (bf16[128,128]{1,0:T(8,128)(2,1)S(1)}, bf16[128,128]{1,0:T(8,128)(2,1)}, u32[]{:S(2)}) copy-start(bf16[128,128]{1,0:T(8,128)(2,1)} %q_ref.3) | copy-start | bytes 98308
  2.3 15.9 %copy-start.11 = (bf16[128,128]{1,0:T(8,128)(2,1)S(1)}, bf16[128,128]{1,0:T(8,128)(2,1)}, u32[]{:S(2)}) copy-start(bf16[128,128]{1,0:T(8,128)(2,1)} %k_ref.3) | copy-start | bytes 98308
  2.3 15.9 %copy-start.13 = (bf16[128,256]{1,0:T(8,128)(2,1)S(1)}, bf16[128,256]{1,0:T(8,128)(2,1)}, u32[]{:S(2)}) copy-start(bf16[128,256]{1,0:T(8,128)(2,1)} %v_ref.1) | copy-start | bytes 196612
  2.3 15.9 %copy-start.15 = (s32[128,2]{0,1:T(2,128)S(1)}, s32[128,2]{0,1:T(2,128)}, u32[]{:S(2)}) copy-start(s32[128,2]{0,1:T(2,128)} %param.11) | copy-start | bytes 3076
  2.3 42.5 %all-to-all-start = ((bf16[16,128,128]{2,1,0:T(8,128)(2,1)}), bf16[16,128,128]{2,1,0:T(8,128)(2,1)S(1)}, u32[]{:S(2)}, u32[]{:S(2)}) async-start(bf16[16,128,128]{2,1,0:T(8,128)(2,1)} %broadcast_in_dim.2), calls=%async_computation | async-start | bytes 1048576 | tf_op jit(solution)/shard_map/all_to_all | solution.py:363
  18.2 0.7 copy-start.14
  26.6 0.7 copy-start.3
  27.2 0.6 copy-start.5
  27.9 0.7 copy-start.7
  28.5 4.0 %collective-permute-start = (f32[4,128,128]{2,1,0:T(8,128)S(1)}, f32[4,128,128]{2,1,0:T(8,128)S(1)}, u32[]{:S(2)}, u32[]{:S(2)}) collective-permute-start(f32[4,128,128]{2,1,0:T(8,128)S(1)} %get-tuple-element.26.own_ref), channel_id=1, source_target_pairs={{0,16},{16,0},{32,48},{48,32},{64,80},{80,64},{96,112},{112,96},{1... | collective-permute-start | bytes 786440 | tf_op jit(solution)/shard_map/ppermute | solution.py:368
  32.5 1.4 %copy-start.1 = (f32[4,128,128]{2,1,0:T(8,128)}, f32[4,128,128]{2,1,0:T(8,128)S(1)}, u32[]{:S(2)}) copy-start(f32[4,128,128]{2,1,0:T(8,128)S(1)} %collective-permute-done.other_ref) | copy-start | bytes 786436
  32.5 12.3 %copy-start = (bf16[256,2048]{1,0:T(8,128)(2,1)S(1)}, bf16[256,2048]{1,0:T(8,128)(2,1)}, u32[]{:S(2)}) copy-start(bf16[256,2048]{1,0:T(8,128)(2,1)} %w_ref.1) | copy-start | bytes 3145732
  33.9 9.4 %collective-permute-start.1 = (f32[4,128,128]{2,1,0:T(8,128)S(1)}, f32[4,128,128]{2,1,0:T(8,128)S(1)}, u32[]{:S(2)}, u32[]{:S(2)}) collective-permute-start(f32[4,128,128]{2,1,0:T(8,128)S(1)} %get-tuple-element.29.own_ref), channel_id=1, source_target_pairs={{0,32},{16,48},{32,0},{48,16},{64,96},{80,112},{96,64},{112,80},{1... | collective-permute-start | bytes 786440 | tf_op jit(solution)/shard_map/ppermute | solution.py:368
  46.5 21.4 %all-to-all-start.1 = ((bf16[32,56,128]{2,1,0:T(8,128)(2,1)}), bf16[32,56,128]{2,1,0:T(8,128)(2,1)S(1)}, u32[]{:S(2)}, u32[]{:S(2)}) async-start(bf16[32,56,128]{2,1,0:T(8,128)(2,1)} %bitcast.4), calls=%async_computation.1 | async-start | bytes 917504 | tf_op jit(solution)/shard_map/all_to_all | solution.py:363
  58.2 17.3 %collective-permute-start.3 = (f32[6,128,128]{2,1,0:T(8,128)}, f32[6,128,128]{2,1,0:T(8,128)S(1)}, u32[]{:S(2)}, u32[]{:S(2)}) collective-permute-start(f32[6,128,128]{2,1,0:T(8,128)} %get-tuple-element.35), channel_id=1, source_target_pairs={{0,16},{16,0},{32,48},{48,32},{64,80},{80,64},{96,112},{112,96},{1... | collective-permute-start | bytes 1179656 | tf_op jit(solution)/shard_map/ppermute | solution.py:368
  60.4 9.1 %collective-permute-start.2 = (f32[2,128,128]{2,1,0:T(8,128)}, f32[2,128,128]{2,1,0:T(8,128)S(1)}, u32[]{:S(2)}, u32[]{:S(2)}) collective-permute-start(f32[2,128,128]{2,1,0:T(8,128)} %get-tuple-element.33), channel_id=1, source_target_pairs={{0,32},{16,48},{32,0},{48,16},{64,96},{80,112},{96,64},{112,80},{1... | collective-permute-start | bytes 393224 | tf_op jit(solution)/shard_map/ppermute | solution.py:368
  64.4 11.2 %collective-permute-start.4 = (bf16[8,128,128]{2,1,0:T(8,128)(2,1)S(1)}, bf16[8,128,128]{2,1,0:T(8,128)(2,1)S(1)}, u32[]{:S(2)}, u32[]{:S(2)}) collective-permute-start(bf16[8,128,128]{2,1,0:T(8,128)(2,1)S(1)} %half_kernel.1), channel_id=1, source_target_pairs={{0,16},{16,0},{32,48},{48,32},{64,80},{80,64},{96,112},{112,96},{1... | collective-permute-start | bytes 786440 | tf_op jit(solution)/shard_map/ppermute | solution.py:368
  69.5 15.0 %all-to-all-start.2 = ((f32[32,16,128]{2,1,0:T(8,128)}), f32[32,16,128]{2,1,0:T(8,128)S(1)}, u32[]{:S(2)}, u32[]{:S(2)}) async-start(f32[32,16,128]{2,1,0:T(8,128)} %bitcast.6), calls=%async_computation.2 | async-start | bytes 524288 | tf_op jit(solution)/shard_map/all_to_all | solution.py:363
  86.7 7.2 %copy-start.2 = (f32[4,128,128]{2,1,0:T(8,128)S(1)}, f32[4,128,128]{2,1,0:T(8,128)}, u32[]{:S(2)}) copy-start(f32[4,128,128]{2,1,0:T(8,128)} %copy-done.1) | copy-start | bytes 786436
  86.7 7.2 %copy-start.4 = (f32[2,128,128]{2,1,0:T(8,128)S(1)}, f32[2,128,128]{2,1,0:T(8,128)}, u32[]{:S(2)}) copy-start(f32[2,128,128]{2,1,0:T(8,128)} %copy-done.3) | copy-start | bytes 393220
  86.7 7.2 %copy-start.6 = (f32[2,128,128]{2,1,0:T(8,128)S(1)}, f32[2,128,128]{2,1,0:T(8,128)}, u32[]{:S(2)}) copy-start(f32[2,128,128]{2,1,0:T(8,128)} %copy-done.5) | copy-start | bytes 393220
  86.7 7.2 %copy-start.8 = (f32[2,128,128]{2,1,0:T(8,128)S(1)}, f32[2,128,128]{2,1,0:T(8,128)}, u32[]{:S(2)}) copy-start(f32[2,128,128]{2,1,0:T(8,128)} %copy-done.7) | copy-start | bytes 393220
  86.8 7.2 %copy-start.10 = (bf16[128,128]{1,0:T(8,128)(2,1)S(1)}, bf16[128,128]{1,0:T(8,128)(2,1)}, u32[]{:S(2)}) copy-start(bf16[128,128]{1,0:T(8,128)(2,1)} %q_ref.3) | copy-start | bytes 98308
  86.8 7.2 %copy-start.12 = (bf16[128,128]{1,0:T(8,128)(2,1)S(1)}, bf16[128,128]{1,0:T(8,128)(2,1)}, u32[]{:S(2)}) copy-start(bf16[128,128]{1,0:T(8,128)(2,1)} %k_ref.3) | copy-start | bytes 98308
  86.8 15.6 %all-to-all-start.3 = ((bf16[32,8,1024]{2,1,0:T(8,128)(2,1)}), bf16[32,8,1024]{2,1,0:T(8,128)(2,1)S(1)}, u32[]{:S(2)}, u32[]{:S(2)}) async-start(bf16[32,8,1024]{2,1,0:T(8,128)(2,1)} %get-tuple-element.46), calls=%async_computation.3 | async-start | bytes 1048576 | tf_op jit(solution)/shard_map/all_to_all | solution.py:363
  90.7 3.2 %collective-permute-start.5 = (f32[2,128,128]{2,1,0:T(8,128)S(1)}, f32[2,128,128]{2,1,0:T(8,128)S(1)}, u32[]{:S(2)}, u32[]{:S(2)}) collective-permute-start(f32[2,128,128]{2,1,0:T(8,128)S(1)} %collective-permute-done.2.near_ref), channel_id=1, source_target_pairs={{0,16},{16,0},{32,48},{48,32},{64,80},{80,64},{96,112},{112,96},{1... | collective-permute-start | bytes 393224 | tf_op jit(solution)/shard_map/ppermute | solution.py:368
